TPU v7x, 32 devices: a whole 2x2x4 slice. The times are simulated.
32 devices in a mesh: psg: 8 (over y, x, core), qry: 4 (over z).
Axes of the slice: x: 2, y: 2, z: 4, core: 2. Of those that a mesh axis runs over, the one named last changes fastest.
Arguments:
- hidden: bfloat16 [512, 4096], P('qry'), may hold values from -6 to 6
- norm_gain: float32 [4096], replicated, may hold values from 0.5 to 1.5
- proj_weight: bfloat16 [4096, 4096], P('psg', 'qry'), may hold values from -0.09375 to 0.09375
- pq_codes: int32 [16384, 512], P('psg', 'qry'), may hold values from 0 to 255
- codebook: bfloat16 [512, 8, 256], P('qry'), may hold values from -560 to 560
- positives: int32 [512], replicated, may hold values from 0 to 16383
Outputs:
- losses: float32 [512], P('qry')
- hidden_grad: bfloat16 [512, 4096], P('qry')
- weight_grad: float32 [4096, 4096], P('psg', 'qry')
- codebook_grad: float32 [512, 8, 256], P('qry')
All inputs are finite; a program needn't handle non-finite values.
Results may differ from a plain program's by a relative error of at most 0.019.
The roundings to bfloat16 on the way count: a program that leaves them out, or rounds other values in their place, can miss the bound.
Values may be sent and summed in bfloat16 or wider, within the bound.
No kernel may reach another device: no remote copies, remote signals or barrier semaphores. Data moves between devices by JAX's collectives and lax.ppermute only.
A program may use at most 128 MiB of HBM per device.

v0:
```python
import jax
import jax.numpy as jnp
from jax import lax
from jax.sharding import PartitionSpec as P

score_scale = 0.0625
norm_eps = 1e-06


def code_hot(code_block, book):
    levels = lax.broadcasted_iota(jnp.int32, code_block.shape + (book.shape[2],), 2)
    return (code_block[:, :, None] == levels).astype(jnp.bfloat16)


def per_device(hidden, norm_gain, proj_weight, pq_codes, codebook, positives):
    gathered = lax.all_gather(hidden, "qry", axis=0, tiled=True)
    floats_all = gathered.astype(jnp.float32)
    inverse_all = lax.rsqrt(jnp.mean(floats_all * floats_all, axis=1, keepdims=True) + norm_eps)
    normed = (floats_all * inverse_all * norm_gain[None, :]).astype(jnp.bfloat16)
    columns = proj_weight.shape[1]
    query_float = jnp.dot(
        normed,
        lax.all_gather(proj_weight, "psg", axis=0, tiled=True),
        preferred_element_type=jnp.float32,
    )
    queries = query_float.astype(jnp.bfloat16)
    passage_count = pq_codes.shape[0]
    sub_count = codebook.shape[0]
    sub_width = codebook.shape[1]
    block_rows = min(passage_count, 512)
    code_blocks = pq_codes.reshape(passage_count // block_rows, block_rows, sub_count)

    def decode(code_block):
        hot_table = code_hot(code_block, codebook)
        vectors = jnp.einsum(
            "pmk,mdk->pmd", hot_table, codebook, preferred_element_type=jnp.float32
        )
        return vectors.astype(jnp.bfloat16).reshape(block_rows, columns)

    passages = lax.map(decode, code_blocks).reshape(passage_count, columns)
    partial_value = (
        lax.dot_general(
            queries, passages, (((1,), (1,)), ((), ())), preferred_element_type=jnp.float32
        )
        * score_scale
    )
    qry_index = lax.axis_index("qry")
    own_rows = hidden.shape[0]
    scores = lax.psum_scatter(partial_value, "qry", scatter_dimension=0, tiled=True)
    row_targets = lax.dynamic_slice_in_dim(positives, qry_index * own_rows, own_rows, 0)
    local_target = row_targets - lax.axis_index("psg") * passage_count
    target = lax.broadcasted_iota(jnp.int32, scores.shape, 1) == local_target[:, None]
    local_max = jnp.max(scores, axis=1)
    positive_part = jnp.sum(jnp.where(target, scores, 0.0), axis=1)
    row_max = lax.pmax(local_max, "psg")
    shifted_total = jnp.sum(jnp.exp(scores - row_max[:, None]), axis=1)
    row_total, positive_score = lax.psum((shifted_total, positive_part), "psg")
    losses = jnp.log(row_total) + row_max - positive_score
    score_grad = (
        jnp.exp(scores - row_max[:, None]) / row_total[:, None] - target.astype(jnp.float32)
    ).astype(jnp.bfloat16)
    all_grad = lax.all_gather(score_grad, "qry", axis=0, tiled=True)
    query_part = jnp.dot(all_grad, passages, preferred_element_type=jnp.float32) * score_scale
    query_grad = lax.psum(query_part, "psg").astype(jnp.bfloat16)
    passage_grad = (
        lax.dot_general(
            all_grad, queries, (((0,), (0,)), ((), ())), preferred_element_type=jnp.float32
        )
        * score_scale
    ).astype(jnp.bfloat16)
    grad_blocks = passage_grad.reshape(
        passage_count // block_rows, block_rows, sub_count, sub_width
    )

    def add_book(carry, paired):
        code_block, grad_block = paired
        hot_table = code_hot(code_block, codebook)
        return (
            carry
            + jnp.einsum("pmk,pmd->mdk", hot_table, grad_block, preferred_element_type=jnp.float32),
            None,
        )

    book_part, unused = lax.scan(
        add_book, jnp.zeros(codebook.shape, jnp.float32), (code_blocks, grad_blocks)
    )
    codebook_grad = lax.psum(book_part.astype(jnp.bfloat16), "psg").astype(jnp.float32)
    row_span = proj_weight.shape[0]
    normed_rows = lax.dynamic_slice_in_dim(normed, lax.axis_index("psg") * row_span, row_span, 1)
    weight_grad = lax.dot_general(
        normed_rows, query_grad, (((0,), (0,)), ((), ())), preferred_element_type=jnp.float32
    )
    norm_part = lax.dot_general(
        query_grad,
        lax.all_gather(proj_weight, "psg", axis=0, tiled=True),
        (((1,), (1,)), ((), ())),
        preferred_element_type=jnp.float32,
    )
    norm_back = lax.psum_scatter(
        norm_part.astype(jnp.bfloat16), "qry", scatter_dimension=0, tiled=True
    ).astype(jnp.float32)
    floats_own = hidden.astype(jnp.float32)
    inverse_own = lax.rsqrt(jnp.mean(floats_own * floats_own, axis=1, keepdims=True) + norm_eps)
    scaled = norm_back * norm_gain[None, :]
    hidden_grad = (
        inverse_own * scaled
        - floats_own
        * inverse_own
        * inverse_own
        * inverse_own
        * jnp.mean(scaled * floats_own, axis=1, keepdims=True)
    ).astype(jnp.bfloat16)
    return (losses, hidden_grad, weight_grad, codebook_grad)


def solution(mesh):
    in_specs = (P("qry", None), P(), P("psg", "qry"), P("psg", "qry"), P("qry", None, None), P())
    out_specs = (P("qry"), P("qry", None), P("psg", "qry"), P("qry", None, None))
    return jax.shard_map(
        per_device, mesh=mesh, in_specs=in_specs, out_specs=out_specs, check_vma=False
    )
```

profile of v0, /device:TPU:0, one launch (start us, length us, event | category | flops | bytes accessed | tf_op | source)
XLA Modules:
  0.0 560.6 jit_solution(67081673315906071)
XLA Ops:
  7.2 0.7 all-gather.4.cloned.1.call-update
  7.9 0.7 all-gather.6.cloned.1.call-update
  8.7 1.6 copy.11
  10.3 61.1 %while.21 = (s32[]{:T(128)}, bf16[4,512,1024]{2,1,0:T(8,128)(2,1)}, s32[4,512,128]{1,2,0:T(8,128)S(1)}, bf16[128,8,256]{2,1,0:T(8,128)(2,1)}, s32[]{:T(128)}) while((s32[]{:T(128)}, bf16[4,512,1024]{2,1,0:T(8,128)(2,1)}, s32[4,512,128]{1,2,0:T(8,128)S(1)}, bf16[128,8,256]{2,1,0:T(8,128)(2,1)}, s32[]{:T(128)}) %tuple.45), condition=%wide.region_2.3_spmd, body=%wide.region_1.2_spmd.sunk | while | flops 285736960 | bytes 6553677 | solution.py:40
  10.3 13.6 %fusion.47 = bf16[1,512,1024]{1,2,0:T(8,128)(2,1)S(1)} fusion(bf16[128,8,256]{2,1,0:T(8,128)(2,1)} %get-tuple-element.164, s32[512,128]{0,1:T(8,128)S(1)} %dynamic-slice_bitcast_fusion.4), kind=kOutput, calls=%fused_computation.4.clone.2 | convolution fusion | flops 285736960 | bytes 1835008 | tf_op jit(solution)/shard_map/while/body/eval_jaxpr/pmk,mdk->pmd/dot_general | solution.py:35
  24.0 0.5 copy.19
  24.5 1.1 constant_dynamic-update-slice_fusion.2
  25.7 13.6 %fusion.47 = bf16[1,512,1024]{1,2,0:T(8,128)(2,1)S(1)} fusion(bf16[128,8,256]{2,1,0:T(8,128)(2,1)} %get-tuple-element.164, s32[512,128]{0,1:T(8,128)S(1)} %dynamic-slice_bitcast_fusion.4), kind=kOutput, calls=%fused_computation.4.clone.2 | convolution fusion | flops 285736960 | bytes 1835008 | tf_op jit(solution)/shard_map/while/body/eval_jaxpr/pmk,mdk->pmd/dot_general | solution.py:35
  39.8 1.0 constant_dynamic-update-slice_fusion.2
  40.9 13.6 %fusion.47 = bf16[1,512,1024]{1,2,0:T(8,128)(2,1)S(1)} fusion(bf16[128,8,256]{2,1,0:T(8,128)(2,1)} %get-tuple-element.164, s32[512,128]{0,1:T(8,128)S(1)} %dynamic-slice_bitcast_fusion.4), kind=kOutput, calls=%fused_computation.4.clone.2 | convolution fusion | flops 285736960 | bytes 1835008 | tf_op jit(solution)/shard_map/while/body/eval_jaxpr/pmk,mdk->pmd/dot_general | solution.py:35
  54.5 0.5 copy.19
  55.1 1.1 constant_dynamic-update-slice_fusion.2
  56.2 13.6 %fusion.47 = bf16[1,512,1024]{1,2,0:T(8,128)(2,1)S(1)} fusion(bf16[128,8,256]{2,1,0:T(8,128)(2,1)} %get-tuple-element.164, s32[512,128]{0,1:T(8,128)S(1)} %dynamic-slice_bitcast_fusion.4), kind=kOutput, calls=%fused_computation.4.clone.2 | convolution fusion | flops 285736960 | bytes 1835008 | tf_op jit(solution)/shard_map/while/body/eval_jaxpr/pmk,mdk->pmd/dot_general | solution.py:35
  70.3 1.1 constant_dynamic-update-slice_fusion.2
  71.4 21.8 %all-gather.4.cloned.1.call-done = bf16[512,4096]{1,0:T(8,128)(2,1)} async-done(((bf16[128,4096]{1,0:T(8,128)(2,1)}), bf16[512,4096]{1,0:T(8,128)(2,1)}) %all-gather.4.cloned.1.call-update) | async-done | bytes 4194320 | tf_op jit(solution)/shard_map/all_gather | solution.py:16
  93.2 3.2 fusion.10
  96.6 3.6 fusion.12
  100.2 47.6 %all-gather.6.cloned.1.call-done = bf16[4096,1024]{1,0:T(8,128)(2,1)} async-done(((bf16[512,1024]{1,0:T(8,128)(2,1)}), bf16[4096,1024]{1,0:T(8,128)(2,1)}) %all-gather.6.cloned.1.call-update) | async-done | bytes 8388624 | tf_op jit(solution)/shard_map/all_gather | solution.py:23
  147.8 9.3 %convolution_convert_fusion.1 = bf16[512,1024]{1,0:T(8,128)(2,1)S(1)} fusion(bf16[512,4096]{1,0:T(8,128)(2,1)} %fusion.12, bf16[4096,1024]{1,0:T(8,128)(2,1)} %all-gather.6.cloned.1.call-done), kind=kOutput, calls=%fused_computation.35 | convolution fusion | flops 4295491584 | bytes 13631488 | tf_op jit(solution)/shard_map/dot_general | solution.py:21
  157.1 1.0 copy-done.7
  158.1 4.3 convolution_multiply_fusion
  162.5 0.8 dynamic-slice_subtract_fusion
  163.2 76.1 %reduce-scatter.3.cloned.1.call-done = f32[128,2048]{1,0:T(8,128)} async-done(((f32[512,2048]{1,0:T(8,128)}), f32[128,2048]{1,0:T(8,128)}) %reduce-scatter.3.cloned.1.call-update) | async-done | bytes 1048592 | tf_op jit(solution)/shard_map/reduce_scatter | solution.py:49
  239.4 1.4 reduce_max.9
  240.7 13.3 %pmax.7 = f32[128]{0:T(128)S(1)} all-reduce(f32[128]{0:T(128)S(1)} %reduce_max.9), channel_id=1, replica_groups=mesh['psg'=8,'qry'=4] {'psg'}, use_global_device_ids=true, to_apply=%region_5.6 | all-reduce | flops 128 | bytes 1024 | tf_op jit(solution)/shard_map/pmax | solution.py:55
  254.0 1.6 fusion.20
  255.6 11.8 %psum.28 = f32[128]{0:T(128)S(1)} all-reduce(f32[128]{0:T(128)S(1)} %get-tuple-element.79), channel_id=1, replica_groups=mesh['psg'=8,'qry'=4] {'psg'}, use_global_device_ids=true, to_apply=%region_7.8 | all-reduce | flops 128 | bytes 1024 | tf_op jit(solution)/shard_map/psum | solution.py:57
  267.4 2.4 subtract_convert_fusion
  270.1 44.5 %all-gather.8.cloned.1.call-done = bf16[512,2048]{1,0:T(8,128)(2,1)} async-done(((bf16[128,2048]{1,0:T(8,128)(2,1)}), bf16[512,2048]{1,0:T(8,128)(2,1)}) %all-gather.8.cloned.1.call-update) | async-done | bytes 2097168 | tf_op jit(solution)/shard_map/all_gather | solution.py:62
  314.7 5.3 convolution_multiply_fusion.1
  320.0 4.3 multiply_convert_fusion
  324.3 6.5 %copy.13 = bf16[2048,1024]{0,1:T(8,128)(2,1)} copy(bf16[2048,1024]{1,0:T(8,128)(2,1)} %multiply_convert_fusion) | data formatting | bytes 8388608 | tf_op jit(solution)/shard_map/convert_element_type | solution.py:70
  330.8 7.8 %reshape.49 = bf16[4,512,128,8]{1,0,3,2:T(4,128)(2,1)} reshape(bf16[2048,1024]{0,1:T(8,128)(2,1)} %copy.13) | data formatting | bytes 8388608 | tf_op jit(solution)/shard_map/reshape | solution.py:71
  338.6 5.0 copy.14
  343.6 57.8 %while.22 = (s32[]{:T(128)}, f32[128,8,256]{2,1,0:T(8,128)}, bf16[4,512,128,8]{1,3,2,0:T(8,128)(2,1)}, s32[4,512,128]{1,2,0:T(8,128)S(1)}, s32[]{:T(128)}, /*index=5*/s32[]{:T(128)}) while((s32[]{:T(128)}, f32[128,8,256]{2,1,0:T(8,128)}, bf16[4,512,128,8]{1,3,2,0:T(8,128)(2,1)}, s32[4,512,128]{1,2,0:T(8,128)S(1)}, s32[]{:T(128)}, ...), condition=%wide.region_15.16_spmd.clone, body=%wide.region_14.15_spmd.clone.sunk | while | flops 285736960 | bytes 3932255 | solution.py:84
  343.6 14.4 %fusion.49 = f32[128,8,256]{2,1,0:T(8,128)} fusion(s32[512,128]{0,1:T(8,128)S(1)} %dynamic-slice_bitcast_fusion.5, f32[128,8,256]{2,1,0:T(8,128)} %get-tuple-element.173, bf16[4,512,128,8]{1,3,2,0:T(8,128)(2,1)} %get-tuple-element.180, s32[]{:T(128)S(6)} %copy.31, pred[]{:T(512)S(6)} %compare.3), kind=kOutput, calls=%fused_computation.10.clone.3 | convolution fusion | flops 285736960 | bytes 3407877 | tf_op jit(solution)/shard_map/while/body/eval_jaxpr/pmk,pmd->mdk/dot_general | solution.py:80
  358.1 14.4 %fusion.49 = f32[128,8,256]{2,1,0:T(8,128)} fusion(s32[512,128]{0,1:T(8,128)S(1)} %dynamic-slice_bitcast_fusion.5, f32[128,8,256]{2,1,0:T(8,128)} %get-tuple-element.173, bf16[4,512,128,8]{1,3,2,0:T(8,128)(2,1)} %get-tuple-element.180, s32[]{:T(128)S(6)} %copy.31, pred[]{:T(512)S(6)} %compare.3), kind=kOutput, calls=%fused_computation.10.clone.3 | convolution fusion | flops 285736960 | bytes 3407877 | tf_op jit(solution)/shard_map/while/body/eval_jaxpr/pmk,pmd->mdk/dot_general | solution.py:80
  372.5 14.4 %fusion.49 = f32[128,8,256]{2,1,0:T(8,128)} fusion(s32[512,128]{0,1:T(8,128)S(1)} %dynamic-slice_bitcast_fusion.5, f32[128,8,256]{2,1,0:T(8,128)} %get-tuple-element.173, bf16[4,512,128,8]{1,3,2,0:T(8,128)(2,1)} %get-tuple-element.180, s32[]{:T(128)S(6)} %copy.31, pred[]{:T(512)S(6)} %compare.3), kind=kOutput, calls=%fused_computation.10.clone.3 | convolution fusion | flops 285736960 | bytes 3407877 | tf_op jit(solution)/shard_map/while/body/eval_jaxpr/pmk,pmd->mdk/dot_general | solution.py:80
  387.0 14.4 %fusion.49 = f32[128,8,256]{2,1,0:T(8,128)} fusion(s32[512,128]{0,1:T(8,128)S(1)} %dynamic-slice_bitcast_fusion.5, f32[128,8,256]{2,1,0:T(8,128)} %get-tuple-element.173, bf16[4,512,128,8]{1,3,2,0:T(8,128)(2,1)} %get-tuple-element.180, s32[]{:T(128)S(6)} %copy.31, pred[]{:T(512)S(6)} %compare.3), kind=kOutput, calls=%fused_computation.10.clone.3 | convolution fusion | flops 285736960 | bytes 3407877 | tf_op jit(solution)/shard_map/while/body/eval_jaxpr/pmk,pmd->mdk/dot_general | solution.py:80
  401.4 2.1 convert_element_type.58
  403.6 60.3 %all-reduce.5 = (f32[128]{0:T(128)S(1)}, bf16[512,1024]{1,0:T(8,128)(2,1)S(1)}) all-reduce(f32[128]{0:T(128)S(1)} %get-tuple-element.80, f32[512,1024]{1,0:T(8,128)S(1)} %convolution_multiply_fusion.1), channel_id=1, replica_groups=mesh['psg'=8,'qry'=4] {'psg'}, use_global_device_ids=true, to_apply=%region_9.10 | all-reduce | flops 524416 | bytes 3146752 | tf_op jit(solution)/shard_map/psum | solution.py:57
  463.9 9.9 %convolution_convert_fusion = bf16[512,4096]{1,0:T(8,128)(2,1)} fusion(bf16[4096,1024]{1,0:T(8,128)(2,1)} %all-gather.6.cloned.1.call-done, bf16[512,1024]{1,0:T(8,128)(2,1)S(1)} %get-tuple-element.98), kind=kOutput, calls=%fused_computation.21 | convolution fusion | flops 4297064448 | bytes 13631488 | tf_op jit(solution)/shard_map/dot_general | solution.py:93
  474.3 0.7 copy-done.3
  475.0 3.1 fusion.21
  478.1 2.2 convert_element_type.59
  480.3 68.7 %reduce-scatter.5.cloned.1.call-done = bf16[128,4096]{1,0:T(8,128)(2,1)} async-done(((bf16[512,4096]{1,0:T(8,128)(2,1)}), bf16[128,4096]{1,0:T(8,128)(2,1)}) %reduce-scatter.5.cloned.1.call-update) | async-done | bytes 1048592 | tf_op jit(solution)/shard_map/reduce_scatter | solution.py:99
  549.0 1.8 fusion.13
  550.8 2.9 fusion.18
  (42 shorter events, 2.5 us)
Async XLA Ops:
  7.2 86.0 %all-gather.4.cloned.1.call-start = ((), (), s32[]{:S(2)}) async-start(), calls=%async_computation.2 | async-start | bytes 5242880 | tf_op jit(solution)/shard_map/all_gather | solution.py:16
  7.9 139.9 %all-gather.6.cloned.1.call-start = ((), (), s32[]{:S(2)}) async-start(), calls=%async_computation.3 | async-start | bytes 9437184 | tf_op jit(solution)/shard_map/all_gather | solution.py:23
  8.6 230.7 %reduce-scatter.3.cloned.1.call-start = ((), (), s32[]{:S(2)}) async-start(), calls=%async_computation.4 | async-start | bytes 5242880 | tf_op jit(solution)/shard_map/reduce_scatter | solution.py:49
  10.3 86.2 %copy-start.4 = (f32[4096]{0:T(1024)S(1)}, f32[4096]{0:T(1024)}, u32[]{:S(2)}) copy-start(f32[4096]{0:T(1024)} %param.11) | copy-start | bytes 49156
  93.2 3.4 copy-start
  147.8 10.3 %copy-start.5 = (bf16[4,512,1024]{2,1,0:T(8,128)(2,1)S(1)}, bf16[4,512,1024]{2,1,0:T(8,128)(2,1)}, u32[]{:S(2)}) copy-start(bf16[4,512,1024]{2,1,0:T(8,128)(2,1)} %get-tuple-element.48) | copy-start | bytes 12582916
  157.1 1.0 copy-start.7
  162.4 152.3 %all-gather.8.cloned.1.call-start = ((), (), s32[]{:S(2)}) async-start(), calls=%async_computation.5 | async-start | bytes 2621440 | tf_op jit(solution)/shard_map/all_gather | solution.py:62
  269.9 208.2 %all-reduce.4.cloned.1.call-start = ((), (), s32[]{:S(2)}) async-start(), calls=%async_computation.7 | async-start | bytes 1048576 | tf_op jit(solution)/shard_map/psum | solution.py:87
  314.7 5.3 copy-start.6
  314.7 5.3 copy-start.8
  403.5 145.5 %reduce-scatter.5.cloned.1.call-start = ((), (), s32[]{:S(2)}) async-start(), calls=%async_computation.6 | async-start | bytes 5242880 | tf_op jit(solution)/shard_map/reduce_scatter | solution.py:99
  463.9 9.9 %copy-start.2 = (bf16[512,1024]{1,0:T(8,128)(2,1)}, bf16[512,1024]{1,0:T(8,128)(2,1)S(1)}, u32[]{:S(2)}) copy-start(bf16[512,1024]{1,0:T(8,128)(2,1)S(1)} %get-tuple-element.98) | copy-start | bytes 3145732
  473.8 1.2 copy-start.3
  473.8 75.2 %copy-start.1 = (bf16[128,4096]{1,0:T(8,128)(2,1)S(1)}, bf16[128,4096]{1,0:T(8,128)(2,1)}, u32[]{:S(2)}) copy-start(bf16[128,4096]{1,0:T(8,128)(2,1)} %param.10) | copy-start | bytes 3145732
Sparse Core Ops, SparseCore 0:
  9.5 83.5 all-gather.3
  95.1 52.7 all-gather.5
  162.5 76.7 reduce-scatter.2
  270.0 44.5 all-gather.7
  403.7 54.7 all-reduce.3
  473.9 75.0 reduce-scatter.4
where the time goes:
time: 562 us; the launch traced here: 561 us
  waiting for transfers between devices  260 us (46%)
  matrix products  148 us (26%)
  blocking collectives  85.4 us (15%)
  local copies, waits for them, and re-layouts  29.3 us (5%)
  other arithmetic  22.6 us (4%)
  between operations  14.2 us (3%)
    reduce_scatter x1, waiting for transfers between devices, per_device(): lax.psum_scatter(partial_value, 'qry', scatter_dimension=0, tiled=True)  76.1 us
    psum x2, blocking collectives, per_device(): row_total, positive_score = lax.psum((shifted_total, positive_part), 'psg')  72.1 us
    reduce_scatter x1, waiting for transfers between devices, per_device(): lax.psum_scatter(norm_part.astype(jnp.bfloat16), 'qry', scatter_dimension...  68.7 us
    dot_general x4, matrix products, add_book(): jnp.einsum('pmk,pmd->mdk', hot_table, grad_block, preferred_element_type=...  57.7 us
    dot_general x4, matrix products, decode(): jnp.einsum('pmk,mdk->pmd', hot_table, codebook, preferred_element_type=jn...  54.6 us
    all_gather x1, waiting for transfers between devices, per_device(): lax.all_gather(proj_weight, 'psg', axis=0, tiled=True)  47.6 us
    all_gather x1, waiting for transfers between devices, per_device(): all_grad = lax.all_gather(score_grad, 'qry', axis=0, tiled=True)  44.5 us
    all_gather x1, waiting for transfers between devices, per_device(): gathered = lax.all_gather(hidden, 'qry', axis=0, tiled=True)  21.8 us
  transfers between devices with their start and end apart: 6, of which 5 were waited for; matrix products, arithmetic and copies ran while one was open for 15% of the time, Pallas kernels for 0%

commit v1 on v0

v1 whole, which is shorter than its diff:
```python
import functools

import jax
import jax.numpy as jnp
from jax import lax
from jax.experimental import pallas as pl
from jax.experimental.pallas import tpu as pltpu
from jax.sharding import PartitionSpec as P

score_scale = 0.0625
norm_eps = 1e-06
bf16 = jnp.bfloat16
f32 = jnp.float32


def whole(array):
    rank = len(array.shape)
    return pl.BlockSpec(array.shape, lambda *step: (0,) * rank)


def cost(flops, moved, exps=0):
    return pl.CostEstimate(flops=int(flops), bytes_accessed=int(moved), transcendentals=int(exps))


def part_body(order, stack, weight, part, rows):
    count, height = part.shape[0], part.shape[1]
    for k in range(count):
        rows[pl.ds(k * height, height), :] = stack[order[k]]
    full = jnp.dot(rows[...], weight[...], preferred_element_type=f32)
    part[...] = full.reshape(part.shape)


def query_part(order, stack, weight):
    count, height, depth = order.shape[0], stack.shape[1], stack.shape[2]
    columns = weight.shape[1]
    return pl.pallas_call(
        part_body,
        grid_spec=pltpu.PrefetchScalarGridSpec(
            num_scalar_prefetch=1,
            grid=(1,),
            in_specs=[whole(stack), whole(weight)],
            out_specs=[
                pl.BlockSpec((count, height, columns), lambda i, order: (0, 0, 0)),
                pl.BlockSpec((count * height, depth), lambda i, order: (0, 0)),
            ],
        ),
        out_shape=[
            jax.ShapeDtypeStruct((count, height, columns), f32),
            jax.ShapeDtypeStruct((count * height, depth), bf16),
        ],
        cost_estimate=cost(2 * count * height * depth * columns, weight.size * 2),
        name="query_part",
    )(order, stack, weight)


def decode_body(order, codes, table, out, index):
    count, width = codes.shape[1], codes.shape[2]
    index[...] = codes[0].astype(f32).astype(jnp.int32)
    for m in range(count):
        full = jnp.broadcast_to(index[m : m + 1, :], (8, width))
        low = full & 127
        high = full >= 128
        values = table[0, 0, pl.ds(m * 8, 8), :].astype(f32)
        first, second = values[:, :128], values[:, 128:]
        pieces = []
        for c in range(width // 128):
            lanes = slice(c * 128, (c + 1) * 128)
            a = jnp.take_along_axis(first, low[:, lanes], axis=1, mode="promise_in_bounds")
            b = jnp.take_along_axis(second, low[:, lanes], axis=1, mode="promise_in_bounds")
            pieces.append(jnp.where(high[:, lanes], b, a))
        out[pl.ds(m * 8, 8), :] = jnp.concatenate(pieces, axis=1).astype(bf16)


def decode(order, codes, tables, layer):
    slices, count, width = codes.shape
    height = count * 8
    return pl.pallas_call(
        decode_body,
        grid_spec=pltpu.PrefetchScalarGridSpec(
            num_scalar_prefetch=1,
            grid=(slices,),
            in_specs=[
                pl.BlockSpec((1, count, width), lambda i, order: (i, 0, 0)),
                pl.BlockSpec(
                    (1, 1, height, tables.shape[3]), lambda i, order: (order[i], layer, 0, 0)
                ),
            ],
            out_specs=pl.BlockSpec((height, width), lambda i, order: (i, 0)),
            scratch_shapes=[pltpu.VMEM((count, width), jnp.int32)],
        ),
        out_shape=jax.ShapeDtypeStruct((slices * height, width), bf16),
        cost_estimate=cost(4 * slices * height * width * 512, slices * height * width * 2),
        name="decode",
    )(order, codes, tables)


def score_body(chunks, blocks, *refs):
    queries, tables = refs[:chunks], refs[chunks : chunks + blocks]
    target, scores, stats, held = refs[chunks + blocks :]
    step, tile = pl.program_id(0), tables[0].shape[1]
    height = queries[0].shape[1]
    rows = scores.shape[0]

    @pl.when(step == 0)
    def gather():
        for c in range(chunks):
            for b in range(blocks):
                held[b, pl.ds(c * height, height), :] = queries[c][b]

    total = jnp.dot(held[0], tables[0][...], preferred_element_type=f32)
    for b in range(1, blocks):
        total += jnp.dot(held[b], tables[b][...], preferred_element_type=f32)
    scores[:, pl.ds(pl.multiple_of(step * tile, tile), tile)] = total * score_scale

    @pl.when(step == pl.num_programs(0) - 1)
    def reduce():
        group = 64
        for r in range(rows // group):
            span = pl.ds(r * group, group)
            value = scores[span, :]
            largest = jnp.max(value, axis=1, keepdims=True)
            expsum = jnp.sum(jnp.exp(value - largest), axis=1, keepdims=True)
            column = lax.broadcasted_iota(jnp.int32, value.shape, 1)
            hit = jnp.sum(
                jnp.where(column == target[span, :], value, 0.0), axis=1, keepdims=True
            )
            lane = lax.broadcasted_iota(jnp.int32, (group, 128), 1)
            packed = jnp.where(lane == 0, largest, jnp.where(lane == 1, expsum, hit))
            stats[span, :] = packed


def scores_of(queries, tables, target):
    chunks, blocks = len(queries), len(tables)
    _, height, depth = queries[0].shape
    width = tables[0].shape[1]
    rows, tile = chunks * height, min(512, width)
    return pl.pallas_call(
        functools.partial(score_body, chunks, blocks),
        grid=(width // tile,),
        in_specs=[whole(q) for q in queries]
        + [pl.BlockSpec((depth, tile), lambda i: (0, i)) for _ in tables]
        + [whole(target)],
        out_specs=[
            pl.BlockSpec((rows, width), lambda i: (0, 0)),
            pl.BlockSpec((rows, 128), lambda i: (0, 0)),
        ],
        out_shape=[
            jax.ShapeDtypeStruct((rows, width), f32),
            jax.ShapeDtypeStruct((rows, 128), f32),
        ],
        scratch_shapes=[pltpu.VMEM((blocks, rows, depth), bf16)],
        cost_estimate=cost(
            2 * rows * blocks * depth * width, blocks * depth * width * 2, rows * width
        ),
        name="scores",
    )(*queries, *tables, target)


def grad_body(scores, largest, total, target, passages, grad, part):
    step, tile = pl.program_id(0), scores.shape[1]
    column = lax.broadcasted_iota(jnp.int32, scores.shape, 1) + step * tile
    hit = (column == target[...]).astype(f32)
    value = (jnp.exp(scores[...] - largest[...]) / total[...] - hit).astype(bf16)
    grad[...] = value
    product = lax.dot_general(
        value, passages[...], (((1,), (1,)), ((), ())), preferred_element_type=f32
    )

    @pl.when(step == 0)
    def begin():
        part[...] = product

    @pl.when(step > 0)
    def add():
        part[...] += product

    @pl.when(step == pl.num_programs(0) - 1)
    def scale():
        part[...] = part[...] * score_scale


def score_grads(scores, largest, total, target, passages):
    rows, width = scores.shape
    depth, tile = passages.shape[0], min(512, width)
    return pl.pallas_call(
        grad_body,
        grid=(width // tile,),
        in_specs=[
            pl.BlockSpec((rows, tile), lambda i: (0, i)),
            whole(largest),
            whole(total),
            whole(target),
            pl.BlockSpec((depth, tile), lambda i: (0, i)),
        ],
        out_specs=[
            pl.BlockSpec((rows, tile), lambda i: (0, i)),
            pl.BlockSpec((rows, depth), lambda i: (0, 0)),
        ],
        out_shape=[
            jax.ShapeDtypeStruct((rows, width), bf16),
            jax.ShapeDtypeStruct((rows, depth), f32),
        ],
        cost_estimate=cost(2 * rows * width * depth, rows * width * 6, rows * width),
        name="score_grads",
    )(scores, largest, total, target, passages)


def book_body(chunks, low_count, group, *refs):
    queries = refs[: 2 * chunks]
    first, second, codes, out, low_codes, high_codes = refs[2 * chunks :]
    count, width = codes.shape[1], codes.shape[2]
    high_count = 256 // low_count
    contract = (((0,), (0,)), ((), ()))
    upper = jnp.concatenate([q[0] for q in queries[:chunks]], axis=0)
    lower = jnp.concatenate([q[0] for q in queries[chunks:]], axis=0)
    grads = lax.dot_general(upper, first[...], contract, preferred_element_type=f32)
    grads += lax.dot_general(lower, second[...], contract, preferred_element_type=f32)
    grads = (grads * score_scale).astype(bf16)
    code = codes[0].astype(f32)
    high = jnp.floor(code * (1.0 / low_count))
    high_codes[...] = high
    low_codes[...] = code - high * low_count
    low_iota = lax.broadcasted_iota(jnp.int32, (low_count, 128), 0).astype(f32).astype(bf16)
    high_iota = lax.broadcasted_iota(jnp.int32, (high_count * 8, 128), 0) // 8
    high_iota = high_iota.astype(f32).astype(bf16)
    low_iota = jnp.tile(low_iota, (1, width // 128))
    high_iota = jnp.tile(high_iota, (1, width // 128))
    one, zero = jnp.ones((), bf16), jnp.zeros((), bf16)
    for g in range(count // group):
        hots, masked = [], []
        for m in range(g * group, (g + 1) * group):
            low = jnp.broadcast_to(low_codes[m : m + 1, :].astype(bf16), (low_count, width))
            top = jnp.broadcast_to(high_codes[m : m + 1, :].astype(bf16), (high_count * 8, width))
            grad = jnp.tile(grads[m * 8 : (m + 1) * 8, :], (high_count, 1))
            hots.append(jnp.where(low == low_iota, one, zero))
            masked.append(jnp.where(top == high_iota, grad, zero))
        product = lax.dot_general(
            jnp.concatenate(masked, axis=0),
            jnp.concatenate(hots, axis=0),
            (((1,), (1,)), ((), ())),
            preferred_element_type=f32,
        )
        for i in range(group):
            height = high_count * 8
            block = product[i * height : (i + 1) * height, i * low_count : (i + 1) * low_count]
            out[g * group + i] = jnp.concatenate(
                [block[b * 8 : (b + 1) * 8, :] for b in range(high_count)], axis=1
            )


def book_grads(queries, grads, codes):
    chunks = len(queries) // 2
    height = queries[0].shape[1]
    slices, count, width = codes.shape
    span = count * 8
    return pl.pallas_call(
        functools.partial(book_body, chunks, 64, 4),
        grid=(slices,),
        in_specs=[pl.BlockSpec((1, height, span), lambda i: (0, 0, i)) for _ in queries]
        + [whole(g) for g in grads]
        + [pl.BlockSpec((1, count, width), lambda i: (i, 0, 0))],
        out_specs=pl.BlockSpec((count, 8, 256), lambda i: (i, 0, 0)),
        out_shape=jax.ShapeDtypeStruct((slices * count, 8, 256), f32),
        scratch_shapes=[pltpu.VMEM((count, width), f32), pltpu.VMEM((count, width), f32)],
        cost_estimate=cost(8 * slices * span * width * 512, slices * span * width * 2),
        name="book_grads",
    )(*queries, *grads, codes)


def back_body(chunks, *refs):
    pieces, weight, out, rows = refs[:chunks], refs[chunks], refs[chunks + 1], refs[chunks + 2]
    height = pieces[0].shape[0]
    for c in range(chunks):
        rows[pl.ds(c * height, height), :] = pieces[c][...]
    out[...] = lax.dot_general(
        rows[...], weight[...], (((1,), (1,)), ((), ())), preferred_element_type=f32
    ).astype(bf16)


def back_part(pieces, weight):
    height, depth = pieces[0].shape
    rows = height * len(pieces)
    return pl.pallas_call(
        functools.partial(back_body, len(pieces)),
        grid=(1,),
        in_specs=[whole(p) for p in pieces] + [whole(weight)],
        out_specs=[
            pl.BlockSpec((rows, weight.shape[0]), lambda i: (0, 0)),
            pl.BlockSpec((rows, depth), lambda i: (0, 0)),
        ],
        out_shape=[
            jax.ShapeDtypeStruct((rows, weight.shape[0]), bf16),
            jax.ShapeDtypeStruct((rows, depth), bf16),
        ],
        cost_estimate=cost(2 * rows * weight.size, rows * depth * 4),
        name="back_part",
    )(*pieces, weight)


def tail_body(chunks, order, *refs):
    pieces = refs[:chunks]
    hidden, gain, inverse, out = refs[chunks:]
    width = pieces[0].shape[1]
    dots = jnp.zeros((hidden.shape[0], 1), f32)
    for c in range(chunks):
        lanes = pl.ds(pl.multiple_of(order[c] * width, width), width)
        scaled = pieces[c][...] * gain[:, lanes]
        dots += jnp.sum(scaled * hidden[:, lanes].astype(f32), axis=1, keepdims=True)
    scale = inverse[...]
    mean = dots * (1.0 / (chunks * width))
    factor = scale * scale * scale * mean
    for c in range(chunks):
        lanes = pl.ds(pl.multiple_of(order[c] * width, width), width)
        scaled = pieces[c][...] * gain[:, lanes]
        out[:, lanes] = (scale * scaled - hidden[:, lanes].astype(f32) * factor).astype(bf16)


def hidden_tail(order, pieces, hidden, gain, inverse):
    return pl.pallas_call(
        functools.partial(tail_body, len(pieces)),
        grid_spec=pltpu.PrefetchScalarGridSpec(
            num_scalar_prefetch=1,
            grid=(1,),
            in_specs=[whole(p) for p in pieces] + [whole(hidden), whole(gain), whole(inverse)],
            out_specs=whole(hidden),
        ),
        out_shape=jax.ShapeDtypeStruct(hidden.shape, bf16),
        cost_estimate=cost(8 * hidden.size, hidden.size * 8),
        name="hidden_tail",
    )(order, *pieces, hidden, gain, inverse)


def reorder_body(order, source, out):
    out[...] = source[...]


def reorder(order, source):
    shape = source.shape
    rest = (0,) * (len(shape) - 1)
    return pl.pallas_call(
        reorder_body,
        grid_spec=pltpu.PrefetchScalarGridSpec(
            num_scalar_prefetch=1,
            grid=(shape[0],),
            in_specs=[pl.BlockSpec((1,) + shape[1:], lambda i, order: (order[i],) + rest)],
            out_specs=pl.BlockSpec((1,) + shape[1:], lambda i, order: (i,) + rest),
        ),
        out_shape=jax.ShapeDtypeStruct(shape, source.dtype),
        name="reorder",
    )(order, source)


def per_device(hidden, norm_gain, proj_weight, pq_codes, codebook, positives):
    shards, owners = lax.axis_size("psg"), lax.axis_size("qry")
    shard, owner = lax.axis_index("psg"), lax.axis_index("qry")
    half = shards // 2
    place = (shard % 2) * half + shard // 2
    steps = jnp.arange(shards, dtype=jnp.int32)
    swapped = steps ^ place

    def core(x):
        return lax.ppermute(x, "psg", [(i, i ^ 1) for i in range(shards)])

    def chip(x, k):
        return lax.ppermute(x, "psg", [(i, i ^ (2 * k)) for i in range(shards)])

    def turn(x, k):
        return lax.ppermute(x, "qry", [(i, (i + k) % owners) for i in range(owners)])

    def collect(x):
        near = [x] + [chip(x, k) for k in range(1, half)]
        return near, [core(piece) for piece in near]

    own_rows, features = hidden.shape
    row_span, columns = proj_weight.shape
    passage_count, sub_count = pq_codes.shape
    queries_all = own_rows * owners
    chunk = queries_all // shards
    per_owner = own_rows // chunk

    floats = hidden.astype(f32)
    inverse = lax.rsqrt(jnp.mean(floats * floats, axis=1, keepdims=True) + norm_eps)
    normed = (floats * inverse * norm_gain[None, :]).astype(bf16)
    slice_own = lax.dynamic_slice_in_dim(normed, shard * row_span, row_span, 1)
    slices = [slice_own] + [turn(slice_own, k) for k in range(1, owners)]
    stack = jnp.concatenate(slices, axis=0).reshape(shards, chunk, row_span)
    from_owner = (owner - swapped // per_owner) % owners
    where_in = from_owner * per_owner + swapped % per_owner

    book_rows = sub_count // shards
    codes_own = pq_codes.astype(bf16).T.reshape(shards, book_rows, passage_count)
    book_own = codebook.reshape(shards, 1, book_rows * 8, codebook.shape[2])
    book_slice = lax.dynamic_index_in_dim(book_own, place, 0, keepdims=False)
    book_slices = jnp.concatenate([turn(book_slice, k) for k in range(1, owners)], axis=0)
    near, far = collect(book_slices)
    books = jnp.stack(near + far)
    codes = [codes_own] + [turn(codes_own, k) for k in range(1, owners)]
    passages = [decode(steps, codes_own, book_own, 0)]
    for k in range(1, owners):
        passages.append(decode(swapped, codes[k], books, k - 1))

    far_part, far_rows = query_part(where_in[half:], stack, proj_weight)
    near_part, near_rows = query_part(where_in[:half], stack, proj_weight)

    def scatter_sum(near_term, far_term):
        summed = near_term + core(far_term)
        total = summed[0]
        for k in range(1, half):
            total = total + chip(summed[k], k)
        return total

    query_own = scatter_sum(near_part, far_part).astype(bf16)
    query_blocks = jnp.stack([query_own] + [turn(query_own, k) for k in range(1, owners)])
    near_queries, far_queries = collect(query_blocks)

    targets = positives.reshape(shards, chunk)[swapped].reshape(2, half * chunk, 1)
    targets = targets - shard * passage_count
    near_scores, near_stats = scores_of(near_queries, passages, targets[0])
    far_scores, far_stats = scores_of(far_queries, passages, targets[1])

    stats = jnp.stack([near_stats[:, :3].T, far_stats[:, :3].T], axis=1)
    stats = stats.reshape(3, 2, half, chunk)

    def merge(values):
        largest = functools.reduce(jnp.maximum, [v[0] for v in values])
        total = sum(v[1] * jnp.exp(v[0] - largest) for v in values)
        return jnp.stack([largest, total, sum(v[2] for v in values)])

    stats = merge([stats, core(stats)[:, ::-1]])
    others = []
    for k in range(1, half):
        other = chip(stats, k)
        others.append(jnp.stack([other[:, :, i ^ k] for i in range(half)], axis=2))
    stats = merge([stats] + others)
    row_max, row_total, positive_score = stats.reshape(3, 2, half * chunk, 1)
    losses_all = (jnp.log(row_total) + row_max - positive_score).reshape(-1)

    far_grad, far_term = score_grads(
        far_scores, row_max[1], row_total[1], targets[1], passages[0]
    )
    near_grad, near_term = score_grads(
        near_scores, row_max[0], row_total[0], targets[0], passages[0]
    )
    query_grad = scatter_sum(
        near_term.reshape(half, chunk, columns), far_term.reshape(half, chunk, columns)
    ).astype(bf16)
    near_pieces, far_pieces = collect(query_grad)

    group = min(sub_count, 16)
    book_part = book_grads(
        near_queries + far_queries,
        [near_grad, far_grad],
        codes_own.reshape(sub_count // group, group, passage_count),
    )
    book_part = reorder(swapped, book_part.reshape(shards, book_rows * 8, 256))
    book_half = book_part[:half] + core(book_part[half:])
    book_sum = book_half[0]
    for k in range(1, half):
        book_sum = book_sum + chip(book_half[k].astype(bf16), k).astype(f32)
    near_books, far_books = collect(book_sum)
    codebook_grad = reorder(swapped, jnp.stack(near_books + far_books)).reshape(codebook.shape)

    back, grad_rows = back_part(near_pieces + far_pieces, proj_weight)
    normed_rows = jnp.concatenate([near_rows, far_rows], axis=0)
    weight_grad = lax.dot_general(
        normed_rows, grad_rows, (((0,), (0,)), ((), ())), preferred_element_type=f32
    )

    def rows_of(array, who):
        first = (who ^ (place // per_owner)) * own_rows
        return lax.dynamic_slice_in_dim(array, first, own_rows, 0)

    def straighten(array):
        bit = 1
        while bit < per_owner:
            shaped = array.reshape((per_owner // (2 * bit), 2, bit * chunk) + array.shape[1:])
            turned = shaped[:, ::-1].reshape(array.shape)
            array = jnp.where((place // bit) % 2 == 1, turned, array)
            bit *= 2
        return array

    back_sum = rows_of(back, owner).astype(f32)
    for k in range(1, owners):
        back_sum = back_sum + turn(rows_of(back, (owner + k) % owners), k).astype(f32)
    back_sum = straighten(back_sum)
    near_back, far_back = collect(back_sum)
    shard_of = (swapped % half) * 2 + swapped // half
    hidden_grad = hidden_tail(
        shard_of, near_back + far_back, hidden, norm_gain[None, :], inverse
    )
    losses = straighten(rows_of(losses_all, owner))
    return (losses, hidden_grad, weight_grad, codebook_grad)


def solution(mesh):
    in_specs = (P("qry", None), P(), P("psg", "qry"), P("psg", "qry"), P("qry", None, None), P())
    out_specs = (P("qry"), P("qry", None), P("psg", "qry"), P("qry", None, None))
    return jax.shard_map(
        per_device, mesh=mesh, in_specs=in_specs, out_specs=out_specs, check_vma=False
    )
```

time: 562 us -> 301 us (0.54)
  waiting for transfers between devices: 260 us -> 75.1 us
  matrix products: 148 us -> 2.04 us
  Pallas kernels: 0 us -> 119 us
  blocking collectives: 85.4 us -> 0 us
  starting transfers between devices: 0.42 us -> 62.4 us
  other arithmetic: 22.6 us -> 7.5 us
  between operations: 14.2 us -> 1.28 us
    dot_general x14 -> x1, matrix products: 148 us -> 2.04 us  [per_device(): lax.dot_general(normed_rows, grad_rows, (((0,), (0,)), ((), ())), preferr...]
    reduce_scatter x2 -> x0, waiting for transfers between devices: 145 us -> none  [the longest x1 76.1 us: per_device(): lax.psum_scatter(partial_value, 'qry', scatter_dimension=0, tiled=True)]
    pallas_call x0 -> x15, Pallas kernels: none -> 119 us  [the longest x4 38.1 us: decode(): pl.pallas_call(decode_body, grid_spec=pltpu.PrefetchScalarGridSpec(num_sc...]
    all_gather x3 -> x0, waiting for transfers between devices: 114 us -> none  [the longest x1 47.6 us: per_device(): lax.all_gather(proj_weight, 'psg', axis=0, tiled=True)]
    ppermute x0 -> x66, waiting for transfers between devices: none -> 75.1 us  [the longest x15 43.5 us: turn(): lax.ppermute(x, 'qry', [(i, (i + k) % owners) for i in range(owners)])]
    psum x2 -> x0, blocking collectives: 72.1 us -> none  [per_device(): row_total, positive_score = lax.psum((shifted_total, positive_part), 'psg')]
    ppermute x0 -> x66, starting transfers between devices: none -> 62.4 us  [the longest x27 32.2 us: chip(): return lax.ppermute(x, 'psg', [(i, i ^ 2 * k) for i in range(shards)])]
    pmax x1 -> x0, blocking collectives: 13.3 us -> none  [per_device(): row_max = lax.pmax(local_max, 'psg')]
  transfers between devices with their start and end apart: 6 -> 66, of which waited for: 5 -> 24; matrix products, arithmetic and copies ran while one was open for 15% -> 9% of each run, Pallas kernels for 0% -> 22%
where the time goes in v1:
time: 301 us; the launch traced here: 298 us
  Pallas kernels  119 us (40%)
  waiting for transfers between devices  75.1 us (25%)
  starting transfers between devices  62.4 us (21%)
  local copies, waits for them, and re-layouts  31.1 us (10%)
  other arithmetic  7.5 us (2%)
    ppermute x15, waiting for transfers between devices, turn(): lax.ppermute(x, 'qry', [(i, (i + k) % owners) for i in range(owners)])  43.5 us
    pallas_call x4, Pallas kernels, decode(): pl.pallas_call(decode_body, grid_spec=pltpu.PrefetchScalarGridSpec(num_sc...  38.1 us
    ppermute x27, starting transfers between devices, chip(): return lax.ppermute(x, 'psg', [(i, i ^ 2 * k) for i in range(shards)])  32.2 us
    ppermute x27, waiting for transfers between devices, chip(): return lax.ppermute(x, 'psg', [(i, i ^ 2 * k) for i in range(shards)])  30.6 us
    ppermute x15, starting transfers between devices, turn(): lax.ppermute(x, 'qry', [(i, (i + k) % owners) for i in range(owners)])  24.5 us
    pallas_call x2, Pallas kernels, scores_of(): pl.pallas_call(functools.partial(score_body, chunks, blocks), grid=(width...  23.5 us
    pallas_call x1, Pallas kernels, book_grads(): pl.pallas_call(functools.partial(book_body, chunks, 64, 4), grid=(slices,...  18.2 us
    unnamed x83, local copies, waits for them, and re-layouts  12.8 us
  transfers between devices with their start and end apart: 66, of which 24 were waited for; matrix products, arithmetic and copies ran while one was open for 9% of the time, Pallas kernels for 22%

profile of v1, /device:TPU:0, one launch (start us, length us, event | category | flops | bytes accessed | tf_op | source)
XLA Modules:
  0.0 298.0 jit_solution(11487211453078764661)
XLA Ops:
  0.7 1.6 convert_element_type.48
  3.4 5.1 %collective-permute-start.2 = (bf16[128,512]{1,0:T(8,128)(2,1)S(1)}, bf16[128,512]{1,0:T(8,128)(2,1)S(1)}, u32[]{:S(2)}, u32[]{:S(2)}) collective-permute-start(bf16[128,512]{1,0:T(8,128)(2,1)S(1)} %fusion.13), channel_id=1, source_target_pairs={{0,3},{1,0},{2,1},{3,2},{4,7},{5,4},{6,5},{7,6},{8,11},{9,8},{10,9... | collective-permute-start | bytes 393224 | tf_op jit(solution)/shard_map/ppermute | solution.py:368
  10.6 2.5 collective-permute-start.13
  15.1 9.6 %decode.4.refs_4_.passages = bf16[1024,2048]{1,0:T(8,128)(2,1)} custom-call(s32[8]{0:T(128)} %iota.9.order, bf16[8,16,2048]{2,1,0:T(8,128)(2,1)} %bitcast.10.codes.refs_10_, bf16[8,1,128,256]{3,2,1,0:T(8,128)(2,1)} %bitcast.205), custom_call_target="tpu_custom_call" | custom-call | flops 4294967296 | bytes 4194304 | tf_op jit(solution)/shard_map/decode/pallas_call | solution.py:77
  27.5 3.0 %collective-permute-done.14 = bf16[1,128,256]{2,1,0:T(8,128)(2,1)S(1)} collective-permute-done((bf16[1,128,256]{2,1,0:T(8,128)(2,1)S(1)}, bf16[1,128,256]{2,1,0:T(8,128)(2,1)S(1)}, u32[]{:S(2)}, u32[]{:S(2)}) %collective-permute-start.14) | collective-permute-done | bytes 65568 | tf_op jit(solution)/shard_map/ppermute | solution.py:368
  30.6 4.5 %collective-permute-start.15 = (bf16[1,128,256]{2,1,0:T(8,128)(2,1)S(1)}, bf16[1,128,256]{2,1,0:T(8,128)(2,1)S(1)}, u32[]{:S(2)}, u32[]{:S(2)}) collective-permute-start(bf16[1,128,256]{2,1,0:T(8,128)(2,1)S(1)} %dynamic-slice_bitcast_fusion), channel_id=1, source_target_pairs={{0,2},{1,3},{2,0},{3,1},{4,6},{5,7},{6,4},{7,5},{8,10},{9,11},{10,... | collective-permute-start | bytes 196616 | tf_op jit(solution)/shard_map/ppermute | solution.py:368
  35.0 2.9 collective-permute-done.15
  38.3 4.0 %collective-permute-done.16 = bf16[1,128,256]{2,1,0:T(8,128)(2,1)S(1)} collective-permute-done((bf16[1,128,256]{2,1,0:T(8,128)(2,1)S(1)}, bf16[1,128,256]{2,1,0:T(8,128)(2,1)S(1)}, u32[]{:S(2)}, u32[]{:S(2)}) %collective-permute-start.16) | collective-permute-done | bytes 65568 | tf_op jit(solution)/shard_map/ppermute | solution.py:368
  47.3 3.5 %query_part.2 = (f32[4,64,1024]{2,1,0:T(8,128)}, bf16[256,512]{1,0:T(8,128)(2,1)}) custom-call(s32[4]{0:T(128)} %get-tuple-element.87.order, bf16[8,64,512]{2,1,0:T(8,128)(2,1)} %bitcast.187, bf16[512,1024]{1,0:T(8,128)(2,1)} %refs_8_.2), custom_call_target="tpu_custom_call" | custom-call | flops 268435456 | bytes 1048576 | tf_op jit(solution)/shard_map/query_part/pallas_call | solution.py:36
  50.7 3.6 %query_part.3 = (f32[4,64,1024]{2,1,0:T(8,128)}, bf16[256,512]{1,0:T(8,128)(2,1)}) custom-call(s32[4]{0:T(128)} %get-tuple-element.86.order, bf16[8,64,512]{2,1,0:T(8,128)(2,1)} %bitcast.188, bf16[512,1024]{1,0:T(8,128)(2,1)} %refs_8_.2), custom_call_target="tpu_custom_call" | custom-call | flops 268435456 | bytes 1048576 | tf_op jit(solution)/shard_map/query_part/pallas_call | solution.py:36
  59.1 2.5 collective-permute-start.6
  63.4 2.2 collective-permute-start.24
  66.3 3.0 %collective-permute-done.6 = f32[64,1024]{1,0:T(8,128)S(1)} collective-permute-done((f32[64,1024]{1,0:T(8,128)S(1)}, f32[64,1024]{1,0:T(8,128)S(1)}, u32[]{:S(2)}, u32[]{:S(2)}) %collective-permute-start.6) | collective-permute-done | bytes 262176 | tf_op jit(solution)/shard_map/ppermute | solution.py:365
  69.3 2.1 collective-permute-start.25
  71.4 3.0 %collective-permute-done.5 = f32[64,1024]{1,0:T(8,128)S(1)} collective-permute-done((f32[64,1024]{1,0:T(8,128)S(1)}, f32[64,1024]{1,0:T(8,128)S(1)}, u32[]{:S(2)}, u32[]{:S(2)}) %collective-permute-start.5) | collective-permute-done | bytes 262176 | tf_op jit(solution)/shard_map/ppermute | solution.py:365
  74.6 2.2 collective-permute-start.9
  76.9 1.9 collective-permute-start.7
  78.9 9.5 %decode.5.refs_5_ = bf16[1024,2048]{1,0:T(8,128)(2,1)} custom-call(s32[8]{0:T(128)} %iota_xor_fusion.order, bf16[8,16,2048]{2,1,0:T(8,128)(2,1)} %copy-done.31, bf16[8,3,128,256]{3,2,1,0:T(8,128)(2,1)} %bitcast_dynamic-update-slice_fusion.table), custom_call_target="tpu_custom_call" | custom-call | flops 4294967296 | bytes 4194304 | tf_op jit(solution)/shard_map/decode/pallas_call | solution.py:77
  88.4 10.7 %collective-permute-done.9 = bf16[64,1024]{1,0:T(8,128)(2,1)S(1)} collective-permute-done((bf16[64,1024]{1,0:T(8,128)(2,1)S(1)}, bf16[64,1024]{1,0:T(8,128)(2,1)S(1)}, u32[]{:S(2)}, u32[]{:S(2)}) %collective-permute-start.9) | collective-permute-done | bytes 131104 | tf_op jit(solution)/shard_map/ppermute | solution.py:368
  99.1 12.6 %collective-permute-done.8 = bf16[64,1024]{1,0:T(8,128)(2,1)S(1)} collective-permute-done((bf16[64,1024]{1,0:T(8,128)(2,1)S(1)}, bf16[64,1024]{1,0:T(8,128)(2,1)S(1)}, u32[]{:S(2)}, u32[]{:S(2)}) %collective-permute-start.8) | collective-permute-done | bytes 131104 | tf_op jit(solution)/shard_map/ppermute | solution.py:368
  111.8 1.6 collective-permute-start.10
  116.1 9.5 %decode.6.refs_6_ = bf16[1024,2048]{1,0:T(8,128)(2,1)} custom-call(s32[8]{0:T(128)} %iota_xor_fusion.order, bf16[8,16,2048]{2,1,0:T(8,128)(2,1)} %copy-done.32, bf16[8,3,128,256]{3,2,1,0:T(8,128)(2,1)} %bitcast_dynamic-update-slice_fusion.table), custom_call_target="tpu_custom_call" | custom-call | flops 4294967296 | bytes 4194304 | tf_op jit(solution)/shard_map/decode/pallas_call | solution.py:77
  125.6 9.5 %decode.7.refs_7_ = bf16[1024,2048]{1,0:T(8,128)(2,1)} custom-call(s32[8]{0:T(128)} %iota_xor_fusion.order, bf16[8,16,2048]{2,1,0:T(8,128)(2,1)} %collective-permute-done.25.codes, bf16[8,3,128,256]{3,2,1,0:T(8,128)(2,1)} %bitcast_dynamic-update-slice_fusion.table), custom_call_target="tpu_custom_call" | custom-call | flops 4294967296 | bytes 4194304 | tf_op jit(solution)/shard_map/decode/pallas_call | solution.py:77
  135.7 2.3 collective-permute-done.11.refs_2_
  138.9 11.7 %scores.2 = (f32[256,2048]{1,0:T(8,128)}, f32[256,128]{1,0:T(8,128)}) custom-call(bf16[4,64,1024]{2,1,0:T(8,128)(2,1)} %copy-done.2, bf16[4,64,1024]{2,1,0:T(8,128)(2,1)} %copy-done.9, bf16[4,64,1024]{2,1,0:T(8,128)(2,1)} %copy-done.10, bf16[4,64,1024]{2,1,0:T(8,128)(2,1)} %copy-done.11, bf16[1024,2048]{1,0:T(8,128)(2,1)} %decode.4.refs_4_.passages, ...), custom_call_target="tpu_custom_call" | custom-call | flops 4294967296 | bytes 16777216 | tf_op jit(solution)/shard_map/scores/pallas_call | solution.py:137
  152.8 11.7 %scores.3 = (f32[256,2048]{1,0:T(8,128)}, f32[256,128]{1,0:T(8,128)}) custom-call(bf16[4,64,1024]{2,1,0:T(8,128)(2,1)} %copy-done.12, bf16[4,64,1024]{2,1,0:T(8,128)(2,1)} %copy-done.13, bf16[4,64,1024]{2,1,0:T(8,128)(2,1)} %collective-permute-done.28.refs_2_.refs_6_, bf16[4,64,1024]{2,1,0:T(8,128)(2,1)} %collective-permute-done.29.refs_3_.refs_7_, ...), custom_call_target="tpu_custom_call" | custom-call | flops 4294967296 | bytes 16777216 | tf_op jit(solution)/shard_map/scores/pallas_call | solution.py:137
  168.9 1.9 collective-permute-start.33
  171.4 2.1 collective-permute-done.33
  177.8 6.1 %score_grads.2 = (bf16[256,2048]{1,0:T(8,128)(2,1)}, f32[256,1024]{1,0:T(8,128)}) custom-call(f32[256,2048]{1,0:T(8,128)} %get-tuple-element.22.scores, f32[256,1]{1,0:T(8,128)} %squeeze.159.largest, f32[256,1]{1,0:T(8,128)} %squeeze.160.total, s32[256,1]{1,0:T(8,128)} %squeeze.163.refs_8_.target, bf16[1024,2048]{1,0:T(8,128)(2,1)} %decode.4.refs_4_.passages), custom_call_target="tpu_custom_call" | custom-call | flops 1073741824 | bytes 3145728 | tf_op jit(solution)/shard_map/score_grads/pallas_call | solution.py:185
  183.9 6.2 %score_grads.3 = (bf16[256,2048]{1,0:T(8,128)(2,1)}, f32[256,1024]{1,0:T(8,128)}) custom-call(f32[256,2048]{1,0:T(8,128)} %get-tuple-element.24.scores, f32[256,1]{1,0:T(8,128)} %squeeze.161.largest, f32[256,1]{1,0:T(8,128)} %squeeze.162.total, s32[256,1]{1,0:T(8,128)} %squeeze.164.refs_8_.target, bf16[1024,2048]{1,0:T(8,128)(2,1)} %decode.4.refs_4_.passages), custom_call_target="tpu_custom_call" | custom-call | flops 1073741824 | bytes 3145728 | tf_op jit(solution)/shard_map/score_grads/pallas_call | solution.py:185
  190.1 18.2 %book_grads.1 = f32[128,8,256]{2,1,0:T(8,128)} custom-call(bf16[4,64,1024]{2,1,0:T(8,128)(2,1)} %copy-done.2, bf16[4,64,1024]{2,1,0:T(8,128)(2,1)} %copy-done.9, bf16[4,64,1024]{2,1,0:T(8,128)(2,1)} %copy-done.10, bf16[4,64,1024]{2,1,0:T(8,128)(2,1)} %copy-done.11, bf16[4,64,1024]{2,1,0:T(8,128)(2,1)} %copy-done.12, bf16[4,64,1024]{2,1,0:T(8,128)(2,1)} %copy-done.13, ...), custom_call_target="tpu_custom_call" | custom-call | flops 8589934592 | bytes 4194304 | tf_op jit(solution)/shard_map/book_grads/pallas_call | solution.py:256
  208.3 5.9 %reorder.2 = f32[8,128,256]{2,1,0:T(8,128)} custom-call(s32[8]{0:T(128)} %iota_xor_fusion.order, f32[8,128,256]{2,1,0:T(8,128)} %bitcast.192), custom_call_target="tpu_custom_call" | custom-call | tf_op jit(solution)/shard_map/reorder/pallas_call | solution.py:340
  214.1 2.0 slice.276
  223.6 1.6 collective-permute-done.58
  234.5 6.9 %collective-permute-done.60 = f32[128,256]{1,0:T(8,128)} collective-permute-done((f32[128,256]{1,0:T(8,128)S(1)}, f32[128,256]{1,0:T(8,128)}, u32[]{:S(2)}, u32[]{:S(2)}) %collective-permute-start.60) | collective-permute-done | bytes 131104 | tf_op jit(solution)/shard_map/ppermute | solution.py:365
  242.9 3.2 %collective-permute-done.36 = f32[64,1024]{1,0:T(8,128)S(1)} collective-permute-done((f32[64,1024]{1,0:T(8,128)S(1)}, f32[64,1024]{1,0:T(8,128)S(1)}, u32[]{:S(2)}, u32[]{:S(2)}) %collective-permute-start.36) | collective-permute-done | bytes 262176 | tf_op jit(solution)/shard_map/ppermute | solution.py:365
  248.2 1.6 collective-permute-start.40
  249.9 2.4 collective-permute-done.38.refs_1_
  252.2 2.7 collective-permute-done.39.refs_2_
  257.6 3.3 %back_part.1 = (bf16[512,512]{1,0:T(8,128)(2,1)}, bf16[512,1024]{1,0:T(8,128)(2,1)}) custom-call(bf16[64,1024]{1,0:T(8,128)(2,1)} %copy-done.14, bf16[64,1024]{1,0:T(8,128)(2,1)} %copy-done.23, bf16[64,1024]{1,0:T(8,128)(2,1)} %copy-done.24, bf16[64,1024]{1,0:T(8,128)(2,1)} %copy-done.25, bf16[64,1024]{1,0:T(8,128)(2,1)} %copy-done.26, ...), custom_call_target="tpu_custom_call" | custom-call | flops 536870912 | bytes 2097152 | tf_op jit(solution)/shard_map/back_part/pallas_call | solution.py:283
  262.5 1.9 collective-permute-start.45
  264.5 4.4 %collective-permute-done.47 = bf16[128,512]{1,0:T(8,128)(2,1)S(1)} collective-permute-done((bf16[128,512]{1,0:T(8,128)(2,1)S(1)}, bf16[128,512]{1,0:T(8,128)(2,1)S(1)}, u32[]{:S(2)}, u32[]{:S(2)}) %collective-permute-start.47) | collective-permute-done | bytes 131104 | tf_op jit(solution)/shard_map/ppermute | solution.py:368
  268.9 5.8 %collective-permute-done.46 = bf16[128,512]{1,0:T(8,128)(2,1)S(1)} collective-permute-done((bf16[128,512]{1,0:T(8,128)(2,1)S(1)}, bf16[128,512]{1,0:T(8,128)(2,1)S(1)}, u32[]{:S(2)}, u32[]{:S(2)}) %collective-permute-start.46) | collective-permute-done | bytes 131104 | tf_op jit(solution)/shard_map/ppermute | solution.py:368
  277.7 1.6 collective-permute-start.50
  282.1 5.9 %reorder.3 = f32[8,128,256]{2,1,0:T(8,128)} custom-call(s32[8]{0:T(128)} %iota_xor_fusion.order, f32[8,128,256]{2,1,0:T(8,128)} %copy-done.3), custom_call_target="tpu_custom_call" | custom-call | tf_op jit(solution)/shard_map/reorder/pallas_call | solution.py:340
  288.5 1.6 collective-permute-done.49.refs_2_
  290.6 2.0 fusion
  293.6 4.4 %hidden_tail.1 = bf16[128,4096]{1,0:T(8,128)(2,1)} custom-call(s32[8]{0:T(128)} %fusion.36.order, f32[128,512]{1,0:T(8,128)} %copy-done.7, f32[128,512]{1,0:T(8,128)} %copy-done.17, f32[128,512]{1,0:T(8,128)} %copy-done.18, f32[128,512]{1,0:T(8,128)} %collective-permute-done.50.refs_3_, f32[128,512]{1,0:T(8,128)} %copy-done.19, f32[128,512]{1,0:T(8,128)} %copy-done.20, ...), custom_call_target="tpu_custom_call" | custom-call | flops 4194304 | bytes 4194304 | tf_op jit(solution)/shard_map/hidden_tail/pallas_call | solution.py:319
  (271 shorter events, 68.7 us)
Async XLA Ops:
  3.4 41.0 %collective-permute-start.2 = (bf16[128,512]{1,0:T(8,128)(2,1)S(1)}, bf16[128,512]{1,0:T(8,128)(2,1)S(1)}, u32[]{:S(2)}, u32[]{:S(2)}) collective-permute-start(bf16[128,512]{1,0:T(8,128)(2,1)S(1)} %fusion.13), channel_id=1, source_target_pairs={{0,3},{1,0},{2,1},{3,2},{4,7},{5,4},{6,5},{7,6},{8,11},{9,8},{10,9... | collective-permute-start | bytes 393224 | tf_op jit(solution)/shard_map/ppermute | solution.py:368
  8.5 37.4 %collective-permute-start.1 = (bf16[128,512]{1,0:T(8,128)(2,1)S(1)}, bf16[128,512]{1,0:T(8,128)(2,1)S(1)}, u32[]{:S(2)}, u32[]{:S(2)}) collective-permute-start(bf16[128,512]{1,0:T(8,128)(2,1)S(1)} %fusion.13), channel_id=1, source_target_pairs={{0,2},{1,3},{2,0},{3,1},{4,6},{5,7},{6,4},{7,5},{8,10},{9,11},{10,... | collective-permute-start | bytes 393224 | tf_op jit(solution)/shard_map/ppermute | solution.py:368
  8.5 37.9 %collective-permute-start = (bf16[128,512]{1,0:T(8,128)(2,1)S(1)}, bf16[128,512]{1,0:T(8,128)(2,1)S(1)}, u32[]{:S(2)}, u32[]{:S(2)}) collective-permute-start(bf16[128,512]{1,0:T(8,128)(2,1)S(1)} %fusion.13), channel_id=1, source_target_pairs={{0,1},{1,2},{2,3},{3,0},{4,5},{5,6},{6,7},{7,4},{8,9},{9,10},{10,1... | collective-permute-start | bytes 393224 | tf_op jit(solution)/shard_map/ppermute | solution.py:368
  10.6 66.3 %collective-permute-start.13 = (bf16[8,16,2048]{2,1,0:T(8,128)(2,1)}, bf16[8,16,2048]{2,1,0:T(8,128)(2,1)S(1)}, u32[]{:S(2)}, u32[]{:S(2)}) collective-permute-start(bf16[8,16,2048]{2,1,0:T(8,128)(2,1)} %bitcast.10.codes.refs_10_), channel_id=1, source_target_pairs={{0,1},{1,2},{2,3},{3,0},{4,5},{5,6},{6,7},{7,4},{8,9},{9,10},{10,1... | collective-permute-start | bytes 1572872 | tf_op jit(solution)/shard_map/ppermute | solution.py:368
  13.9 16.6 %collective-permute-start.14 = (bf16[1,128,256]{2,1,0:T(8,128)(2,1)S(1)}, bf16[1,128,256]{2,1,0:T(8,128)(2,1)S(1)}, u32[]{:S(2)}, u32[]{:S(2)}) collective-permute-start(bf16[1,128,256]{2,1,0:T(8,128)(2,1)S(1)} %dynamic-slice_bitcast_fusion), channel_id=1, source_target_pairs={{0,1},{1,2},{2,3},{3,0},{4,5},{5,6},{6,7},{7,4},{8,9},{9,10},{10,1... | collective-permute-start | bytes 196616 | tf_op jit(solution)/shard_map/ppermute | solution.py:368
  30.6 7.4 %collective-permute-start.15 = (bf16[1,128,256]{2,1,0:T(8,128)(2,1)S(1)}, bf16[1,128,256]{2,1,0:T(8,128)(2,1)S(1)}, u32[]{:S(2)}, u32[]{:S(2)}) collective-permute-start(bf16[1,128,256]{2,1,0:T(8,128)(2,1)S(1)} %dynamic-slice_bitcast_fusion), channel_id=1, source_target_pairs={{0,2},{1,3},{2,0},{3,1},{4,6},{5,7},{6,4},{7,5},{8,10},{9,11},{10,... | collective-permute-start | bytes 196616 | tf_op jit(solution)/shard_map/ppermute | solution.py:368
  42.2 12.1 %collective-permute-start.17 = (bf16[3,128,256]{2,1,0:T(8,128)(2,1)S(1)}, bf16[3,128,256]{2,1,0:T(8,128)(2,1)S(1)}, u32[]{:S(2)}, u32[]{:S(2)}) collective-permute-start(bf16[3,128,256]{2,1,0:T(8,128)(2,1)S(1)} %constant_dynamic-update-slice_fusion), channel_id=1, source_target_pairs={{0,8},{4,12},{8,0},{12,4},{16,24},{20,28},{24,16},{28,20},{1,9},{5... | collective-permute-start | bytes 589832 | tf_op jit(solution)/shard_map/ppermute | solution.py:365
  44.4 11.1 %collective-permute-start.18 = (bf16[3,128,256]{2,1,0:T(8,128)(2,1)S(1)}, bf16[3,128,256]{2,1,0:T(8,128)(2,1)S(1)}, u32[]{:S(2)}, u32[]{:S(2)}) collective-permute-start(bf16[3,128,256]{2,1,0:T(8,128)(2,1)S(1)} %constant_dynamic-update-slice_fusion), channel_id=1, source_target_pairs={{0,16},{4,20},{8,24},{12,28},{16,0},{20,4},{24,8},{28,12},{1,17},{... | collective-permute-start | bytes 589832 | tf_op jit(solution)/shard_map/ppermute | solution.py:365
  45.9 10.3 %collective-permute-start.19 = (bf16[3,128,256]{2,1,0:T(8,128)(2,1)S(1)}, bf16[3,128,256]{2,1,0:T(8,128)(2,1)S(1)}, u32[]{:S(2)}, u32[]{:S(2)}) collective-permute-start(bf16[3,128,256]{2,1,0:T(8,128)(2,1)S(1)} %constant_dynamic-update-slice_fusion), channel_id=1, source_target_pairs={{0,24},{4,28},{8,16},{12,20},{16,8},{20,12},{24,0},{28,4},{1,25},{... | collective-permute-start | bytes 589832 | tf_op jit(solution)/shard_map/ppermute | solution.py:365
  46.4 11.0 %collective-permute-start.20 = (bf16[3,128,256]{2,1,0:T(8,128)(2,1)S(1)}, bf16[3,128,256]{2,1,0:T(8,128)(2,1)S(1)}, u32[]{:S(2)}, u32[]{:S(2)}) collective-permute-start(bf16[3,128,256]{2,1,0:T(8,128)(2,1)S(1)} %constant_dynamic-update-slice_fusion), channel_id=1, source_target_pairs={{0,4},{4,0},{8,12},{12,8},{16,20},{20,16},{24,28},{28,24},{1,5},{5... | collective-permute-start | bytes 589832 | tf_op jit(solution)/shard_map/ppermute | solution.py:362
  56.2 5.9 %collective-permute-start.22 = (bf16[3,128,256]{2,1,0:T(8,128)(2,1)S(1)}, bf16[3,128,256]{2,1,0:T(8,128)(2,1)S(1)}, u32[]{:S(2)}, u32[]{:S(2)}) collective-permute-start(bf16[3,128,256]{2,1,0:T(8,128)(2,1)S(1)} %collective-permute-done.18), channel_id=1, source_target_pairs={{0,4},{4,0},{8,12},{12,8},{16,20},{20,16},{24,28},{28,24},{1,5},{5... | collective-permute-start | bytes 589832 | tf_op jit(solution)/shard_map/ppermute | solution.py:362
  57.4 5.9 %collective-permute-start.23 = (bf16[3,128,256]{2,1,0:T(8,128)(2,1)S(1)}, bf16[3,128,256]{2,1,0:T(8,128)(2,1)S(1)}, u32[]{:S(2)}, u32[]{:S(2)}) collective-permute-start(bf16[3,128,256]{2,1,0:T(8,128)(2,1)S(1)} %collective-permute-done.19), channel_id=1, source_target_pairs={{0,4},{4,0},{8,12},{12,8},{16,20},{20,16},{24,28},{28,24},{1,5},{5... | collective-permute-start | bytes 589832 | tf_op jit(solution)/shard_map/ppermute | solution.py:362
  59.1 10.2 %collective-permute-start.6 = (f32[64,1024]{1,0:T(8,128)S(1)}, f32[64,1024]{1,0:T(8,128)S(1)}, u32[]{:S(2)}, u32[]{:S(2)}) collective-permute-start(f32[64,1024]{1,0:T(8,128)S(1)} %get-tuple-element.43), channel_id=1, source_target_pairs={{0,24},{4,28},{8,16},{12,20},{16,8},{20,12},{24,0},{28,4},{1,25},{... | collective-permute-start | bytes 786440 | tf_op jit(solution)/shard_map/ppermute | solution.py:365
  61.6 12.8 %collective-permute-start.5 = (f32[64,1024]{1,0:T(8,128)S(1)}, f32[64,1024]{1,0:T(8,128)S(1)}, u32[]{:S(2)}, u32[]{:S(2)}) collective-permute-start(f32[64,1024]{1,0:T(8,128)S(1)} %get-tuple-element.44), channel_id=1, source_target_pairs={{0,16},{4,20},{8,24},{12,28},{16,0},{20,4},{24,8},{28,12},{1,17},{... | collective-permute-start | bytes 786440 | tf_op jit(solution)/shard_map/ppermute | solution.py:365
  62.1 12.4 %collective-permute-start.4 = (f32[64,1024]{1,0:T(8,128)S(1)}, f32[64,1024]{1,0:T(8,128)S(1)}, u32[]{:S(2)}, u32[]{:S(2)}) collective-permute-start(f32[64,1024]{1,0:T(8,128)S(1)} %get-tuple-element.42), channel_id=1, source_target_pairs={{0,8},{4,12},{8,0},{12,4},{16,24},{20,28},{24,16},{28,20},{1,9},{5... | collective-permute-start | bytes 786440 | tf_op jit(solution)/shard_map/ppermute | solution.py:365
  63.4 52.0 %collective-permute-start.24 = (bf16[8,16,2048]{2,1,0:T(8,128)(2,1)}, bf16[8,16,2048]{2,1,0:T(8,128)(2,1)S(1)}, u32[]{:S(2)}, u32[]{:S(2)}) collective-permute-start(bf16[8,16,2048]{2,1,0:T(8,128)(2,1)} %bitcast.10.codes.refs_10_), channel_id=1, source_target_pairs={{0,2},{1,3},{2,0},{3,1},{4,6},{5,7},{6,4},{7,5},{8,10},{9,11},{10,... | collective-permute-start | bytes 1572872 | tf_op jit(solution)/shard_map/ppermute | solution.py:368
  69.3 56.4 %collective-permute-start.25 = (bf16[8,16,2048]{2,1,0:T(8,128)(2,1)}, bf16[8,16,2048]{2,1,0:T(8,128)(2,1)}, u32[]{:S(2)}, u32[]{:S(2)}) collective-permute-start(bf16[8,16,2048]{2,1,0:T(8,128)(2,1)} %bitcast.10.codes.refs_10_), channel_id=1, source_target_pairs={{0,3},{1,0},{2,1},{3,2},{4,7},{5,4},{6,5},{7,6},{8,11},{9,8},{10,9... | collective-permute-start | bytes 1572872 | tf_op jit(solution)/shard_map/ppermute | solution.py:368
  74.6 24.5 %collective-permute-start.9 = (bf16[64,1024]{1,0:T(8,128)(2,1)S(1)}, bf16[64,1024]{1,0:T(8,128)(2,1)S(1)}, u32[]{:S(2)}, u32[]{:S(2)}) collective-permute-start(bf16[64,1024]{1,0:T(8,128)(2,1)S(1)} %fusion.11), channel_id=1, source_target_pairs={{0,3},{1,0},{2,1},{3,2},{4,7},{5,4},{6,5},{7,6},{8,11},{9,8},{10,9... | collective-permute-start | bytes 393224 | tf_op jit(solution)/shard_map/ppermute | solution.py:368
  76.7 35.0 %collective-permute-start.8 = (bf16[64,1024]{1,0:T(8,128)(2,1)S(1)}, bf16[64,1024]{1,0:T(8,128)(2,1)S(1)}, u32[]{:S(2)}, u32[]{:S(2)}) collective-permute-start(bf16[64,1024]{1,0:T(8,128)(2,1)S(1)} %fusion.11), channel_id=1, source_target_pairs={{0,2},{1,3},{2,0},{3,1},{4,6},{5,7},{6,4},{7,5},{8,10},{9,11},{10,... | collective-permute-start | bytes 393224 | tf_op jit(solution)/shard_map/ppermute | solution.py:368
  76.9 34.8 %collective-permute-start.7 = (bf16[64,1024]{1,0:T(8,128)(2,1)S(1)}, bf16[64,1024]{1,0:T(8,128)(2,1)S(1)}, u32[]{:S(2)}, u32[]{:S(2)}) collective-permute-start(bf16[64,1024]{1,0:T(8,128)(2,1)S(1)} %fusion.11), channel_id=1, source_target_pairs={{0,1},{1,2},{2,3},{3,0},{4,5},{5,6},{6,7},{7,4},{8,9},{9,10},{10,1... | collective-permute-start | bytes 393224 | tf_op jit(solution)/shard_map/ppermute | solution.py:368
  111.8 23.4 %collective-permute-start.10 = (bf16[4,64,1024]{2,1,0:T(8,128)(2,1)S(1)}, bf16[4,64,1024]{2,1,0:T(8,128)(2,1)S(1)}, u32[]{:S(2)}, u32[]{:S(2)}) collective-permute-start(bf16[4,64,1024]{2,1,0:T(8,128)(2,1)S(1)} %pad_maximum_fusion.1.refs_0_), channel_id=1, source_target_pairs={{0,8},{4,12},{8,0},{12,4},{16,24},{20,28},{24,16},{28,20},{1,9},{5... | collective-permute-start | bytes 1572872 | tf_op jit(solution)/shard_map/ppermute | solution.py:365
  113.4 24.6 %collective-permute-start.11 = (bf16[4,64,1024]{2,1,0:T(8,128)(2,1)S(1)}, bf16[4,64,1024]{2,1,0:T(8,128)(2,1)S(1)}, u32[]{:S(2)}, u32[]{:S(2)}) collective-permute-start(bf16[4,64,1024]{2,1,0:T(8,128)(2,1)S(1)} %pad_maximum_fusion.1.refs_0_), channel_id=1, source_target_pairs={{0,16},{4,20},{8,24},{12,28},{16,0},{20,4},{24,8},{28,12},{1,17},{... | collective-permute-start | bytes 1572872 | tf_op jit(solution)/shard_map/ppermute | solution.py:365
  114.9 23.1 %collective-permute-start.12 = (bf16[4,64,1024]{2,1,0:T(8,128)(2,1)S(1)}, bf16[4,64,1024]{2,1,0:T(8,128)(2,1)S(1)}, u32[]{:S(2)}, u32[]{:S(2)}) collective-permute-start(bf16[4,64,1024]{2,1,0:T(8,128)(2,1)S(1)} %pad_maximum_fusion.1.refs_0_), channel_id=1, source_target_pairs={{0,24},{4,28},{8,16},{12,20},{16,8},{20,12},{24,0},{28,4},{1,25},{... | collective-permute-start | bytes 1572872 | tf_op jit(solution)/shard_map/ppermute | solution.py:365
  135.1 16.6 %collective-permute-start.26 = (bf16[4,64,1024]{2,1,0:T(8,128)(2,1)S(1)}, bf16[4,64,1024]{2,1,0:T(8,128)(2,1)S(1)}, u32[]{:S(2)}, u32[]{:S(2)}) collective-permute-start(bf16[4,64,1024]{2,1,0:T(8,128)(2,1)S(1)} %pad_maximum_fusion.1.refs_0_), channel_id=1, source_target_pairs={{0,4},{4,0},{8,12},{12,8},{16,20},{20,16},{24,28},{28,24},{1,5},{5... | collective-permute-start | bytes 1572872 | tf_op jit(solution)/shard_map/ppermute | solution.py:362
  135.2 16.6 %collective-permute-start.27 = (bf16[4,64,1024]{2,1,0:T(8,128)(2,1)S(1)}, bf16[4,64,1024]{2,1,0:T(8,128)(2,1)S(1)}, u32[]{:S(2)}, u32[]{:S(2)}) collective-permute-start(bf16[4,64,1024]{2,1,0:T(8,128)(2,1)S(1)} %collective-permute-done.10.refs_1_), channel_id=1, source_target_pairs={{0,4},{4,0},{8,12},{12,8},{16,20},{20,16},{24,28},{28,24},{1,5},{5... | collective-permute-start | bytes 1572872 | tf_op jit(solution)/shard_map/ppermute | solution.py:362
  138.0 13.8 %collective-permute-start.28 = (bf16[4,64,1024]{2,1,0:T(8,128)(2,1)S(1)}, bf16[4,64,1024]{2,1,0:T(8,128)(2,1)}, u32[]{:S(2)}, u32[]{:S(2)}) collective-permute-start(bf16[4,64,1024]{2,1,0:T(8,128)(2,1)S(1)} %collective-permute-done.11.refs_2_), channel_id=1, source_target_pairs={{0,4},{4,0},{8,12},{12,8},{16,20},{20,16},{24,28},{28,24},{1,5},{5... | collective-permute-start | bytes 1572872 | tf_op jit(solution)/shard_map/ppermute | solution.py:362
  138.0 13.8 %collective-permute-start.29 = (bf16[4,64,1024]{2,1,0:T(8,128)(2,1)S(1)}, bf16[4,64,1024]{2,1,0:T(8,128)(2,1)}, u32[]{:S(2)}, u32[]{:S(2)}) collective-permute-start(bf16[4,64,1024]{2,1,0:T(8,128)(2,1)S(1)} %collective-permute-done.12.refs_3_), channel_id=1, source_target_pairs={{0,4},{4,0},{8,12},{12,8},{16,20},{20,16},{24,28},{28,24},{1,5},{5... | collective-permute-start | bytes 1572872 | tf_op jit(solution)/shard_map/ppermute | solution.py:362
  217.4 12.0 %collective-permute-start.34 = (f32[4,64,1024]{2,1,0:T(8,128)}, f32[4,64,1024]{2,1,0:T(8,128)S(1)}, u32[]{:S(2)}, u32[]{:S(2)}) collective-permute-start(f32[4,64,1024]{2,1,0:T(8,128)} %bitcast.206), channel_id=1, source_target_pairs={{0,4},{4,0},{8,12},{12,8},{16,20},{20,16},{24,28},{28,24},{1,5},{5... | collective-permute-start | bytes 3145736 | tf_op jit(solution)/shard_map/ppermute | solution.py:362
  219.5 5.7 %collective-permute-start.58 = (bf16[128,256]{1,0:T(8,128)(2,1)S(1)}, bf16[128,256]{1,0:T(8,128)(2,1)S(1)}, u32[]{:S(2)}, u32[]{:S(2)}) collective-permute-start(bf16[128,256]{1,0:T(8,128)(2,1)S(1)} %get-tuple-element.49), channel_id=1, source_target_pairs={{0,24},{4,28},{8,16},{12,20},{16,8},{20,12},{24,0},{28,4},{1,25},{... | collective-permute-start | bytes 196616 | tf_op jit(solution)/shard_map/ppermute | solution.py:365
  225.9 6.8 %collective-permute-start.59 = (f32[128,256]{1,0:T(8,128)S(1)}, f32[128,256]{1,0:T(8,128)}, u32[]{:S(2)}, u32[]{:S(2)}) collective-permute-start(f32[128,256]{1,0:T(8,128)S(1)} %get-tuple-element.33), channel_id=1, source_target_pairs={{0,8},{4,12},{8,0},{12,4},{16,24},{20,28},{24,16},{28,20},{1,9},{5... | collective-permute-start | bytes 393224 | tf_op jit(solution)/shard_map/ppermute | solution.py:365
  227.4 14.0 %collective-permute-start.60 = (f32[128,256]{1,0:T(8,128)S(1)}, f32[128,256]{1,0:T(8,128)}, u32[]{:S(2)}, u32[]{:S(2)}) collective-permute-start(f32[128,256]{1,0:T(8,128)S(1)} %get-tuple-element.33), channel_id=1, source_target_pairs={{0,16},{4,20},{8,24},{12,28},{16,0},{20,4},{24,8},{28,12},{1,17},{... | collective-permute-start | bytes 393224 | tf_op jit(solution)/shard_map/ppermute | solution.py:365
  227.9 20.3 %collective-permute-start.61 = (f32[128,256]{1,0:T(8,128)S(1)}, f32[128,256]{1,0:T(8,128)S(1)}, u32[]{:S(2)}, u32[]{:S(2)}) collective-permute-start(f32[128,256]{1,0:T(8,128)S(1)} %get-tuple-element.33), channel_id=1, source_target_pairs={{0,24},{4,28},{8,16},{12,20},{16,8},{20,12},{24,0},{28,4},{1,25},{... | collective-permute-start | bytes 393224 | tf_op jit(solution)/shard_map/ppermute | solution.py:365
  229.7 12.6 %collective-permute-start.37 = (f32[64,1024]{1,0:T(8,128)S(1)}, f32[64,1024]{1,0:T(8,128)S(1)}, u32[]{:S(2)}, u32[]{:S(2)}) collective-permute-start(f32[64,1024]{1,0:T(8,128)S(1)} %get-tuple-element.40), channel_id=1, source_target_pairs={{0,24},{4,28},{8,16},{12,20},{16,8},{20,12},{24,0},{28,4},{1,25},{... | collective-permute-start | bytes 786440 | tf_op jit(solution)/shard_map/ppermute | solution.py:365
  231.2 14.9 %collective-permute-start.36 = (f32[64,1024]{1,0:T(8,128)S(1)}, f32[64,1024]{1,0:T(8,128)S(1)}, u32[]{:S(2)}, u32[]{:S(2)}) collective-permute-start(f32[64,1024]{1,0:T(8,128)S(1)} %get-tuple-element.41), channel_id=1, source_target_pairs={{0,16},{4,20},{8,24},{12,28},{16,0},{20,4},{24,8},{28,12},{1,17},{... | collective-permute-start | bytes 786440 | tf_op jit(solution)/shard_map/ppermute | solution.py:365
  232.7 13.4 %collective-permute-start.35 = (f32[64,1024]{1,0:T(8,128)S(1)}, f32[64,1024]{1,0:T(8,128)S(1)}, u32[]{:S(2)}, u32[]{:S(2)}) collective-permute-start(f32[64,1024]{1,0:T(8,128)S(1)} %get-tuple-element.39), channel_id=1, source_target_pairs={{0,8},{4,12},{8,0},{12,4},{16,24},{20,28},{24,16},{28,20},{1,9},{5... | collective-permute-start | bytes 786440 | tf_op jit(solution)/shard_map/ppermute | solution.py:365
  241.4 8.4 %collective-permute-start.62 = (f32[128,256]{1,0:T(8,128)S(1)}, f32[128,256]{1,0:T(8,128)S(1)}, u32[]{:S(2)}, u32[]{:S(2)}) collective-permute-start(f32[128,256]{1,0:T(8,128)S(1)} %get-tuple-element.33), channel_id=1, source_target_pairs={{0,4},{4,0},{8,12},{12,8},{16,20},{20,16},{24,28},{28,24},{1,5},{5... | collective-permute-start | bytes 393224 | tf_op jit(solution)/shard_map/ppermute | solution.py:362
  242.3 20.1 %collective-permute-start.63 = (f32[128,256]{1,0:T(8,128)}, f32[128,256]{1,0:T(8,128)S(1)}, u32[]{:S(2)}, u32[]{:S(2)}) collective-permute-start(f32[128,256]{1,0:T(8,128)} %collective-permute-done.59), channel_id=1, source_target_pairs={{0,4},{4,0},{8,12},{12,8},{16,20},{20,16},{24,28},{28,24},{1,5},{5... | collective-permute-start | bytes 393224 | tf_op jit(solution)/shard_map/ppermute | solution.py:362
  246.2 6.0 %collective-permute-start.38 = (bf16[64,1024]{1,0:T(8,128)(2,1)S(1)}, bf16[64,1024]{1,0:T(8,128)(2,1)S(1)}, u32[]{:S(2)}, u32[]{:S(2)}) collective-permute-start(bf16[64,1024]{1,0:T(8,128)(2,1)S(1)} %fusion.7.refs_0_), channel_id=1, source_target_pairs={{0,8},{4,12},{8,0},{12,4},{16,24},{20,28},{24,16},{28,20},{1,9},{5... | collective-permute-start | bytes 393224 | tf_op jit(solution)/shard_map/ppermute | solution.py:365
  247.1 7.8 %collective-permute-start.39 = (bf16[64,1024]{1,0:T(8,128)(2,1)S(1)}, bf16[64,1024]{1,0:T(8,128)(2,1)S(1)}, u32[]{:S(2)}, u32[]{:S(2)}) collective-permute-start(bf16[64,1024]{1,0:T(8,128)(2,1)S(1)} %fusion.7.refs_0_), channel_id=1, source_target_pairs={{0,16},{4,20},{8,24},{12,28},{16,0},{20,4},{24,8},{28,12},{1,17},{... | collective-permute-start | bytes 393224 | tf_op jit(solution)/shard_map/ppermute | solution.py:365
  248.2 6.8 %collective-permute-start.40 = (bf16[64,1024]{1,0:T(8,128)(2,1)S(1)}, bf16[64,1024]{1,0:T(8,128)(2,1)S(1)}, u32[]{:S(2)}, u32[]{:S(2)}) collective-permute-start(bf16[64,1024]{1,0:T(8,128)(2,1)S(1)} %fusion.7.refs_0_), channel_id=1, source_target_pairs={{0,24},{4,28},{8,16},{12,20},{16,8},{20,12},{24,0},{28,4},{1,25},{... | collective-permute-start | bytes 393224 | tf_op jit(solution)/shard_map/ppermute | solution.py:365
  255.5 23.8 %collective-permute-start.64 = (f32[128,256]{1,0:T(8,128)}, f32[128,256]{1,0:T(8,128)}, u32[]{:S(2)}, u32[]{:S(2)}) collective-permute-start(f32[128,256]{1,0:T(8,128)} %collective-permute-done.60), channel_id=1, source_target_pairs={{0,4},{4,0},{8,12},{12,8},{16,20},{20,16},{24,28},{28,24},{1,5},{5... | collective-permute-start | bytes 393224 | tf_op jit(solution)/shard_map/ppermute | solution.py:362
  255.6 24.6 %collective-permute-start.65 = (f32[128,256]{1,0:T(8,128)S(1)}, f32[128,256]{1,0:T(8,128)}, u32[]{:S(2)}, u32[]{:S(2)}) collective-permute-start(f32[128,256]{1,0:T(8,128)S(1)} %collective-permute-done.61), channel_id=1, source_target_pairs={{0,4},{4,0},{8,12},{12,8},{16,20},{20,16},{24,28},{28,24},{1,5},{5... | collective-permute-start | bytes 393224 | tf_op jit(solution)/shard_map/ppermute | solution.py:362
  262.0 6.9 %collective-permute-start.47 = (bf16[128,512]{1,0:T(8,128)(2,1)S(1)}, bf16[128,512]{1,0:T(8,128)(2,1)S(1)}, u32[]{:S(2)}, u32[]{:S(2)}) collective-permute-start(bf16[128,512]{1,0:T(8,128)(2,1)S(1)} %get-tuple-element.46), channel_id=1, source_target_pairs={{0,3},{1,0},{2,1},{3,2},{4,7},{5,4},{6,5},{7,6},{8,11},{9,8},{10,9... | collective-permute-start | bytes 393224 | tf_op jit(solution)/shard_map/ppermute | solution.py:368
  262.0 12.6 %collective-permute-start.46 = (bf16[128,512]{1,0:T(8,128)(2,1)S(1)}, bf16[128,512]{1,0:T(8,128)(2,1)S(1)}, u32[]{:S(2)}, u32[]{:S(2)}) collective-permute-start(bf16[128,512]{1,0:T(8,128)(2,1)S(1)} %get-tuple-element.47), channel_id=1, source_target_pairs={{0,2},{1,3},{2,0},{3,1},{4,6},{5,7},{6,4},{7,5},{8,10},{9,11},{10,... | collective-permute-start | bytes 393224 | tf_op jit(solution)/shard_map/ppermute | solution.py:368
  262.5 12.2 %collective-permute-start.45 = (bf16[128,512]{1,0:T(8,128)(2,1)S(1)}, bf16[128,512]{1,0:T(8,128)(2,1)S(1)}, u32[]{:S(2)}, u32[]{:S(2)}) collective-permute-start(bf16[128,512]{1,0:T(8,128)(2,1)S(1)} %get-tuple-element.45), channel_id=1, source_target_pairs={{0,1},{1,2},{2,3},{3,0},{4,5},{5,6},{6,7},{7,4},{8,9},{9,10},{10,1... | collective-permute-start | bytes 393224 | tf_op jit(solution)/shard_map/ppermute | solution.py:368
  275.7 12.2 %collective-permute-start.48 = (f32[128,512]{1,0:T(8,128)S(1)}, f32[128,512]{1,0:T(8,128)S(1)}, u32[]{:S(2)}, u32[]{:S(2)}) collective-permute-start(f32[128,512]{1,0:T(8,128)S(1)} %bitcast_select_fusion.refs_0_), channel_id=1, source_target_pairs={{0,8},{4,12},{8,0},{12,4},{16,24},{20,28},{24,16},{28,20},{1,9},{5... | collective-permute-start | bytes 786440 | tf_op jit(solution)/shard_map/ppermute | solution.py:365
  276.9 13.2 %collective-permute-start.49 = (f32[128,512]{1,0:T(8,128)S(1)}, f32[128,512]{1,0:T(8,128)S(1)}, u32[]{:S(2)}, u32[]{:S(2)}) collective-permute-start(f32[128,512]{1,0:T(8,128)S(1)} %bitcast_select_fusion.refs_0_), channel_id=1, source_target_pairs={{0,16},{4,20},{8,24},{12,28},{16,0},{20,4},{24,8},{28,12},{1,17},{... | collective-permute-start | bytes 786440 | tf_op jit(solution)/shard_map/ppermute | solution.py:365
  277.7 12.4 %collective-permute-start.50 = (f32[128,512]{1,0:T(8,128)S(1)}, f32[128,512]{1,0:T(8,128)}, u32[]{:S(2)}, u32[]{:S(2)}) collective-permute-start(f32[128,512]{1,0:T(8,128)S(1)} %bitcast_select_fusion.refs_0_), channel_id=1, source_target_pairs={{0,24},{4,28},{8,16},{12,20},{16,8},{20,12},{24,0},{28,4},{1,25},{... | collective-permute-start | bytes 786440 | tf_op jit(solution)/shard_map/ppermute | solution.py:365
  (51 other events, 236.7 us)

commit v2 on v1

v2 whole, which is shorter than its diff:
```python
import functools

import jax
import jax.numpy as jnp
from jax import lax
from jax.experimental import pallas as pl
from jax.experimental.pallas import tpu as pltpu
from jax.sharding import PartitionSpec as P


score_scale = 0.0625
norm_eps = 1e-06
bf16 = jnp.bfloat16
f32 = jnp.float32


def whole(array):
    rank = len(array.shape)
    return pl.BlockSpec(array.shape, lambda *step: (0,) * rank)


def cost(flops, moved, exps=0):
    return pl.CostEstimate(flops=int(flops), bytes_accessed=int(moved), transcendentals=int(exps))


def arrange_body(count, order, *refs):
    pieces, out = refs[:-1], refs[-1]
    for c, piece in enumerate(pieces):
        for i in range(count):
            out[order[c * count + i]] = piece[i].astype(out.dtype)


def arrange(order, pieces, kind=None):
    count = pieces[0].shape[0]
    shape = (count * len(pieces),) + pieces[0].shape[1:]
    rank = len(shape)
    return pl.pallas_call(
        functools.partial(arrange_body, count),
        grid_spec=pltpu.PrefetchScalarGridSpec(
            num_scalar_prefetch=1,
            grid=(1,),
            in_specs=[whole(p) for p in pieces],
            out_specs=pl.BlockSpec(shape, lambda i, order: (0,) * rank),
        ),
        out_shape=jax.ShapeDtypeStruct(shape, kind or pieces[0].dtype),
        cost_estimate=cost(0, 8 * len(pieces) * pieces[0].size),
        name="arrange",
    )(order, *pieces)


def decode_body(*refs):
    parts, table, out, index = refs[:-3], refs[-3], refs[-2], refs[-1]
    count, width = index.shape
    index[...] = sum(codes[0].astype(f32) for codes in parts).astype(jnp.int32)
    for m in range(count):
        full = jnp.broadcast_to(index[m : m + 1, :], (8, width))
        low = full & 127
        high = full >= 128
        values = table[0, pl.ds(m * 8, 8), :].astype(f32)
        first, second = values[:, :128], values[:, 128:]
        pieces = []
        for c in range(width // 128):
            lanes = slice(c * 128, (c + 1) * 128)
            a = jnp.take_along_axis(first, low[:, lanes], axis=1, mode="promise_in_bounds")
            b = jnp.take_along_axis(second, low[:, lanes], axis=1, mode="promise_in_bounds")
            pieces.append(jnp.where(high[:, lanes], b, a))
        out[pl.ds(m * 8, 8), :] = jnp.concatenate(pieces, axis=1).astype(bf16)


def decode(parts, tables, layer):
    slices, count, width = parts[0].shape
    height = count * 8
    return pl.pallas_call(
        decode_body,
        grid=(slices,),
        in_specs=[
            pl.BlockSpec((1, count, width), lambda i: (i, 0, 0)) for _ in parts
        ]
        + [pl.BlockSpec((1, height, tables.shape[2]), lambda i: (i, layer, 0))],
        out_specs=pl.BlockSpec((height, width), lambda i: (i, 0)),
        scratch_shapes=[pltpu.VMEM((count, width), jnp.int32)],
        out_shape=jax.ShapeDtypeStruct((slices * height, width), bf16),
        cost_estimate=cost(4 * slices * height * width * 512, slices * height * width * 2),
        name="decode",
    )(*parts, tables)


def score_body(chunks, blocks, *refs):
    queries, tables = refs[:chunks], refs[chunks : chunks + blocks]
    target, scores, stats, held = refs[chunks + blocks :]
    step, tile = pl.program_id(0), tables[0].shape[1]
    height = queries[0].shape[1]
    rows = scores.shape[0]

    @pl.when(step == 0)
    def gather():
        for c in range(chunks):
            for b in range(blocks):
                held[b, pl.ds(c * height, height), :] = queries[c][b]

    total = jnp.dot(held[0], tables[0][...], preferred_element_type=f32)
    for b in range(1, blocks):
        total += jnp.dot(held[b], tables[b][...], preferred_element_type=f32)
    scores[:, pl.ds(pl.multiple_of(step * tile, tile), tile)] = total * score_scale

    @pl.when(step == pl.num_programs(0) - 1)
    def reduce():
        group = 128
        for r in range(rows // group):
            span = pl.ds(r * group, group)
            value = scores[span, :]
            largest = jnp.max(value, axis=1, keepdims=True)
            expsum = jnp.sum(jnp.exp(value - largest), axis=1, keepdims=True)
            column = lax.broadcasted_iota(jnp.int32, value.shape, 1)
            hit = jnp.sum(
                jnp.where(column == target[span, :], value, 0.0), axis=1, keepdims=True
            )
            lane = lax.broadcasted_iota(jnp.int32, (group, 128), 1)
            packed = jnp.where(lane == 0, largest, jnp.where(lane == 1, expsum, hit))
            stats[:, span] = packed.T[:8]


def scores_of(queries, tables, target):
    chunks, blocks = len(queries), len(tables)
    _, height, depth = queries[0].shape
    width = tables[0].shape[1]
    rows, tile = chunks * height, min(512, width)
    return pl.pallas_call(
        functools.partial(score_body, chunks, blocks),
        grid=(width // tile,),
        in_specs=[whole(q) for q in queries]
        + [pl.BlockSpec((depth, tile), lambda i: (0, i)) for _ in tables]
        + [whole(target)],
        out_specs=[
            pl.BlockSpec((rows, width), lambda i: (0, 0)),
            pl.BlockSpec((8, rows), lambda i: (0, 0)),
        ],
        out_shape=[
            jax.ShapeDtypeStruct((rows, width), f32),
            jax.ShapeDtypeStruct((8, rows), f32),
        ],
        scratch_shapes=[pltpu.VMEM((blocks, rows, depth), bf16)],
        cost_estimate=cost(
            2 * rows * blocks * depth * width, blocks * depth * width * 2, rows * width
        ),
        name="scores",
    )(*queries, *tables, target)


def shuffle(value, offset, chunk):
    count = value.shape[1] // chunk
    return jnp.concatenate(
        [value[:, (c ^ offset) * chunk : ((c ^ offset) + 1) * chunk] for c in range(count)], axis=1
    )


def grad_body(shards, *refs):
    stats = refs[:shards]
    scores, target, passages, grad, near, far, losses, largest, total = refs[shards:]
    step, tile = pl.program_id(0), scores.shape[1]
    rows = scores.shape[0]

    @pl.when(step == 0)
    def merge():
        values = [shuffle(s[...], c, rows // shards) for c, s in enumerate(stats)]
        most = functools.reduce(jnp.maximum, [v[0:1] for v in values])
        summed = sum(v[1:2] * jnp.exp(v[0:1] - most) for v in values)
        hits = sum(v[2:3] for v in values)
        losses[...] = jnp.broadcast_to(jnp.log(summed) + most - hits, losses.shape)
        largest[...] = jnp.broadcast_to(most, (128, rows)).T
        total[...] = jnp.broadcast_to(summed, (128, rows)).T
        near[...] = jnp.zeros_like(near)
        far[...] = jnp.zeros_like(far)

    group = 128
    for r in range(rows // group):
        span = pl.ds(r * group, group)
        shifted = scores[span, :] - jnp.tile(largest[span, :], (1, tile // 128))
        column = lax.broadcasted_iota(jnp.int32, (group, tile), 1) + step * tile
        hit = (column == target[span, :]).astype(f32)
        value = jnp.exp(shifted) / jnp.tile(total[span, :], (1, tile // 128)) - hit
        grad[span, :] = value.astype(bf16)
    term = score_scale * lax.dot_general(
        grad[...], passages[...], (((1,), (1,)), ((), ())), preferred_element_type=f32
    )
    near[...] += term[: rows // 2].reshape(near.shape)
    far[...] += term[rows // 2 :].reshape(far.shape)


def score_grads(scores, stats, target, passages):
    rows, width = scores.shape
    depth, tile = passages.shape[0], min(512, width)
    term = (len(stats) // 2, rows // len(stats), depth)
    return pl.pallas_call(
        functools.partial(grad_body, len(stats)),
        grid=(width // tile,),
        in_specs=[whole(s) for s in stats]
        + [
            pl.BlockSpec((rows, tile), lambda i: (0, i)),
            whole(target),
            pl.BlockSpec((depth, tile), lambda i: (0, i)),
        ],
        out_specs=[
            pl.BlockSpec((rows, tile), lambda i: (0, i)),
            pl.BlockSpec(term, lambda i: (0, 0, 0)),
            pl.BlockSpec(term, lambda i: (0, 0, 0)),
            pl.BlockSpec((8, rows), lambda i: (0, 0)),
        ],
        out_shape=[
            jax.ShapeDtypeStruct((rows, width), bf16),
            jax.ShapeDtypeStruct(term, f32),
            jax.ShapeDtypeStruct(term, f32),
            jax.ShapeDtypeStruct((8, rows), f32),
        ],
        scratch_shapes=[pltpu.VMEM((rows, 128), f32), pltpu.VMEM((rows, 128), f32)],
        cost_estimate=cost(2 * rows * width * depth, rows * width * 6, rows * width),
        name="score_grads",
    )(*stats, scores, target, passages)


def book_body(chunks, low_count, group, order, *refs):
    queries = refs[:chunks]
    score_grad, codes, out, low_codes, high_codes = refs[chunks:]
    count, width = codes.shape[1], codes.shape[2]
    high_count = 256 // low_count
    contract = (((0,), (0,)), ((), ()))
    rows = jnp.concatenate([q[0] for q in queries], axis=0)
    grads = lax.dot_general(rows, score_grad[...], contract, preferred_element_type=f32)
    grads = (grads * score_scale).astype(bf16)
    code = codes[0].astype(f32)
    high = jnp.floor(code * (1.0 / low_count))
    high_codes[...] = high
    low_codes[...] = code - high * low_count
    low_iota = lax.broadcasted_iota(jnp.int32, (low_count, 128), 0).astype(f32).astype(bf16)
    high_iota = lax.broadcasted_iota(jnp.int32, (high_count * 8, 128), 0) // 8
    high_iota = high_iota.astype(f32).astype(bf16)
    low_iota = jnp.tile(low_iota, (1, width // 128))
    high_iota = jnp.tile(high_iota, (1, width // 128))
    one, zero = jnp.ones((), bf16), jnp.zeros((), bf16)
    for g in range(count // group):
        hots, masked = [], []
        for m in range(g * group, (g + 1) * group):
            low = jnp.broadcast_to(low_codes[m : m + 1, :].astype(bf16), (low_count, width))
            top = jnp.broadcast_to(high_codes[m : m + 1, :].astype(bf16), (high_count * 8, width))
            grad = jnp.tile(grads[m * 8 : (m + 1) * 8, :], (high_count, 1))
            hots.append(jnp.where(low == low_iota, one, zero))
            masked.append(jnp.where(top == high_iota, grad, zero))
        product = lax.dot_general(
            jnp.concatenate(masked, axis=0),
            jnp.concatenate(hots, axis=0),
            (((1,), (1,)), ((), ())),
            preferred_element_type=f32,
        )
        for i in range(group):
            height = high_count * 8
            block = product[i * height : (i + 1) * height, i * low_count : (i + 1) * low_count]
            out[g * group + i] = jnp.concatenate(
                [block[b * 8 : (b + 1) * 8, :] for b in range(high_count)], axis=1
            )


def book_grads(order, queries, score_grad, codes):
    chunks = len(queries)
    height = queries[0].shape[1]
    count, width = codes.shape[1:]
    slices, span = order.shape[0], count * 8
    return pl.pallas_call(
        functools.partial(book_body, chunks, 64, 4),
        grid_spec=pltpu.PrefetchScalarGridSpec(
            num_scalar_prefetch=1,
            grid=(slices,),
            in_specs=[
                pl.BlockSpec((1, height, span), lambda i, order: (0, 0, order[i])) for _ in queries
            ]
            + [
                pl.BlockSpec(score_grad.shape, lambda i, order: (0, 0)),
                pl.BlockSpec((1, count, width), lambda i, order: (order[i], 0, 0)),
            ],
            out_specs=pl.BlockSpec((count, 8, 256), lambda i, order: (i, 0, 0)),
            scratch_shapes=[pltpu.VMEM((count, width), f32), pltpu.VMEM((count, width), f32)],
        ),
        out_shape=jax.ShapeDtypeStruct((slices * count, 8, 256), f32),
        cost_estimate=cost(8 * slices * span * width * 512, slices * span * width * 2),
        name="book_grads",
    )(order, *queries, score_grad, codes)


def back_body(chunks, owners, order, *refs):
    pieces, weight = refs[:chunks], refs[chunks]
    outs, rows, sorted_rows = refs[chunks + 1 : -2], refs[-2], refs[-1]
    height = pieces[0].shape[0]
    for c in range(chunks):
        rows[pl.ds(c * height, height), :] = pieces[c][...]
        sorted_rows[order[c]] = pieces[c][...]
    span = rows.shape[0] // owners
    result = lax.dot_general(
        sorted_rows[...].reshape(rows.shape),
        weight[...],
        (((1,), (1,)), ((), ())),
        preferred_element_type=f32,
    ).astype(bf16)
    for k in range(owners):
        outs[k][...] = result[k * span : (k + 1) * span]


def back_part(order, pieces, weight, owners):
    height, depth = pieces[0].shape
    rows, width = height * len(pieces), weight.shape[0]
    blocks = [jax.ShapeDtypeStruct((rows // owners, width), bf16)] * owners
    return pl.pallas_call(
        functools.partial(back_body, len(pieces), owners),
        grid_spec=pltpu.PrefetchScalarGridSpec(
            num_scalar_prefetch=1,
            grid=(1,),
            in_specs=[whole(p) for p in pieces] + [whole(weight)],
            out_specs=[whole(b) for b in blocks]
            + [pl.BlockSpec((rows, depth), lambda i, order: (0, 0))],
            scratch_shapes=[pltpu.VMEM((len(pieces), height, depth), bf16)],
        ),
        out_shape=blocks + [jax.ShapeDtypeStruct((rows, depth), bf16)],
        cost_estimate=cost(2 * rows * weight.size, rows * depth * 4),
        name="back_part",
    )(order, *pieces, weight)


def tail_body(chunks, order, *refs):
    pieces = refs[:chunks]
    hidden, gain, inverse, out = refs[chunks:]
    width = pieces[0].shape[1]
    dots = jnp.zeros((hidden.shape[0], 1), f32)
    for c in range(chunks):
        lanes = pl.ds(pl.multiple_of(order[c] * width, width), width)
        scaled = pieces[c][...] * gain[:, lanes]
        dots += jnp.sum(scaled * hidden[:, lanes].astype(f32), axis=1, keepdims=True)
    scale = inverse[...]
    mean = dots * (1.0 / (chunks * width))
    factor = scale * scale * scale * mean
    for c in range(chunks):
        lanes = pl.ds(pl.multiple_of(order[c] * width, width), width)
        scaled = pieces[c][...] * gain[:, lanes]
        out[:, lanes] = (scale * scaled - hidden[:, lanes].astype(f32) * factor).astype(bf16)


def hidden_tail(order, pieces, hidden, gain, inverse):
    rows, features = hidden.shape
    height = rows
    by_rows = lambda i, order: (i, 0)
    return pl.pallas_call(
        functools.partial(tail_body, len(pieces)),
        grid_spec=pltpu.PrefetchScalarGridSpec(
            num_scalar_prefetch=1,
            grid=(rows // height,),
            in_specs=[pl.BlockSpec((height, p.shape[1]), by_rows) for p in pieces]
            + [
                pl.BlockSpec((height, features), by_rows),
                whole(gain),
                pl.BlockSpec((height, 1), by_rows),
            ],
            out_specs=pl.BlockSpec((height, features), by_rows),
        ),
        out_shape=jax.ShapeDtypeStruct(hidden.shape, bf16),
        cost_estimate=cost(8 * hidden.size, hidden.size * 8),
        name="hidden_tail",
    )(order, *pieces, hidden, gain, inverse)


def run_device(hidden, norm_gain, proj_weight, pq_codes, codebook, positives):
    shards, owners = lax.axis_size("psg"), lax.axis_size("qry")
    shard, owner = lax.axis_index("psg"), lax.axis_index("qry")
    half = shards // 2
    place = (shard % 2) * half + shard // 2
    steps = jnp.arange(shards, dtype=jnp.int32)
    swapped = steps ^ place

    def core(x):
        return lax.ppermute(x, "psg", [(i, i ^ 1) for i in range(shards)])

    def chip(x, k):
        return lax.ppermute(x, "psg", [(i, i ^ (2 * k)) for i in range(shards)])

    def turn(x, k):
        return lax.ppermute(x, "qry", [(i, i ^ k) for i in range(owners)])

    def collect(x):
        near = [x] + [chip(x, k) for k in range(1, half)]
        return near, [core(piece) for piece in near]

    def after(value, *others):
        return lax.optimization_barrier((value,) + others)[0]

    own_rows, _ = hidden.shape
    row_span, columns = proj_weight.shape
    passage_count, sub_count = pq_codes.shape
    queries_all = own_rows * owners
    chunk = queries_all // shards
    per_owner = own_rows // chunk

    book_rows = sub_count // shards
    book_own = codebook.reshape(shards, book_rows * 8, codebook.shape[2])
    book_slice = lax.dynamic_slice_in_dim(book_own, place, 1, 0)
    book_slices = jnp.concatenate([turn(book_slice, k) for k in range(1, owners)], axis=1)
    near, far = collect(book_slices)
    books = arrange(swapped, near + far)

    floats = hidden.astype(f32)
    inverse = lax.rsqrt(jnp.mean(floats * floats, axis=1, keepdims=True) + norm_eps)
    first = shard * row_span
    part = lax.dynamic_slice_in_dim(hidden, first, row_span, 1).astype(f32)
    part_gain = lax.dynamic_slice_in_dim(norm_gain, first, row_span, 0)
    slice_own = (part * inverse * part_gain[None, :]).astype(bf16)
    slices = [slice_own] + [turn(slice_own, k) for k in range(1, owners)]
    codes_own = pq_codes.astype(bf16).T.reshape(shards, book_rows, passage_count)
    source = after(owner ^ (steps // per_owner), codes_own)
    goes_to = (source * per_owner + steps % per_owner) ^ place
    normed_rows = arrange(goes_to, [s.reshape(per_owner, chunk, row_span) for s in slices])
    normed_rows = normed_rows.reshape(queries_all, row_span)

    def term_of(rows):
        return jnp.dot(rows, proj_weight, preferred_element_type=f32).reshape(half, chunk, columns)

    def scatter_sum(near_term, far_term):
        arrived = core(far_term)
        summed = [near_term[k] + arrived[k] for k in range(half)]
        total = summed[0]
        for k in range(1, half):
            total = total + chip(summed[k], k)
        return total, summed

    far_part = term_of(normed_rows[half * chunk :])
    near_part = after(term_of(normed_rows[: half * chunk]))
    query_own, _ = scatter_sum(near_part, far_part)
    query_own = query_own.astype(bf16)
    first_passages = decode([codes_own], book_own, 0)

    turned = [turn(query_own, k) for k in range(1, owners)]
    query_blocks = jnp.stack([query_own] + turned)
    near_queries, far_queries = collect(query_blocks)

    def hop(x, pairs):
        return lax.ppermute(x, "qry", pairs)

    passages = [first_passages]
    codes = {}
    waiting = after(codes_own, query_blocks)
    for k in range(1, owners):
        if owners == 4 and k == 3:
            passed = after(codes[2][0], query_blocks)
            codes[k] = [hop(waiting, [(1, 2), (2, 1)]), hop(passed, [(1, 0), (2, 3)])]
        else:
            codes[k] = [turn(codes_own if k <= owners // 2 else waiting, k)]
        passages.append(decode(codes[k], books, k - 1))

    targets = positives.reshape(shards, chunk)[swapped].reshape(queries_all, 1)
    targets = targets - shard * passage_count
    query_chunks = near_queries + far_queries
    scores, stats = scores_of(query_chunks, passages, targets)
    near_stats, far_stats = collect(stats)
    score_grad, near_term, far_term, losses_all = score_grads(
        scores, near_stats + far_stats, targets, passages[0]
    )
    query_grad, grad_sums = scatter_sum(near_term, far_term)
    near_pieces, far_pieces = collect(query_grad.astype(bf16))

    def book_terms(order):
        grads = after(score_grad, grad_sums[-1])
        if book_rows % 16 == 0:
            return book_grads(order, query_chunks, grads, codes_own).reshape(
                order.shape[0], book_rows * 8, 256
            )
        group = min(sub_count, 16)
        grouped = codes_own.reshape(sub_count // group, group, passage_count)
        book = book_grads(steps[: sub_count // group], query_chunks, grads, grouped)
        return book.reshape(shards, book_rows * 8, 256)[order]

    far_book = core(book_terms(swapped[half:]))
    first_book = book_terms(swapped[1:half])

    dest = ((swapped // per_owner) ^ owner) * per_owner + swapped % per_owner
    *back, grad_rows = back_part(dest, near_pieces + far_pieces, proj_weight, owners)
    weight_grad = lax.dot_general(
        normed_rows, grad_rows, (((0,), (0,)), ((), ())), preferred_element_type=f32
    )
    second_book = book_terms(swapped[:1])
    book_sum = second_book[0] + far_book[0]
    for k in range(1, half):
        book_half = (first_book[k - 1] + far_book[k]).astype(bf16)
        book_sum = book_sum + chip(book_half, k).astype(f32)
    near_books, far_books = collect(book_sum[None].astype(bf16))
    codebook_grad = arrange(swapped, near_books + far_books, f32).reshape(codebook.shape)

    def rows_of(array, who):
        first = (who ^ (place // per_owner)) * own_rows
        return lax.dynamic_slice_in_dim(array, first, own_rows, 0)

    def straighten(array):
        bit = 1
        while bit < per_owner:
            shaped = array.reshape(per_owner // (2 * bit), 2, bit * chunk)
            turned = shaped[:, ::-1].reshape(array.shape)
            array = jnp.where((place // bit) % 2 == 1, turned, array)
            bit *= 2
        return array

    back_sum = back[0].astype(f32)
    for k in range(1, owners):
        back_sum = back_sum + turn(back[k], k).astype(f32)
    near_back, far_back = collect(back_sum)
    shard_of = (swapped % half) * 2 + swapped // half
    hidden_grad = hidden_tail(
        shard_of, near_back + far_back, hidden, norm_gain[None, :], inverse
    )
    losses = straighten(rows_of(losses_all[0], owner))
    return (losses, hidden_grad, weight_grad, codebook_grad)


def solution(mesh):
    in_specs = (P("qry", None), P(), P("psg", "qry"), P("psg", "qry"), P("qry", None, None), P())
    out_specs = (P("qry"), P("qry", None), P("psg", "qry"), P("qry", None, None))
    return jax.shard_map(
        run_device, mesh=mesh, in_specs=in_specs, out_specs=out_specs, check_vma=False
    )
```

time: 301 us -> 244 us (0.81)
  waiting for transfers between devices: 75.1 us -> 46.3 us
  local copies, waits for them, and re-layouts: 31.1 us -> 11.2 us
  Pallas kernels: 119 us -> 103 us
  other arithmetic: 7.5 us -> 13.5 us
    ppermute x15 -> x16, waiting for transfers between devices: 43.5 us -> 18.1 us  [the longest x14 18.1 us: turn(): return lax.ppermute(x, 'qry', [(i, i ^ k) for i in range(owners)])]
    pallas_call x12, Pallas kernels: 90.7 us -> 81.7 us  [the longest x4 35.3 us: decode(): pl.pallas_call(decode_body, grid=(slices,), in_specs=[pl.BlockSpec((1, co...]
    unnamed x83 -> x96, local copies, waits for them, and re-layouts: 12.8 us -> 4.76 us
    squeeze x22 -> x0, local copies, waits for them, and re-layouts: 6.8 us -> none  [the longest x1 0.84 us: per_device(): book_slice = lax.dynamic_index_in_dim(book_own, place, 0, keepdims=False)]
    pallas_call x2 -> x1, Pallas kernels: 23.5 us -> 17.3 us  [scores_of(): pl.pallas_call(functools.partial(score_body, chunks, blocks), grid=(width...]
    ppermute x27, waiting for transfers between devices: 30.6 us -> 25.9 us  [chip(): return lax.ppermute(x, 'psg', [(i, i ^ 2 * k) for i in range(shards)])]
    ppermute x15 -> x16, starting transfers between devices: 24.5 us -> 25.1 us  [the longest x14 22.4 us: turn(): return lax.ppermute(x, 'qry', [(i, i ^ k) for i in range(owners)])]
  transfers between devices with their start and end apart: 66 -> 70, of which waited for: 24 -> 21; matrix products, arithmetic and copies ran while one was open for 9% -> 7% of each run, Pallas kernels for 22% -> 30%
where the time goes in v2:
time: 244 us; the launch traced here: 242 us
  Pallas kernels  103 us (42%)
  starting transfers between devices  61.9 us (25%)
  waiting for transfers between devices  46.3 us (19%)
  other arithmetic  13.5 us (6%)
  local copies, waits for them, and re-layouts  11.2 us (5%)
  matrix products  3.95 us (2%)
    pallas_call x4, Pallas kernels, decode(): pl.pallas_call(decode_body, grid=(slices,), in_specs=[pl.BlockSpec((1, co...  35.3 us
    ppermute x27, starting transfers between devices, chip(): return lax.ppermute(x, 'psg', [(i, i ^ 2 * k) for i in range(shards)])  32.5 us
    ppermute x27, waiting for transfers between devices, chip(): return lax.ppermute(x, 'psg', [(i, i ^ 2 * k) for i in range(shards)])  25.9 us
    pallas_call x3, Pallas kernels, book_grads(): pl.pallas_call(functools.partial(book_body, chunks, 64, 4), grid_spec=plt...  25.7 us
    ppermute x14, starting transfers between devices, turn(): return lax.ppermute(x, 'qry', [(i, i ^ k) for i in range(owners)])  22.4 us
    ppermute x14, waiting for transfers between devices, turn(): return lax.ppermute(x, 'qry', [(i, i ^ k) for i in range(owners)])  18.1 us
    pallas_call x1, Pallas kernels, scores_of(): pl.pallas_call(functools.partial(score_body, chunks, blocks), grid=(width...  17.3 us
    pallas_call x3, Pallas kernels, arrange(): pl.pallas_call(functools.partial(arrange_body, count), grid_spec=pltpu.Pr...  8.72 us
  transfers between devices with their start and end apart: 70, of which 21 were waited for; matrix products, arithmetic and copies ran while one was open for 7% of the time, Pallas kernels for 30%

profile of v2, /device:TPU:0, one launch (start us, length us, event | category | flops | bytes accessed | tf_op | source)
XLA Modules:
  0.0 241.6 jit_solution(15010239229777445376)
XLA Ops:
  0.6 1.5 multiply_reduce_fusion
  4.0 3.1 %collective-permute-start = (bf16[128,512]{1,0:T(8,128)(2,1)S(1)}, bf16[128,512]{1,0:T(8,128)(2,1)S(1)}, u32[]{:S(2)}, u32[]{:S(2)}) collective-permute-start(bf16[128,512]{1,0:T(8,128)(2,1)S(1)} %multiply_convert_fusion), channel_id=1, source_target_pairs={{0,1},{1,0},{2,3},{3,2},{4,5},{5,4},{6,7},{7,6},{8,9},{9,8},{10,11... | collective-permute-start | bytes 393224 | tf_op jit(solution)/shard_map/ppermute | solution.py:382
  7.2 2.6 %collective-permute-start.1 = (bf16[128,512]{1,0:T(8,128)(2,1)S(1)}, bf16[128,512]{1,0:T(8,128)(2,1)S(1)}, u32[]{:S(2)}, u32[]{:S(2)}) collective-permute-start(bf16[128,512]{1,0:T(8,128)(2,1)S(1)} %multiply_convert_fusion), channel_id=1, source_target_pairs={{0,2},{1,3},{2,0},{3,1},{4,6},{5,7},{6,4},{7,5},{8,10},{9,11},{10,... | collective-permute-start | bytes 393224 | tf_op jit(solution)/shard_map/ppermute | solution.py:382
  12.2 7.8 %collective-permute-done.1 = bf16[128,512]{1,0:T(8,128)(2,1)S(1)} collective-permute-done((bf16[128,512]{1,0:T(8,128)(2,1)S(1)}, bf16[128,512]{1,0:T(8,128)(2,1)S(1)}, u32[]{:S(2)}, u32[]{:S(2)}) %collective-permute-start.1) | collective-permute-done | bytes 131104 | tf_op jit(solution)/shard_map/ppermute | solution.py:382
  20.8 2.6 %arrange.3 = bf16[8,64,512]{2,1,0:T(8,128)(2,1)} custom-call(s32[8]{0:T(128)} %fusion.34.order, bf16[2,64,512]{2,1,0:T(8,128)(2,1)} %bitcast.123, bf16[2,64,512]{2,1,0:T(8,128)(2,1)} %bitcast.125, bf16[2,64,512]{2,1,0:T(8,128)(2,1)} %bitcast.126, bf16[2,64,512]{2,1,0:T(8,128)(2,1)} %bitcast.127), custom_call_target="tpu_custom_call" | custom-call | bytes 2097152 | tf_op jit(solution)/shard_map/arrange/pallas_call | solution.py:37
  23.3 1.5 fusion
  25.8 2.0 collective-permute-start.18
  28.7 1.5 collective-permute-start.20
  31.9 1.6 collective-permute-start.4
  33.5 1.5 collective-permute-start.5
  36.1 1.5 collective-permute-start.28
  37.6 1.6 collective-permute-start.21
  39.2 2.0 collective-permute-done.4
  41.2 1.5 collective-permute-start.22
  42.7 4.5 %collective-permute-done.5 = f32[64,1024]{1,0:T(8,128)S(1)} collective-permute-done((f32[64,1024]{1,0:T(8,128)S(1)}, f32[64,1024]{1,0:T(8,128)S(1)}, u32[]{:S(2)}, u32[]{:S(2)}) %collective-permute-start.5) | collective-permute-done | bytes 262176 | tf_op jit(solution)/shard_map/ppermute | solution.py:379
  51.0 2.0 collective-permute-start.8
  53.1 2.4 %collective-permute-done.22.refs_2_ = bf16[1,384,256]{2,1,0:T(8,128)(2,1)} collective-permute-done((bf16[1,384,256]{2,1,0:T(8,128)(2,1)S(1)}, bf16[1,384,256]{2,1,0:T(8,128)(2,1)}, u32[]{:S(2)}, u32[]{:S(2)}) %collective-permute-start.22) | collective-permute-done | bytes 196640 | tf_op jit(solution)/shard_map/ppermute | solution.py:379
  55.5 2.4 collective-permute-start.9
  57.9 8.7 %decode.4.refs_8_.refs_10_ = bf16[1024,2048]{1,0:T(8,128)(2,1)} custom-call(bf16[8,16,2048]{2,1,0:T(8,128)(2,1)} %bitcast.116, bf16[8,128,256]{2,1,0:T(8,128)(2,1)} %bitcast.133), custom_call_target="tpu_custom_call" | custom-call | flops 4294967296 | bytes 4194304 | tf_op jit(solution)/shard_map/decode/pallas_call | solution.py:73
  67.7 2.0 collective-permute-done.8
  70.8 1.6 collective-permute-start.10
  72.5 1.4 collective-permute-start.11
  77.4 3.4 %arrange.4.refs_1_.refs_2_ = bf16[8,384,256]{2,1,0:T(8,128)(2,1)} custom-call(s32[8]{0:T(128)} %iota_xor_fusion.order, bf16[1,384,256]{2,1,0:T(8,128)(2,1)} %copy-done.13, bf16[1,384,256]{2,1,0:T(8,128)(2,1)} %copy-done.21, bf16[1,384,256]{2,1,0:T(8,128)(2,1)} %collective-permute-done.22.refs_2_, bf16[1,384,256]{2,1,0:T(8,128)(2,1)} %collective-permute-done.23.refs_3_, ...), custom_call_target="tpu_custom_call" | custom-call | bytes 6291456 | tf_op jit(solution)/shard_map/arrange/pallas_call | solution.py:37
  81.6 1.5 collective-permute-start.29
  83.1 8.7 %decode.6.refs_10_ = bf16[1024,2048]{1,0:T(8,128)(2,1)} custom-call(bf16[8,16,2048]{2,1,0:T(8,128)(2,1)} %copy-done.46, bf16[8,384,256]{2,1,0:T(8,128)(2,1)} %arrange.4.refs_1_.refs_2_), custom_call_target="tpu_custom_call" | custom-call | flops 4294967296 | bytes 4194304 | tf_op jit(solution)/shard_map/decode/pallas_call | solution.py:73
  92.4 4.8 %collective-permute-done.11.refs_2_ = bf16[4,64,1024]{2,1,0:T(8,128)(2,1)S(1)} collective-permute-done((bf16[4,64,1024]{2,1,0:T(8,128)(2,1)S(1)}, bf16[4,64,1024]{2,1,0:T(8,128)(2,1)S(1)}, u32[]{:S(2)}, u32[]{:S(2)}) %collective-permute-start.11) | collective-permute-done | bytes 524320 | tf_op jit(solution)/shard_map/ppermute | solution.py:379
  97.8 8.7 %decode.5.refs_9_ = bf16[1024,2048]{1,0:T(8,128)(2,1)} custom-call(bf16[8,16,2048]{2,1,0:T(8,128)(2,1)} %collective-permute-done.17.refs_0_, bf16[8,384,256]{2,1,0:T(8,128)(2,1)} %arrange.4.refs_1_.refs_2_), custom_call_target="tpu_custom_call" | custom-call | flops 4294967296 | bytes 4194304 | tf_op jit(solution)/shard_map/decode/pallas_call | solution.py:73
  106.5 9.1 %decode.7.refs_11_ = bf16[1024,2048]{1,0:T(8,128)(2,1)} custom-call(bf16[8,16,2048]{2,1,0:T(8,128)(2,1)} %collective-permute-done.29.refs_0_, bf16[8,16,2048]{2,1,0:T(8,128)(2,1)} %collective-permute-done.30.refs_1_, bf16[8,384,256]{2,1,0:T(8,128)(2,1)} %arrange.4.refs_1_.refs_2_), custom_call_target="tpu_custom_call" | custom-call | flops 4294967296 | bytes 4194304 | tf_op jit(solution)/shard_map/decode/pallas_call | solution.py:73
  115.7 17.3 %scores.1 = (f32[512,2048]{1,0:T(8,128)}, f32[8,512]{1,0:T(8,128)}) custom-call(bf16[4,64,1024]{2,1,0:T(8,128)(2,1)} %copy-done.4, bf16[4,64,1024]{2,1,0:T(8,128)(2,1)} %copy-done.10, bf16[4,64,1024]{2,1,0:T(8,128)(2,1)} %copy-done.11, bf16[4,64,1024]{2,1,0:T(8,128)(2,1)} %copy-done.12, bf16[4,64,1024]{2,1,0:T(8,128)(2,1)} %collective-permute-done.13.refs_4_, ...), custom_call_target="tpu_custom_call" | custom-call | flops 8589934592 | bytes 16777216 | tf_op jit(solution)/shard_map/scores/pallas_call | solution.py:128
  134.9 1.5 collective-permute-start.33
  137.7 2.1 collective-permute-done.33.refs_3_
  141.6 7.8 %score_grads.1 = (bf16[512,2048]{1,0:T(8,128)(2,1)}, f32[4,64,1024]{2,1,0:T(8,128)}, f32[4,64,1024]{2,1,0:T(8,128)}, f32[8,512]{1,0:T(8,128)}) custom-call(f32[8,512]{1,0:T(8,128)} %get-tuple-element.22.refs_0_, f32[8,512]{1,0:T(8,128)} %copy-done.37, f32[8,512]{1,0:T(8,128)} %copy-done.38, f32[8,512]{1,0:T(8,128)} %copy-done.39, f32[8,512]{1,0:T(8,128)} %copy-done.40, ...), custom_call_target="tpu_custom_call" | custom-call | flops 2147483648 | bytes 6291456 | tf_op jit(solution)/shard_map/score_grads/pallas_call | solution.py:194
  153.6 1.6 collective-permute-start.41
  157.2 11.4 %book_grads.4 = f32[64,8,256]{2,1,0:T(8,128)} custom-call(s32[4]{0:T(128)} %slice.112.order, bf16[4,64,1024]{2,1,0:T(8,128)(2,1)} %copy-done.4, bf16[4,64,1024]{2,1,0:T(8,128)(2,1)} %copy-done.10, bf16[4,64,1024]{2,1,0:T(8,128)(2,1)} %copy-done.11, bf16[4,64,1024]{2,1,0:T(8,128)(2,1)} %copy-done.12, bf16[4,64,1024]{2,1,0:T(8,128)(2,1)} %collective-permute-done.13.refs_4_, ...), custom_call_target="tpu_custom_call" | custom-call | flops 4294967296 | bytes 2097152 | tf_op jit(solution)/shard_map/book_grads/pallas_call | solution.py:267
  169.8 1.6 collective-permute-start.42
  173.4 9.3 %book_grads.5 = f32[48,8,256]{2,1,0:T(8,128)} custom-call(s32[3]{0:T(128)} %slice.114.order, bf16[4,64,1024]{2,1,0:T(8,128)(2,1)} %copy-done.4, bf16[4,64,1024]{2,1,0:T(8,128)(2,1)} %copy-done.10, bf16[4,64,1024]{2,1,0:T(8,128)(2,1)} %copy-done.11, bf16[4,64,1024]{2,1,0:T(8,128)(2,1)} %copy-done.12, bf16[4,64,1024]{2,1,0:T(8,128)(2,1)} %collective-permute-done.13.refs_4_, ...), custom_call_target="tpu_custom_call" | custom-call | flops 3221225472 | bytes 1572864 | tf_op jit(solution)/shard_map/book_grads/pallas_call | solution.py:267
  184.9 1.6 collective-permute-start.60
  188.5 5.0 %book_grads.3 = f32[16,8,256]{2,1,0:T(8,128)} custom-call(s32[1]{0:T(128)} %bitcast.134, bf16[4,64,1024]{2,1,0:T(8,128)(2,1)} %copy-done.4, bf16[4,64,1024]{2,1,0:T(8,128)(2,1)} %copy-done.10, bf16[4,64,1024]{2,1,0:T(8,128)(2,1)} %copy-done.11, bf16[4,64,1024]{2,1,0:T(8,128)(2,1)} %copy-done.12, bf16[4,64,1024]{2,1,0:T(8,128)(2,1)} %collective-permute-done.13.refs_4_, ...), custom_call_target="tpu_custom_call" | custom-call | flops 1073741824 | bytes 524288 | tf_op jit(solution)/shard_map/book_grads/pallas_call | solution.py:267
  194.8 4.1 %back_part.1 = (bf16[128,512]{1,0:T(8,128)(2,1)}, bf16[128,512]{1,0:T(8,128)(2,1)}, bf16[128,512]{1,0:T(8,128)(2,1)}, bf16[128,512]{1,0:T(8,128)(2,1)}, bf16[512,1024]{1,0:T(8,128)(2,1)}) custom-call(s32[8]{0:T(128)} %fusion.33.order, bf16[64,1024]{1,0:T(8,128)(2,1)} %copy-done.8, bf16[64,1024]{1,0:T(8,128)(2,1)} %copy-done.23, bf16[64,1024]{1,0:T(8,128)(2,1)} %copy-done.24, ...), custom_call_target="tpu_custom_call" | custom-call | flops 536870912 | bytes 2097152 | tf_op jit(solution)/shard_map/back_part/pallas_call | solution.py:310
  199.0 2.8 %collective-permute-start.49 = (bf16[128,512]{1,0:T(8,128)(2,1)}, bf16[128,512]{1,0:T(8,128)(2,1)S(1)}, u32[]{:S(2)}, u32[]{:S(2)}) collective-permute-start(bf16[128,512]{1,0:T(8,128)(2,1)} %get-tuple-element.28), channel_id=1, source_target_pairs={{0,1},{1,0},{2,3},{3,2},{4,5},{5,4},{6,7},{7,6},{8,9},{9,8},{10,11... | collective-permute-start | bytes 393224 | tf_op jit(solution)/shard_map/ppermute | solution.py:382
  204.5 1.6 collective-permute-start.63
  206.7 1.4 collective-permute-start.65
  208.1 6.3 %collective-permute-done.50 = bf16[128,512]{1,0:T(8,128)(2,1)S(1)} collective-permute-done((bf16[128,512]{1,0:T(8,128)(2,1)}, bf16[128,512]{1,0:T(8,128)(2,1)S(1)}, u32[]{:S(2)}, u32[]{:S(2)}) %collective-permute-start.50) | collective-permute-done | bytes 131104 | tf_op jit(solution)/shard_map/ppermute | solution.py:382
  215.3 1.6 collective-permute-start.52
  224.6 6.4 %collective-permute-done.53.refs_2_ = f32[128,512]{1,0:T(8,128)S(1)} collective-permute-done((f32[128,512]{1,0:T(8,128)S(1)}, f32[128,512]{1,0:T(8,128)S(1)}, u32[]{:S(2)}, u32[]{:S(2)}) %collective-permute-start.53) | collective-permute-done | bytes 262176 | tf_op jit(solution)/shard_map/ppermute | solution.py:379
  231.5 2.0 fusion.41
  233.5 2.8 %arrange.5 = f32[8,128,256]{2,1,0:T(8,128)} custom-call(s32[8]{0:T(128)} %iota_xor_fusion.order, bf16[1,128,256]{2,1,0:T(8,128)(2,1)} %copy-done.20, bf16[1,128,256]{2,1,0:T(8,128)(2,1)} %copy-done.33, bf16[1,128,256]{2,1,0:T(8,128)(2,1)} %copy-done.34, bf16[1,128,256]{2,1,0:T(8,128)(2,1)} %collective-permute-done.65.refs_3_, ...), custom_call_target="tpu_custom_call" | custom-call | bytes 2097152 | tf_op jit(solution)/shard_map/arrange/pallas_call | solution.py:37
  237.2 4.4 %hidden_tail.1 = bf16[128,4096]{1,0:T(8,128)(2,1)} custom-call(s32[8]{0:T(128)} %fusion.37.order, f32[128,512]{1,0:T(8,128)} %copy-done.6, f32[128,512]{1,0:T(8,128)} %copy-done.14, f32[128,512]{1,0:T(8,128)} %copy-done.15, f32[128,512]{1,0:T(8,128)} %copy-done.16, f32[128,512]{1,0:T(8,128)} %copy-done.17, f32[128,512]{1,0:T(8,128)} %copy-done.18, ...), custom_call_target="tpu_custom_call" | custom-call | flops 4194304 | bytes 4194304 | tf_op jit(solution)/shard_map/hidden_tail/pallas_call | solution.py:348
  (241 shorter events, 54.3 us)
Async XLA Ops:
  7.2 12.9 %collective-permute-start.1 = (bf16[128,512]{1,0:T(8,128)(2,1)S(1)}, bf16[128,512]{1,0:T(8,128)(2,1)S(1)}, u32[]{:S(2)}, u32[]{:S(2)}) collective-permute-start(bf16[128,512]{1,0:T(8,128)(2,1)S(1)} %multiply_convert_fusion), channel_id=1, source_target_pairs={{0,2},{1,3},{2,0},{3,1},{4,6},{5,7},{6,4},{7,5},{8,10},{9,11},{10,... | collective-permute-start | bytes 393224 | tf_op jit(solution)/shard_map/ppermute | solution.py:382
  9.7 10.3 %collective-permute-start.2 = (bf16[128,512]{1,0:T(8,128)(2,1)S(1)}, bf16[128,512]{1,0:T(8,128)(2,1)S(1)}, u32[]{:S(2)}, u32[]{:S(2)}) collective-permute-start(bf16[128,512]{1,0:T(8,128)(2,1)S(1)} %multiply_convert_fusion), channel_id=1, source_target_pairs={{0,3},{1,2},{2,1},{3,0},{4,7},{5,6},{6,5},{7,4},{8,11},{9,10},{10,... | collective-permute-start | bytes 393224 | tf_op jit(solution)/shard_map/ppermute | solution.py:382
  25.8 9.3 %collective-permute-start.18 = (bf16[1,128,256]{2,1,0:T(8,128)(2,1)S(1)}, bf16[1,128,256]{2,1,0:T(8,128)(2,1)S(1)}, u32[]{:S(2)}, u32[]{:S(2)}) collective-permute-start(bf16[1,128,256]{2,1,0:T(8,128)(2,1)S(1)} %constant_dynamic-slice_fusion.1), channel_id=1, source_target_pairs={{0,1},{1,0},{2,3},{3,2},{4,5},{5,4},{6,7},{7,6},{8,9},{9,8},{10,11... | collective-permute-start | bytes 196616 | tf_op jit(solution)/shard_map/ppermute | solution.py:382
  27.7 8.4 %collective-permute-start.19 = (bf16[1,128,256]{2,1,0:T(8,128)(2,1)S(1)}, bf16[1,128,256]{2,1,0:T(8,128)(2,1)S(1)}, u32[]{:S(2)}, u32[]{:S(2)}) collective-permute-start(bf16[1,128,256]{2,1,0:T(8,128)(2,1)S(1)} %constant_dynamic-slice_fusion.1), channel_id=1, source_target_pairs={{0,2},{1,3},{2,0},{3,1},{4,6},{5,7},{6,4},{7,5},{8,10},{9,11},{10,... | collective-permute-start | bytes 196616 | tf_op jit(solution)/shard_map/ppermute | solution.py:382
  28.7 8.9 %collective-permute-start.20 = (bf16[1,128,256]{2,1,0:T(8,128)(2,1)S(1)}, bf16[1,128,256]{2,1,0:T(8,128)(2,1)S(1)}, u32[]{:S(2)}, u32[]{:S(2)}) collective-permute-start(bf16[1,128,256]{2,1,0:T(8,128)(2,1)S(1)} %constant_dynamic-slice_fusion.1), channel_id=1, source_target_pairs={{0,3},{1,2},{2,1},{3,0},{4,7},{5,6},{6,5},{7,4},{8,11},{9,10},{10,... | collective-permute-start | bytes 196616 | tf_op jit(solution)/shard_map/ppermute | solution.py:382
  31.9 9.2 %collective-permute-start.4 = (f32[64,1024]{1,0:T(8,128)S(1)}, f32[64,1024]{1,0:T(8,128)S(1)}, u32[]{:S(2)}, u32[]{:S(2)}) collective-permute-start(f32[64,1024]{1,0:T(8,128)S(1)} %get-tuple-element.37), channel_id=1, source_target_pairs={{0,8},{4,12},{8,0},{12,4},{16,24},{20,28},{24,16},{28,20},{1,9},{5... | collective-permute-start | bytes 786440 | tf_op jit(solution)/shard_map/ppermute | solution.py:379
  33.5 13.7 %collective-permute-start.5 = (f32[64,1024]{1,0:T(8,128)S(1)}, f32[64,1024]{1,0:T(8,128)S(1)}, u32[]{:S(2)}, u32[]{:S(2)}) collective-permute-start(f32[64,1024]{1,0:T(8,128)S(1)} %get-tuple-element.39), channel_id=1, source_target_pairs={{0,16},{4,20},{8,24},{12,28},{16,0},{20,4},{24,8},{28,12},{1,17},{... | collective-permute-start | bytes 786440 | tf_op jit(solution)/shard_map/ppermute | solution.py:379
  35.0 13.0 %collective-permute-start.6 = (f32[64,1024]{1,0:T(8,128)S(1)}, f32[64,1024]{1,0:T(8,128)S(1)}, u32[]{:S(2)}, u32[]{:S(2)}) collective-permute-start(f32[64,1024]{1,0:T(8,128)S(1)} %get-tuple-element.38), channel_id=1, source_target_pairs={{0,24},{4,28},{8,16},{12,20},{16,8},{20,12},{24,0},{28,4},{1,25},{... | collective-permute-start | bytes 786440 | tf_op jit(solution)/shard_map/ppermute | solution.py:379
  36.1 30.7 %collective-permute-start.28 = (bf16[8,16,2048]{2,1,0:T(8,128)(2,1)S(1)}, bf16[8,16,2048]{2,1,0:T(8,128)(2,1)S(1)}, u32[]{:S(2)}, u32[]{:S(2)}) collective-permute-start(bf16[8,16,2048]{2,1,0:T(8,128)(2,1)S(1)} %bitcast.115), channel_id=1, source_target_pairs={{0,2},{1,3},{2,0},{3,1},{4,6},{5,7},{6,4},{7,5},{8,10},{9,11},{10,... | collective-permute-start | bytes 1572872 | tf_op jit(solution)/shard_map/ppermute | solution.py:382
  37.6 13.4 %collective-permute-start.21 = (bf16[1,384,256]{2,1,0:T(8,128)(2,1)S(1)}, bf16[1,384,256]{2,1,0:T(8,128)(2,1)S(1)}, u32[]{:S(2)}, u32[]{:S(2)}) collective-permute-start(bf16[1,384,256]{2,1,0:T(8,128)(2,1)S(1)} %constant_dynamic-update-slice_fusion.refs_0_), channel_id=1, source_target_pairs={{0,8},{4,12},{8,0},{12,4},{16,24},{20,28},{24,16},{28,20},{1,9},{5... | collective-permute-start | bytes 589832 | tf_op jit(solution)/shard_map/ppermute | solution.py:379
  41.2 14.3 %collective-permute-start.22 = (bf16[1,384,256]{2,1,0:T(8,128)(2,1)S(1)}, bf16[1,384,256]{2,1,0:T(8,128)(2,1)}, u32[]{:S(2)}, u32[]{:S(2)}) collective-permute-start(bf16[1,384,256]{2,1,0:T(8,128)(2,1)S(1)} %constant_dynamic-update-slice_fusion.refs_0_), channel_id=1, source_target_pairs={{0,16},{4,20},{8,24},{12,28},{16,0},{20,4},{24,8},{28,12},{1,17},{... | collective-permute-start | bytes 589832 | tf_op jit(solution)/shard_map/ppermute | solution.py:379
  47.2 19.5 %collective-permute-start.23 = (bf16[1,384,256]{2,1,0:T(8,128)(2,1)S(1)}, bf16[1,384,256]{2,1,0:T(8,128)(2,1)}, u32[]{:S(2)}, u32[]{:S(2)}) collective-permute-start(bf16[1,384,256]{2,1,0:T(8,128)(2,1)S(1)} %constant_dynamic-update-slice_fusion.refs_0_), channel_id=1, source_target_pairs={{0,24},{4,28},{8,16},{12,20},{16,8},{20,12},{24,0},{28,4},{1,25},{... | collective-permute-start | bytes 589832 | tf_op jit(solution)/shard_map/ppermute | solution.py:379
  49.1 18.5 %collective-permute-start.7 = (bf16[64,1024]{1,0:T(8,128)(2,1)S(1)}, bf16[64,1024]{1,0:T(8,128)(2,1)S(1)}, u32[]{:S(2)}, u32[]{:S(2)}) collective-permute-start(bf16[64,1024]{1,0:T(8,128)(2,1)S(1)} %fusion.19), channel_id=1, source_target_pairs={{0,1},{1,0},{2,3},{3,2},{4,5},{5,4},{6,7},{7,6},{8,9},{9,8},{10,11... | collective-permute-start | bytes 393224 | tf_op jit(solution)/shard_map/ppermute | solution.py:382
  51.0 18.6 %collective-permute-start.8 = (bf16[64,1024]{1,0:T(8,128)(2,1)S(1)}, bf16[64,1024]{1,0:T(8,128)(2,1)S(1)}, u32[]{:S(2)}, u32[]{:S(2)}) collective-permute-start(bf16[64,1024]{1,0:T(8,128)(2,1)S(1)} %fusion.19), channel_id=1, source_target_pairs={{0,2},{1,3},{2,0},{3,1},{4,6},{5,7},{6,4},{7,5},{8,10},{9,11},{10,... | collective-permute-start | bytes 393224 | tf_op jit(solution)/shard_map/ppermute | solution.py:382
  55.5 14.2 %collective-permute-start.9 = (bf16[64,1024]{1,0:T(8,128)(2,1)S(1)}, bf16[64,1024]{1,0:T(8,128)(2,1)S(1)}, u32[]{:S(2)}, u32[]{:S(2)}) collective-permute-start(bf16[64,1024]{1,0:T(8,128)(2,1)S(1)} %fusion.19), channel_id=1, source_target_pairs={{0,3},{1,2},{2,1},{3,0},{4,7},{5,6},{6,5},{7,4},{8,11},{9,10},{10,... | collective-permute-start | bytes 393224 | tf_op jit(solution)/shard_map/ppermute | solution.py:382
  66.7 15.0 %collective-permute-start.17 = (bf16[8,16,2048]{2,1,0:T(8,128)(2,1)S(1)}, bf16[8,16,2048]{2,1,0:T(8,128)(2,1)}, u32[]{:S(2)}, u32[]{:S(2)}) collective-permute-start(bf16[8,16,2048]{2,1,0:T(8,128)(2,1)S(1)} %bitcast.120), channel_id=1, source_target_pairs={{0,1},{1,0},{2,3},{3,2},{4,5},{5,4},{6,7},{7,6},{8,9},{9,8},{10,11... | collective-permute-start | bytes 1572872 | tf_op jit(solution)/shard_map/ppermute | solution.py:382
  70.8 21.1 %collective-permute-start.10 = (bf16[4,64,1024]{2,1,0:T(8,128)(2,1)S(1)}, bf16[4,64,1024]{2,1,0:T(8,128)(2,1)S(1)}, u32[]{:S(2)}, u32[]{:S(2)}) collective-permute-start(bf16[4,64,1024]{2,1,0:T(8,128)(2,1)S(1)} %pad_maximum_fusion.refs_0_), channel_id=1, source_target_pairs={{0,8},{4,12},{8,0},{12,4},{16,24},{20,28},{24,16},{28,20},{1,9},{5... | collective-permute-start | bytes 1572872 | tf_op jit(solution)/shard_map/ppermute | solution.py:379
  72.5 24.8 %collective-permute-start.11 = (bf16[4,64,1024]{2,1,0:T(8,128)(2,1)S(1)}, bf16[4,64,1024]{2,1,0:T(8,128)(2,1)S(1)}, u32[]{:S(2)}, u32[]{:S(2)}) collective-permute-start(bf16[4,64,1024]{2,1,0:T(8,128)(2,1)S(1)} %pad_maximum_fusion.refs_0_), channel_id=1, source_target_pairs={{0,16},{4,20},{8,24},{12,28},{16,0},{20,4},{24,8},{28,12},{1,17},{... | collective-permute-start | bytes 1572872 | tf_op jit(solution)/shard_map/ppermute | solution.py:379
  73.9 23.4 %collective-permute-start.12 = (bf16[4,64,1024]{2,1,0:T(8,128)(2,1)S(1)}, bf16[4,64,1024]{2,1,0:T(8,128)(2,1)S(1)}, u32[]{:S(2)}, u32[]{:S(2)}) collective-permute-start(bf16[4,64,1024]{2,1,0:T(8,128)(2,1)S(1)} %pad_maximum_fusion.refs_0_), channel_id=1, source_target_pairs={{0,24},{4,28},{8,16},{12,20},{16,8},{20,12},{24,0},{28,4},{1,25},{... | collective-permute-start | bytes 1572872 | tf_op jit(solution)/shard_map/ppermute | solution.py:379
  74.6 17.3 %collective-permute-start.30 = (bf16[8,16,2048]{2,1,0:T(8,128)(2,1)}, bf16[8,16,2048]{2,1,0:T(8,128)(2,1)}, u32[]{:S(2)}, u32[]{:S(2)}) collective-permute-start(bf16[8,16,2048]{2,1,0:T(8,128)(2,1)} %copy-done.46), channel_id=1, source_target_pairs={{1,0},{2,3},{5,4},{6,7},{9,8},{10,11},{13,12},{14,15},{17,16},{18,... | collective-permute-start | bytes 1572872 | tf_op jit(solution)/shard_map/ppermute | solution.py:440
  81.6 24.9 %collective-permute-start.29 = (bf16[8,16,2048]{2,1,0:T(8,128)(2,1)S(1)}, bf16[8,16,2048]{2,1,0:T(8,128)(2,1)}, u32[]{:S(2)}, u32[]{:S(2)}) collective-permute-start(bf16[8,16,2048]{2,1,0:T(8,128)(2,1)S(1)} %bitcast.121), channel_id=1, source_target_pairs={{1,2},{2,1},{5,6},{6,5},{9,10},{10,9},{13,14},{14,13},{17,18},{18,... | collective-permute-start | bytes 1572872 | tf_op jit(solution)/shard_map/ppermute | solution.py:440
  91.9 23.8 %collective-permute-start.13 = (bf16[4,64,1024]{2,1,0:T(8,128)(2,1)S(1)}, bf16[4,64,1024]{2,1,0:T(8,128)(2,1)}, u32[]{:S(2)}, u32[]{:S(2)}) collective-permute-start(bf16[4,64,1024]{2,1,0:T(8,128)(2,1)S(1)} %pad_maximum_fusion.refs_0_), channel_id=1, source_target_pairs={{0,4},{4,0},{8,12},{12,8},{16,20},{20,16},{24,28},{28,24},{1,5},{5... | collective-permute-start | bytes 1572872 | tf_op jit(solution)/shard_map/ppermute | solution.py:376
  92.0 23.7 %collective-permute-start.14 = (bf16[4,64,1024]{2,1,0:T(8,128)(2,1)S(1)}, bf16[4,64,1024]{2,1,0:T(8,128)(2,1)}, u32[]{:S(2)}, u32[]{:S(2)}) collective-permute-start(bf16[4,64,1024]{2,1,0:T(8,128)(2,1)S(1)} %collective-permute-done.10.refs_1_), channel_id=1, source_target_pairs={{0,4},{4,0},{8,12},{12,8},{16,20},{20,16},{24,28},{28,24},{1,5},{5... | collective-permute-start | bytes 1572872 | tf_op jit(solution)/shard_map/ppermute | solution.py:376
  97.3 18.4 %collective-permute-start.15 = (bf16[4,64,1024]{2,1,0:T(8,128)(2,1)S(1)}, bf16[4,64,1024]{2,1,0:T(8,128)(2,1)}, u32[]{:S(2)}, u32[]{:S(2)}) collective-permute-start(bf16[4,64,1024]{2,1,0:T(8,128)(2,1)S(1)} %collective-permute-done.11.refs_2_), channel_id=1, source_target_pairs={{0,4},{4,0},{8,12},{12,8},{16,20},{20,16},{24,28},{28,24},{1,5},{5... | collective-permute-start | bytes 1572872 | tf_op jit(solution)/shard_map/ppermute | solution.py:376
  97.3 18.4 %collective-permute-start.16 = (bf16[4,64,1024]{2,1,0:T(8,128)(2,1)S(1)}, bf16[4,64,1024]{2,1,0:T(8,128)(2,1)}, u32[]{:S(2)}, u32[]{:S(2)}) collective-permute-start(bf16[4,64,1024]{2,1,0:T(8,128)(2,1)S(1)} %collective-permute-done.12.refs_3_), channel_id=1, source_target_pairs={{0,4},{4,0},{8,12},{12,8},{16,20},{20,16},{24,28},{28,24},{1,5},{5... | collective-permute-start | bytes 1572872 | tf_op jit(solution)/shard_map/ppermute | solution.py:376
  153.6 15.1 %collective-permute-start.41 = (f32[64,1024]{1,0:T(8,128)S(1)}, f32[64,1024]{1,0:T(8,128)S(1)}, u32[]{:S(2)}, u32[]{:S(2)}) collective-permute-start(f32[64,1024]{1,0:T(8,128)S(1)} %get-tuple-element.35), channel_id=1, source_target_pairs={{0,24},{4,28},{8,16},{12,20},{16,8},{20,12},{24,0},{28,4},{1,25},{... | collective-permute-start | bytes 786440 | tf_op jit(solution)/shard_map/ppermute | solution.py:379
  155.2 13.4 %collective-permute-start.39 = (f32[64,1024]{1,0:T(8,128)S(1)}, f32[64,1024]{1,0:T(8,128)S(1)}, u32[]{:S(2)}, u32[]{:S(2)}) collective-permute-start(f32[64,1024]{1,0:T(8,128)S(1)} %get-tuple-element.34), channel_id=1, source_target_pairs={{0,8},{4,12},{8,0},{12,4},{16,24},{20,28},{24,16},{28,20},{1,9},{5... | collective-permute-start | bytes 786440 | tf_op jit(solution)/shard_map/ppermute | solution.py:379
  155.9 12.7 %collective-permute-start.40 = (f32[64,1024]{1,0:T(8,128)S(1)}, f32[64,1024]{1,0:T(8,128)}, u32[]{:S(2)}, u32[]{:S(2)}) collective-permute-start(f32[64,1024]{1,0:T(8,128)S(1)} %get-tuple-element.36), channel_id=1, source_target_pairs={{0,16},{4,20},{8,24},{12,28},{16,0},{20,4},{24,8},{28,12},{1,17},{... | collective-permute-start | bytes 786440 | tf_op jit(solution)/shard_map/ppermute | solution.py:379
  168.5 15.2 %collective-permute-start.59 = (f32[4,128,256]{2,1,0:T(8,128)}, f32[4,128,256]{2,1,0:T(8,128)S(1)}, u32[]{:S(2)}, u32[]{:S(2)}) collective-permute-start(f32[4,128,256]{2,1,0:T(8,128)} %bitcast.135), channel_id=1, source_target_pairs={{0,4},{4,0},{8,12},{12,8},{16,20},{20,16},{24,28},{28,24},{1,5},{5... | collective-permute-start | bytes 1572872 | tf_op jit(solution)/shard_map/ppermute | solution.py:376
  169.8 12.9 %collective-permute-start.42 = (bf16[64,1024]{1,0:T(8,128)(2,1)S(1)}, bf16[64,1024]{1,0:T(8,128)(2,1)S(1)}, u32[]{:S(2)}, u32[]{:S(2)}) collective-permute-start(bf16[64,1024]{1,0:T(8,128)(2,1)S(1)} %fusion.11.refs_0_), channel_id=1, source_target_pairs={{0,8},{4,12},{8,0},{12,4},{16,24},{20,28},{24,16},{28,20},{1,9},{5... | collective-permute-start | bytes 393224 | tf_op jit(solution)/shard_map/ppermute | solution.py:379
  171.4 11.9 %collective-permute-start.43 = (bf16[64,1024]{1,0:T(8,128)(2,1)S(1)}, bf16[64,1024]{1,0:T(8,128)(2,1)S(1)}, u32[]{:S(2)}, u32[]{:S(2)}) collective-permute-start(bf16[64,1024]{1,0:T(8,128)(2,1)S(1)} %fusion.11.refs_0_), channel_id=1, source_target_pairs={{0,16},{4,20},{8,24},{12,28},{16,0},{20,4},{24,8},{28,12},{1,17},{... | collective-permute-start | bytes 393224 | tf_op jit(solution)/shard_map/ppermute | solution.py:379
  172.0 11.4 %collective-permute-start.44 = (bf16[64,1024]{1,0:T(8,128)(2,1)S(1)}, bf16[64,1024]{1,0:T(8,128)(2,1)S(1)}, u32[]{:S(2)}, u32[]{:S(2)}) collective-permute-start(bf16[64,1024]{1,0:T(8,128)(2,1)S(1)} %fusion.11.refs_0_), channel_id=1, source_target_pairs={{0,24},{4,28},{8,16},{12,20},{16,8},{20,12},{24,0},{28,4},{1,25},{... | collective-permute-start | bytes 393224 | tf_op jit(solution)/shard_map/ppermute | solution.py:379
  183.3 10.3 %collective-permute-start.47 = (bf16[64,1024]{1,0:T(8,128)(2,1)S(1)}, bf16[64,1024]{1,0:T(8,128)(2,1)S(1)}, u32[]{:S(2)}, u32[]{:S(2)}) collective-permute-start(bf16[64,1024]{1,0:T(8,128)(2,1)S(1)} %collective-permute-done.43.refs_2_), channel_id=1, source_target_pairs={{0,4},{4,0},{8,12},{12,8},{16,20},{20,16},{24,28},{28,24},{1,5},{5... | collective-permute-start | bytes 393224 | tf_op jit(solution)/shard_map/ppermute | solution.py:376
  183.4 10.2 %collective-permute-start.48 = (bf16[64,1024]{1,0:T(8,128)(2,1)S(1)}, bf16[64,1024]{1,0:T(8,128)(2,1)S(1)}, u32[]{:S(2)}, u32[]{:S(2)}) collective-permute-start(bf16[64,1024]{1,0:T(8,128)(2,1)S(1)} %collective-permute-done.44.refs_3_), channel_id=1, source_target_pairs={{0,4},{4,0},{8,12},{12,8},{16,20},{20,16},{24,28},{28,24},{1,5},{5... | collective-permute-start | bytes 393224 | tf_op jit(solution)/shard_map/ppermute | solution.py:376
  184.9 18.2 %collective-permute-start.60 = (bf16[128,256]{1,0:T(8,128)(2,1)S(1)}, bf16[128,256]{1,0:T(8,128)(2,1)S(1)}, u32[]{:S(2)}, u32[]{:S(2)}) collective-permute-start(bf16[128,256]{1,0:T(8,128)(2,1)S(1)} %get-tuple-element.40), channel_id=1, source_target_pairs={{0,8},{4,12},{8,0},{12,4},{16,24},{20,28},{24,16},{28,20},{1,9},{5... | collective-permute-start | bytes 196616 | tf_op jit(solution)/shard_map/ppermute | solution.py:379
  186.4 18.0 %collective-permute-start.61 = (bf16[128,256]{1,0:T(8,128)(2,1)S(1)}, bf16[128,256]{1,0:T(8,128)(2,1)S(1)}, u32[]{:S(2)}, u32[]{:S(2)}) collective-permute-start(bf16[128,256]{1,0:T(8,128)(2,1)S(1)} %get-tuple-element.42), channel_id=1, source_target_pairs={{0,16},{4,20},{8,24},{12,28},{16,0},{20,4},{24,8},{28,12},{1,17},{... | collective-permute-start | bytes 196616 | tf_op jit(solution)/shard_map/ppermute | solution.py:379
  187.1 17.4 %collective-permute-start.62 = (bf16[128,256]{1,0:T(8,128)(2,1)S(1)}, bf16[128,256]{1,0:T(8,128)(2,1)S(1)}, u32[]{:S(2)}, u32[]{:S(2)}) collective-permute-start(bf16[128,256]{1,0:T(8,128)(2,1)S(1)} %get-tuple-element.41), channel_id=1, source_target_pairs={{0,24},{4,28},{8,16},{12,20},{16,8},{20,12},{24,0},{28,4},{1,25},{... | collective-permute-start | bytes 196616 | tf_op jit(solution)/shard_map/ppermute | solution.py:379
  201.8 12.6 %collective-permute-start.50 = (bf16[128,512]{1,0:T(8,128)(2,1)}, bf16[128,512]{1,0:T(8,128)(2,1)S(1)}, u32[]{:S(2)}, u32[]{:S(2)}) collective-permute-start(bf16[128,512]{1,0:T(8,128)(2,1)} %get-tuple-element.29), channel_id=1, source_target_pairs={{0,2},{1,3},{2,0},{3,1},{4,6},{5,7},{6,4},{7,5},{8,10},{9,11},{10,... | collective-permute-start | bytes 393224 | tf_op jit(solution)/shard_map/ppermute | solution.py:382
  203.1 11.3 %collective-permute-start.51 = (bf16[128,512]{1,0:T(8,128)(2,1)}, bf16[128,512]{1,0:T(8,128)(2,1)S(1)}, u32[]{:S(2)}, u32[]{:S(2)}) collective-permute-start(bf16[128,512]{1,0:T(8,128)(2,1)} %get-tuple-element.30), channel_id=1, source_target_pairs={{0,3},{1,2},{2,1},{3,0},{4,7},{5,6},{6,5},{7,4},{8,11},{9,10},{10,... | collective-permute-start | bytes 393224 | tf_op jit(solution)/shard_map/ppermute | solution.py:382
  204.5 12.4 %collective-permute-start.63 = (bf16[1,128,256]{2,1,0:T(8,128)(2,1)S(1)}, bf16[1,128,256]{2,1,0:T(8,128)(2,1)S(1)}, u32[]{:S(2)}, u32[]{:S(2)}) collective-permute-start(bf16[1,128,256]{2,1,0:T(8,128)(2,1)S(1)} %fusion.31.refs_0_), channel_id=1, source_target_pairs={{0,8},{4,12},{8,0},{12,4},{16,24},{20,28},{24,16},{28,20},{1,9},{5... | collective-permute-start | bytes 196616 | tf_op jit(solution)/shard_map/ppermute | solution.py:379
  206.1 11.5 %collective-permute-start.64 = (bf16[1,128,256]{2,1,0:T(8,128)(2,1)S(1)}, bf16[1,128,256]{2,1,0:T(8,128)(2,1)S(1)}, u32[]{:S(2)}, u32[]{:S(2)}) collective-permute-start(bf16[1,128,256]{2,1,0:T(8,128)(2,1)S(1)} %fusion.31.refs_0_), channel_id=1, source_target_pairs={{0,16},{4,20},{8,24},{12,28},{16,0},{20,4},{24,8},{28,12},{1,17},{... | collective-permute-start | bytes 196616 | tf_op jit(solution)/shard_map/ppermute | solution.py:379
  206.7 14.5 %collective-permute-start.65 = (bf16[1,128,256]{2,1,0:T(8,128)(2,1)S(1)}, bf16[1,128,256]{2,1,0:T(8,128)(2,1)}, u32[]{:S(2)}, u32[]{:S(2)}) collective-permute-start(bf16[1,128,256]{2,1,0:T(8,128)(2,1)S(1)} %fusion.31.refs_0_), channel_id=1, source_target_pairs={{0,24},{4,28},{8,16},{12,20},{16,8},{20,12},{24,0},{28,4},{1,25},{... | collective-permute-start | bytes 196616 | tf_op jit(solution)/shard_map/ppermute | solution.py:379
  215.3 9.2 %collective-permute-start.52 = (f32[128,512]{1,0:T(8,128)S(1)}, f32[128,512]{1,0:T(8,128)S(1)}, u32[]{:S(2)}, u32[]{:S(2)}) collective-permute-start(f32[128,512]{1,0:T(8,128)S(1)} %convert_add_fusion.refs_0_), channel_id=1, source_target_pairs={{0,8},{4,12},{8,0},{12,4},{16,24},{20,28},{24,16},{28,20},{1,9},{5... | collective-permute-start | bytes 786440 | tf_op jit(solution)/shard_map/ppermute | solution.py:379
  216.9 14.1 %collective-permute-start.53 = (f32[128,512]{1,0:T(8,128)S(1)}, f32[128,512]{1,0:T(8,128)S(1)}, u32[]{:S(2)}, u32[]{:S(2)}) collective-permute-start(f32[128,512]{1,0:T(8,128)S(1)} %convert_add_fusion.refs_0_), channel_id=1, source_target_pairs={{0,16},{4,20},{8,24},{12,28},{16,0},{20,4},{24,8},{28,12},{1,17},{... | collective-permute-start | bytes 786440 | tf_op jit(solution)/shard_map/ppermute | solution.py:379
  217.5 13.4 %collective-permute-start.54 = (f32[128,512]{1,0:T(8,128)S(1)}, f32[128,512]{1,0:T(8,128)S(1)}, u32[]{:S(2)}, u32[]{:S(2)}) collective-permute-start(f32[128,512]{1,0:T(8,128)S(1)} %convert_add_fusion.refs_0_), channel_id=1, source_target_pairs={{0,24},{4,28},{8,16},{12,20},{16,8},{20,12},{24,0},{28,4},{1,25},{... | collective-permute-start | bytes 786440 | tf_op jit(solution)/shard_map/ppermute | solution.py:379
  222.4 11.1 %collective-permute-start.69 = (bf16[1,128,256]{2,1,0:T(8,128)(2,1)}, bf16[1,128,256]{2,1,0:T(8,128)(2,1)}, u32[]{:S(2)}, u32[]{:S(2)}) collective-permute-start(bf16[1,128,256]{2,1,0:T(8,128)(2,1)} %collective-permute-done.65.refs_3_), channel_id=1, source_target_pairs={{0,4},{4,0},{8,12},{12,8},{16,20},{20,16},{24,28},{28,24},{1,5},{5... | collective-permute-start | bytes 196616 | tf_op jit(solution)/shard_map/ppermute | solution.py:376
  223.1 13.3 %collective-permute-start.55 = (f32[128,512]{1,0:T(8,128)S(1)}, f32[128,512]{1,0:T(8,128)S(1)}, u32[]{:S(2)}, u32[]{:S(2)}) collective-permute-start(f32[128,512]{1,0:T(8,128)S(1)} %convert_add_fusion.refs_0_), channel_id=1, source_target_pairs={{0,4},{4,0},{8,12},{12,8},{16,20},{20,16},{24,28},{28,24},{1,5},{5... | collective-permute-start | bytes 786440 | tf_op jit(solution)/shard_map/ppermute | solution.py:376
  224.6 11.8 %collective-permute-start.56 = (f32[128,512]{1,0:T(8,128)S(1)}, f32[128,512]{1,0:T(8,128)S(1)}, u32[]{:S(2)}, u32[]{:S(2)}) collective-permute-start(f32[128,512]{1,0:T(8,128)S(1)} %collective-permute-done.52.refs_1_), channel_id=1, source_target_pairs={{0,4},{4,0},{8,12},{12,8},{16,20},{20,16},{24,28},{28,24},{1,5},{5... | collective-permute-start | bytes 786440 | tf_op jit(solution)/shard_map/ppermute | solution.py:376
  (69 other events, 530.3 us)

commit v3 on v2

--- a/solution.py
+++ b/solution.py
@@ -21,6 +21,12 @@
 
 def cost(flops, moved, exps=0):
     return pl.CostEstimate(flops=int(flops), bytes_accessed=int(moved), transcendentals=int(exps))
+
+
+def tree(values, join=lambda a, b: a + b):
+    while len(values) > 1:
+        values = [join(values[i], values[i + 1]) for i in range(0, len(values), 2)]
+    return values[0]
 
 
 def arrange_body(count, order, *refs):
@@ -50,13 +56,13 @@
 
 def decode_body(*refs):
     parts, table, out, index = refs[:-3], refs[-3], refs[-2], refs[-1]
-    count, width = index.shape
-    index[...] = sum(codes[0].astype(f32) for codes in parts).astype(jnp.int32)
-    for m in range(count):
-        full = jnp.broadcast_to(index[m : m + 1, :], (8, width))
+    pair, count, width = index.shape
+    index[...] = sum(codes[...].astype(f32) for codes in parts).astype(jnp.int32)
+    for j, m in [(j, m) for j in range(pair) for m in range(count)]:
+        full = jnp.broadcast_to(index[j, m : m + 1, :], (8, width))
         low = full & 127
         high = full >= 128
-        values = table[0, pl.ds(m * 8, 8), :].astype(f32)
+        values = table[j, pl.ds(m * 8, 8), :].astype(f32)
         first, second = values[:, :128], values[:, 128:]
         pieces = []
         for c in range(width // 128):
@@ -64,7 +70,7 @@
             a = jnp.take_along_axis(first, low[:, lanes], axis=1, mode="promise_in_bounds")
             b = jnp.take_along_axis(second, low[:, lanes], axis=1, mode="promise_in_bounds")
             pieces.append(jnp.where(high[:, lanes], b, a))
-        out[pl.ds(m * 8, 8), :] = jnp.concatenate(pieces, axis=1).astype(bf16)
+        out[pl.ds((j * count + m) * 8, 8), :] = jnp.concatenate(pieces, axis=1).astype(bf16)
 
 
 def decode(parts, tables, layer):
@@ -72,79 +78,121 @@
     height = count * 8
     return pl.pallas_call(
         decode_body,
-        grid=(slices,),
-        in_specs=[
-            pl.BlockSpec((1, count, width), lambda i: (i, 0, 0)) for _ in parts
-        ]
-        + [pl.BlockSpec((1, height, tables.shape[2]), lambda i: (i, layer, 0))],
-        out_specs=pl.BlockSpec((height, width), lambda i: (i, 0)),
-        scratch_shapes=[pltpu.VMEM((count, width), jnp.int32)],
+        grid=(slices // 2,),
+        in_specs=[pl.BlockSpec((2, count, width), lambda i: (i, 0, 0)) for _ in parts]
+        + [pl.BlockSpec((2, height, tables.shape[2]), lambda i: (i, layer, 0))],
+        out_specs=pl.BlockSpec((2 * height, width), lambda i: (i, 0)),
+        scratch_shapes=[pltpu.VMEM((2, count, width), jnp.int32)],
         out_shape=jax.ShapeDtypeStruct((slices * height, width), bf16),
         cost_estimate=cost(4 * slices * height * width * 512, slices * height * width * 2),
         name="decode",
     )(*parts, tables)
 
 
+def column_of(row):
+    return jnp.broadcast_to(row, (128, row.shape[1])).T
+
+
 def score_body(chunks, blocks, *refs):
-    queries, tables = refs[:chunks], refs[chunks : chunks + blocks]
-    target, scores, stats, held = refs[chunks + blocks :]
-    step, tile = pl.program_id(0), tables[0].shape[1]
-    height = queries[0].shape[1]
+    own, others = refs[:chunks], refs[chunks : 2 * chunks]
+    tables = refs[2 * chunks : 2 * chunks + blocks]
+    target, scores, stats, own_rows, held, places, packed = refs[2 * chunks + blocks :]
+    step, last = pl.program_id(0), pl.num_programs(0) - 1
+    tile = tables[0].shape[1]
+    height = own[0].shape[0]
     rows = scores.shape[0]
+    group = 128
 
     @pl.when(step == 0)
     def gather():
         for c in range(chunks):
-            for b in range(blocks):
-                held[b, pl.ds(c * height, height), :] = queries[c][b]
-
-    total = jnp.dot(held[0], tables[0][...], preferred_element_type=f32)
-    for b in range(1, blocks):
-        total += jnp.dot(held[b], tables[b][...], preferred_element_type=f32)
-    scores[:, pl.ds(pl.multiple_of(step * tile, tile), tile)] = total * score_scale
-
-    @pl.when(step == pl.num_programs(0) - 1)
-    def reduce():
-        group = 128
+            own_rows[pl.ds(c * height, height), :] = own[c][...]
+            held[0, pl.ds(c * height, height), :] = own[c][...]
+            for b in range(1, blocks):
+                held[b, pl.ds(c * height, height), :] = others[c][b - 1]
+        places[...] = column_of(target[...])
+        packed[...] = jnp.zeros_like(packed)
+
+    def multiply():
+        total = jnp.dot(held[0], tables[0][...], preferred_element_type=f32)
+        for b in range(1, blocks):
+            total += jnp.dot(held[b], tables[b][...], preferred_element_type=f32)
+        scores[:, pl.ds(pl.multiple_of(step * tile, tile), tile)] = total * score_scale
+
+    def reduce(t):
+        column = lax.broadcasted_iota(jnp.int32, (group, tile), 1) + t * tile
+        column = column.astype(f32)
+        lane = lax.broadcasted_iota(jnp.int32, (group, 128), 1) - 3 * t
         for r in range(rows // group):
             span = pl.ds(r * group, group)
-            value = scores[span, :]
+            value = scores[span, pl.ds(pl.multiple_of(t * tile, tile), tile)]
             largest = jnp.max(value, axis=1, keepdims=True)
             expsum = jnp.sum(jnp.exp(value - largest), axis=1, keepdims=True)
-            column = lax.broadcasted_iota(jnp.int32, value.shape, 1)
-            hit = jnp.sum(
-                jnp.where(column == target[span, :], value, 0.0), axis=1, keepdims=True
+            found = column == jnp.tile(places[span, :], (1, tile // 128))
+            hit = jnp.sum(jnp.where(found, value, 0.0), axis=1, keepdims=True)
+            row = jnp.where(lane == 1, expsum, jnp.where(lane == 2, hit, packed[span, :]))
+            packed[span, :] = jnp.where(lane == 0, largest, row)
+
+    @pl.when(step == 0)
+    def begin():
+        multiply()
+
+    @pl.when((step > 0) & (step < last))
+    def both():
+        reduce(step - 1)
+        multiply()
+
+    @pl.when(step == last)
+    def finish():
+        reduce(last - 1)
+        tiles = scores.shape[1] // tile
+        for r in range(rows // group):
+            span = pl.ds(r * group, group)
+            turned = packed[span, :].T
+            most = functools.reduce(
+                jnp.maximum, [turned[3 * t : 3 * t + 1] for t in range(tiles)]
             )
-            lane = lax.broadcasted_iota(jnp.int32, (group, 128), 1)
-            packed = jnp.where(lane == 0, largest, jnp.where(lane == 1, expsum, hit))
-            stats[:, span] = packed.T[:8]
-
-
-def scores_of(queries, tables, target):
+            total = sum(
+                turned[3 * t + 1 : 3 * t + 2] * jnp.exp(turned[3 * t : 3 * t + 1] - most)
+                for t in range(tiles)
+            )
+            hits = sum(turned[3 * t + 2 : 3 * t + 3] for t in range(tiles))
+            stats[:, span] = jnp.concatenate(
+                [most, total, hits, jnp.zeros((5, group), f32)], axis=0
+            )
+
+
+def scores_of(own, queries, tables, target):
     chunks, blocks = len(queries), len(tables)
-    _, height, depth = queries[0].shape
+    height, depth = own[0].shape
     width = tables[0].shape[1]
     rows, tile = chunks * height, min(512, width)
     return pl.pallas_call(
         functools.partial(score_body, chunks, blocks),
-        grid=(width // tile,),
-        in_specs=[whole(q) for q in queries]
-        + [pl.BlockSpec((depth, tile), lambda i: (0, i)) for _ in tables]
+        grid=(width // tile + 1,),
+        in_specs=[whole(q) for q in own + queries]
+        + [pl.BlockSpec((depth, tile), lambda i: (0, jnp.minimum(i, width // tile - 1))) for _ in tables]
         + [whole(target)],
         out_specs=[
             pl.BlockSpec((rows, width), lambda i: (0, 0)),
             pl.BlockSpec((8, rows), lambda i: (0, 0)),
+            pl.BlockSpec((rows, depth), lambda i: (0, 0)),
         ],
         out_shape=[
             jax.ShapeDtypeStruct((rows, width), f32),
             jax.ShapeDtypeStruct((8, rows), f32),
+            jax.ShapeDtypeStruct((rows, depth), bf16),
         ],
-        scratch_shapes=[pltpu.VMEM((blocks, rows, depth), bf16)],
+        scratch_shapes=[
+            pltpu.VMEM((blocks, rows, depth), bf16),
+            pltpu.VMEM((rows, 128), f32),
+            pltpu.VMEM((rows, 128), f32),
+        ],
         cost_estimate=cost(
             2 * rows * blocks * depth * width, blocks * depth * width * 2, rows * width
         ),
         name="scores",
-    )(*queries, *tables, target)
+    )(*own, *queries, *tables, target)
 
 
 def shuffle(value, offset, chunk):
@@ -156,19 +204,21 @@
 
 def grad_body(shards, *refs):
     stats = refs[:shards]
-    scores, target, passages, grad, near, far, losses, largest, total = refs[shards:]
+    scores, target, passages, grad, near, far, losses = refs[shards:-3]
+    largest, total, places = refs[-3:]
     step, tile = pl.program_id(0), scores.shape[1]
     rows = scores.shape[0]
 
     @pl.when(step == 0)
     def merge():
         values = [shuffle(s[...], c, rows // shards) for c, s in enumerate(stats)]
-        most = functools.reduce(jnp.maximum, [v[0:1] for v in values])
-        summed = sum(v[1:2] * jnp.exp(v[0:1] - most) for v in values)
-        hits = sum(v[2:3] for v in values)
+        most = tree([v[0:1] for v in values], jnp.maximum)
+        summed = tree([v[1:2] * jnp.exp(v[0:1] - most) for v in values])
+        hits = tree([v[2:3] for v in values])
         losses[...] = jnp.broadcast_to(jnp.log(summed) + most - hits, losses.shape)
-        largest[...] = jnp.broadcast_to(most, (128, rows)).T
-        total[...] = jnp.broadcast_to(summed, (128, rows)).T
+        largest[...] = column_of(most)
+        total[...] = column_of(1.0 / summed)
+        places[...] = column_of(target[...])
         near[...] = jnp.zeros_like(near)
         far[...] = jnp.zeros_like(far)
 
@@ -176,9 +226,9 @@
     for r in range(rows // group):
         span = pl.ds(r * group, group)
         shifted = scores[span, :] - jnp.tile(largest[span, :], (1, tile // 128))
-        column = lax.broadcasted_iota(jnp.int32, (group, tile), 1) + step * tile
-        hit = (column == target[span, :]).astype(f32)
-        value = jnp.exp(shifted) / jnp.tile(total[span, :], (1, tile // 128)) - hit
+        column = (lax.broadcasted_iota(jnp.int32, (group, tile), 1) + step * tile).astype(f32)
+        hit = (column == jnp.tile(places[span, :], (1, tile // 128))).astype(f32)
+        value = jnp.exp(shifted) * jnp.tile(total[span, :], (1, tile // 128)) - hit
         grad[span, :] = value.astype(bf16)
     term = score_scale * lax.dot_general(
         grad[...], passages[...], (((1,), (1,)), ((), ())), preferred_element_type=f32
@@ -212,21 +262,15 @@
             jax.ShapeDtypeStruct(term, f32),
             jax.ShapeDtypeStruct((8, rows), f32),
         ],
-        scratch_shapes=[pltpu.VMEM((rows, 128), f32), pltpu.VMEM((rows, 128), f32)],
+        scratch_shapes=[pltpu.VMEM((rows, 128), f32)] * 3,
         cost_estimate=cost(2 * rows * width * depth, rows * width * 6, rows * width),
         name="score_grads",
     )(*stats, scores, target, passages)
 
 
-def book_body(chunks, low_count, group, order, *refs):
-    queries = refs[:chunks]
-    score_grad, codes, out, low_codes, high_codes = refs[chunks:]
+def book_body(low_count, group, order, grads, codes, out, low_codes, high_codes):
     count, width = codes.shape[1], codes.shape[2]
     high_count = 256 // low_count
-    contract = (((0,), (0,)), ((), ()))
-    rows = jnp.concatenate([q[0] for q in queries], axis=0)
-    grads = lax.dot_general(rows, score_grad[...], contract, preferred_element_type=f32)
-    grads = (grads * score_scale).astype(bf16)
     code = codes[0].astype(f32)
     high = jnp.floor(code * (1.0 / low_count))
     high_codes[...] = high
@@ -242,7 +286,7 @@
         for m in range(g * group, (g + 1) * group):
             low = jnp.broadcast_to(low_codes[m : m + 1, :].astype(bf16), (low_count, width))
             top = jnp.broadcast_to(high_codes[m : m + 1, :].astype(bf16), (high_count * 8, width))
-            grad = jnp.tile(grads[m * 8 : (m + 1) * 8, :], (high_count, 1))
+            grad = jnp.tile(grads[pl.ds(m * 8, 8), :], (high_count, 1))
             hots.append(jnp.where(low == low_iota, one, zero))
             masked.append(jnp.where(top == high_iota, grad, zero))
         product = lax.dot_general(
@@ -259,30 +303,25 @@
             )
 
 
-def book_grads(order, queries, score_grad, codes):
-    chunks = len(queries)
-    height = queries[0].shape[1]
+def book_grads(order, grads, codes):
     count, width = codes.shape[1:]
     slices, span = order.shape[0], count * 8
     return pl.pallas_call(
-        functools.partial(book_body, chunks, 64, 4),
+        functools.partial(book_body, 32, 4),
         grid_spec=pltpu.PrefetchScalarGridSpec(
             num_scalar_prefetch=1,
             grid=(slices,),
             in_specs=[
-                pl.BlockSpec((1, height, span), lambda i, order: (0, 0, order[i])) for _ in queries
-            ]
-            + [
-                pl.BlockSpec(score_grad.shape, lambda i, order: (0, 0)),
+                pl.BlockSpec((span, width), lambda i, order: (order[i], 0)),
                 pl.BlockSpec((1, count, width), lambda i, order: (order[i], 0, 0)),
             ],
             out_specs=pl.BlockSpec((count, 8, 256), lambda i, order: (i, 0, 0)),
             scratch_shapes=[pltpu.VMEM((count, width), f32), pltpu.VMEM((count, width), f32)],
         ),
         out_shape=jax.ShapeDtypeStruct((slices * count, 8, 256), f32),
-        cost_estimate=cost(8 * slices * span * width * 512, slices * span * width * 2),
+        cost_estimate=cost(4 * slices * span * width * 512, slices * span * width * 2),
         name="book_grads",
-    )(order, *queries, score_grad, codes)
+    )(order, grads, codes)
 
 
 def back_body(chunks, owners, order, *refs):
@@ -323,45 +362,49 @@
     )(order, *pieces, weight)
 
 
-def tail_body(chunks, order, *refs):
-    pieces = refs[:chunks]
-    hidden, gain, inverse, out = refs[chunks:]
+def tail_body(chunks, order, places, *refs):
+    pieces, books = refs[:chunks], refs[chunks : 2 * chunks]
+    hidden, gain, out, book_out = refs[2 * chunks :]
+    for c in range(chunks):
+        book_out[places[c]] = books[c][...].astype(f32)
     width = pieces[0].shape[1]
-    dots = jnp.zeros((hidden.shape[0], 1), f32)
+    dots, squares = [], []
     for c in range(chunks):
         lanes = pl.ds(pl.multiple_of(order[c] * width, width), width)
-        scaled = pieces[c][...] * gain[:, lanes]
-        dots += jnp.sum(scaled * hidden[:, lanes].astype(f32), axis=1, keepdims=True)
-    scale = inverse[...]
-    mean = dots * (1.0 / (chunks * width))
-    factor = scale * scale * scale * mean
+        value = hidden[:, lanes].astype(f32)
+        scaled = pieces[c][...].astype(f32) * gain[:, lanes]
+        dots.append(jnp.sum(scaled * value, axis=1, keepdims=True))
+        squares.append(jnp.sum(value * value, axis=1, keepdims=True))
+    count = chunks * width
+    scale = lax.rsqrt(tree(squares) / count + norm_eps)
+    factor = scale * scale * scale * (tree(dots) / count)
     for c in range(chunks):
         lanes = pl.ds(pl.multiple_of(order[c] * width, width), width)
-        scaled = pieces[c][...] * gain[:, lanes]
+        scaled = pieces[c][...].astype(f32) * gain[:, lanes]
         out[:, lanes] = (scale * scaled - hidden[:, lanes].astype(f32) * factor).astype(bf16)
 
 
-def hidden_tail(order, pieces, hidden, gain, inverse):
-    rows, features = hidden.shape
-    height = rows
-    by_rows = lambda i, order: (i, 0)
-    return pl.pallas_call(
-        functools.partial(tail_body, len(pieces)),
+def tail(order, places, pieces, books, width, book_shape, hidden, gain):
+    shared = books is None
+    rows = hidden.shape[0]
+    book_rows, levels = book_shape
+    here = width // levels if shared else 0
+    book_spec = pl.BlockSpec((book_rows, levels), lambda i, order, places: (0, here))
+    piece_spec = pl.BlockSpec((rows, width), lambda i, order, places: (0, 0))
+    count = len(pieces)
+    out_books = jax.ShapeDtypeStruct((count, book_rows, levels), f32)
+    return pl.pallas_call(
+        functools.partial(tail_body, count),
         grid_spec=pltpu.PrefetchScalarGridSpec(
-            num_scalar_prefetch=1,
-            grid=(rows // height,),
-            in_specs=[pl.BlockSpec((height, p.shape[1]), by_rows) for p in pieces]
-            + [
-                pl.BlockSpec((height, features), by_rows),
-                whole(gain),
-                pl.BlockSpec((height, 1), by_rows),
-            ],
-            out_specs=pl.BlockSpec((height, features), by_rows),
+            num_scalar_prefetch=2,
+            grid=(1,),
+            in_specs=[piece_spec] * count + [book_spec] * count + [whole(hidden), whole(gain)],
+            out_specs=[whole(hidden), whole(out_books)],
         ),
-        out_shape=jax.ShapeDtypeStruct(hidden.shape, bf16),
+        out_shape=[jax.ShapeDtypeStruct(hidden.shape, bf16), out_books],
         cost_estimate=cost(8 * hidden.size, hidden.size * 8),
-        name="hidden_tail",
-    )(order, *pieces, hidden, gain, inverse)
+        name="tail",
+    )(order, places, *pieces, *(pieces if shared else books), hidden, gain)
 
 
 def run_device(hidden, norm_gain, proj_weight, pq_codes, codebook, positives):
@@ -410,7 +453,9 @@
     slice_own = (part * inverse * part_gain[None, :]).astype(bf16)
     slices = [slice_own] + [turn(slice_own, k) for k in range(1, owners)]
     codes_own = pq_codes.astype(bf16).T.reshape(shards, book_rows, passage_count)
-    source = after(owner ^ (steps // per_owner), codes_own)
+    targets = positives.reshape(shards, chunk)[swapped].reshape(1, queries_all)
+    targets = (targets - shard * passage_count).astype(f32)
+    source = after(owner ^ (steps // per_owner), codes_own, targets)
     goes_to = (source * per_owner + steps % per_owner) ^ place
     normed_rows = arrange(goes_to, [s.reshape(per_owner, chunk, row_span) for s in slices])
     normed_rows = normed_rows.reshape(queries_all, row_span)
@@ -432,9 +477,10 @@
     query_own = query_own.astype(bf16)
     first_passages = decode([codes_own], book_own, 0)
 
-    turned = [turn(query_own, k) for k in range(1, owners)]
-    query_blocks = jnp.stack([query_own] + turned)
+    query_blocks = jnp.stack([turn(query_own, k) for k in range(1, owners)])
+    near_own, far_own = collect(query_own)
     near_queries, far_queries = collect(query_blocks)
+    own_chunks = near_own + far_own
 
     def hop(x, pairs):
         return lax.ppermute(x, "qry", pairs)
@@ -450,10 +496,8 @@
             codes[k] = [turn(codes_own if k <= owners // 2 else waiting, k)]
         passages.append(decode(codes[k], books, k - 1))
 
-    targets = positives.reshape(shards, chunk)[swapped].reshape(queries_all, 1)
-    targets = targets - shard * passage_count
     query_chunks = near_queries + far_queries
-    scores, stats = scores_of(query_chunks, passages, targets)
+    scores, stats, own_rows_all = scores_of(own_chunks, query_chunks, passages, targets)
     near_stats, far_stats = collect(stats)
     score_grad, near_term, far_term, losses_all = score_grads(
         scores, near_stats + far_stats, targets, passages[0]
@@ -461,32 +505,40 @@
     query_grad, grad_sums = scatter_sum(near_term, far_term)
     near_pieces, far_pieces = collect(query_grad.astype(bf16))
 
-    def book_terms(order):
-        grads = after(score_grad, grad_sums[-1])
+    passage_grad = lax.dot_general(
+        own_rows_all,
+        after(score_grad, grad_sums[-1]),
+        (((0,), (0,)), ((), ())),
+        preferred_element_type=f32,
+    )
+    passage_grad = (passage_grad * score_scale).astype(bf16)
+
+    def book_of(order):
         if book_rows % 16 == 0:
-            return book_grads(order, query_chunks, grads, codes_own).reshape(
+            return book_grads(order, passage_grad, codes_own).reshape(
                 order.shape[0], book_rows * 8, 256
             )
         group = min(sub_count, 16)
         grouped = codes_own.reshape(sub_count // group, group, passage_count)
-        book = book_grads(steps[: sub_count // group], query_chunks, grads, grouped)
+        book = book_grads(steps[: sub_count // group], passage_grad, grouped)
         return book.reshape(shards, book_rows * 8, 256)[order]
 
-    far_book = core(book_terms(swapped[half:]))
-    first_book = book_terms(swapped[1:half])
+    part = half // 2
+    far_book = [core(book_of(swapped[half : half + part]))]
+    both = book_of(jnp.concatenate([swapped[half + part :], swapped[part:half]]))
+    far_book.append(core(both[:part]))
+    near_book = [book_of(swapped[:part]), both[part:]]
+    halves = [near_book[k // part][k % part] + far_book[k // part][k % part] for k in range(half)]
+    book_sum = halves[0]
+    for k in range(1, half):
+        book_sum = book_sum + chip(halves[k].astype(bf16), k).astype(f32)
+    book_sum = book_sum.astype(bf16)
 
     dest = ((swapped // per_owner) ^ owner) * per_owner + swapped % per_owner
     *back, grad_rows = back_part(dest, near_pieces + far_pieces, proj_weight, owners)
     weight_grad = lax.dot_general(
         normed_rows, grad_rows, (((0,), (0,)), ((), ())), preferred_element_type=f32
     )
-    second_book = book_terms(swapped[:1])
-    book_sum = second_book[0] + far_book[0]
-    for k in range(1, half):
-        book_half = (first_book[k - 1] + far_book[k]).astype(bf16)
-        book_sum = book_sum + chip(book_half, k).astype(f32)
-    near_books, far_books = collect(book_sum[None].astype(bf16))
-    codebook_grad = arrange(swapped, near_books + far_books, f32).reshape(codebook.shape)
 
     def rows_of(array, who):
         first = (who ^ (place // per_owner)) * own_rows
@@ -504,11 +556,27 @@
     back_sum = back[0].astype(f32)
     for k in range(1, owners):
         back_sum = back_sum + turn(back[k], k).astype(f32)
-    near_back, far_back = collect(back_sum)
+    back_sum = back_sum.astype(bf16)
+    book_shape = book_sum.shape
+    shared = book_shape[0] == own_rows and row_span % book_shape[1] == 0
+    books_last = None
+    if shared:
+        near_back, far_back = collect(jnp.concatenate([back_sum, book_sum], axis=1))
+    else:
+        near_back, far_back = collect(back_sum)
+        books_last = sum(collect(book_sum), [])
     shard_of = (swapped % half) * 2 + swapped // half
-    hidden_grad = hidden_tail(
-        shard_of, near_back + far_back, hidden, norm_gain[None, :], inverse
-    )
+    hidden_grad, codebook_grad = tail(
+        shard_of,
+        swapped,
+        near_back + far_back,
+        books_last,
+        row_span,
+        book_shape,
+        hidden,
+        norm_gain[None, :],
+    )
+    codebook_grad = codebook_grad.reshape(codebook.shape)
     losses = straighten(rows_of(losses_all[0], owner))
     return (losses, hidden_grad, weight_grad, codebook_grad)
 

time: 244 us -> 275 us (1.13)
  waiting for transfers between devices: 46.3 us -> 82.2 us
  Pallas kernels: 103 us -> 89.8 us
  matrix products: 3.95 us -> 12.4 us
    ppermute x14, waiting for transfers between devices: 18.1 us -> 42 us  [turn(): return lax.ppermute(x, 'qry', [(i, i ^ k) for i in range(owners)])]
    ppermute x27, waiting for transfers between devices: 25.9 us -> 38.1 us  [chip(): return lax.ppermute(x, 'psg', [(i, i ^ 2 * k) for i in range(shards)])]
    pallas_call x8, Pallas kernels: 65.5 us -> 55.9 us  [the longest x4 32.7 us: decode(): pl.pallas_call(decode_body, grid=(slices // 2,), in_specs=[pl.BlockSpec((...]
    dot_general x0 -> x1, matrix products: none -> 6.33 us  [run_device(): lax.dot_general(own_rows_all, after(score_grad, grad_sums[-1]), (((0,), (...]
    pallas_call x3 -> x2, Pallas kernels: 8.72 us -> 5.96 us  [arrange(): pl.pallas_call(functools.partial(arrange_body, count), grid_spec=pltpu.Pr...]
  transfers between devices with their start and end apart: 70 -> 71, of which waited for: 21 -> 17; matrix products, arithmetic and copies ran while one was open for 7% -> 9% of each run, Pallas kernels for 30% -> 21%
where the time goes in v3:
time: 275 us; the launch traced here: 274 us
  Pallas kernels  89.8 us (33%)
  waiting for transfers between devices  82.2 us (30%)
  starting transfers between devices  63.2 us (23%)
  other arithmetic  14.1 us (5%)
  matrix products  12.4 us (5%)
  local copies, waits for them, and re-layouts  10.7 us (4%)
    ppermute x14, waiting for transfers between devices, turn(): return lax.ppermute(x, 'qry', [(i, i ^ k) for i in range(owners)])  42 us
    ppermute x27, waiting for transfers between devices, chip(): return lax.ppermute(x, 'psg', [(i, i ^ 2 * k) for i in range(shards)])  38.1 us
    pallas_call x4, Pallas kernels, decode(): pl.pallas_call(decode_body, grid=(slices // 2,), in_specs=[pl.BlockSpec((...  32.7 us
    ppermute x27, starting transfers between devices, chip(): return lax.ppermute(x, 'psg', [(i, i ^ 2 * k) for i in range(shards)])  31.9 us
    ppermute x14, starting transfers between devices, turn(): return lax.ppermute(x, 'qry', [(i, i ^ k) for i in range(owners)])  24.3 us
    pallas_call x3, Pallas kernels, book_grads(): pl.pallas_call(functools.partial(book_body, 32, 4), grid_spec=pltpu.Prefe...  18.3 us
    pallas_call x1, Pallas kernels, scores_of(): pl.pallas_call(functools.partial(score_body, chunks, blocks), grid=(width...  16.5 us
    pallas_call x1, Pallas kernels, score_grads(): pl.pallas_call(functools.partial(grad_body, len(stats)), grid=(width // t...  7.29 us
  transfers between devices with their start and end apart: 71, of which 17 were waited for; matrix products, arithmetic and copies ran while one was open for 9% of the time, Pallas kernels for 21%

profile of v3, /device:TPU:0, one launch (start us, length us, event | category | flops | bytes accessed | tf_op | source)
XLA Modules:
  0.0 273.8 jit_solution(4177422792371940793)
XLA Ops:
  0.6 1.6 multiply_reduce_fusion
  4.0 3.1 %collective-permute-start = (bf16[128,512]{1,0:T(8,128)(2,1)S(1)}, bf16[128,512]{1,0:T(8,128)(2,1)S(1)}, u32[]{:S(2)}, u32[]{:S(2)}) collective-permute-start(bf16[128,512]{1,0:T(8,128)(2,1)S(1)} %multiply_convert_fusion.1), channel_id=1, source_target_pairs={{0,1},{1,0},{2,3},{3,2},{4,5},{5,4},{6,7},{7,6},{8,9},{9,8},{10,11... | collective-permute-start | bytes 393224 | tf_op jit(solution)/shard_map/ppermute | solution.py:425
  7.2 2.6 collective-permute-start.1
  13.8 6.2 %collective-permute-done.1 = bf16[128,512]{1,0:T(8,128)(2,1)S(1)} collective-permute-done((bf16[128,512]{1,0:T(8,128)(2,1)S(1)}, bf16[128,512]{1,0:T(8,128)(2,1)S(1)}, u32[]{:S(2)}, u32[]{:S(2)}) %collective-permute-start.1) | collective-permute-done | bytes 131104 | tf_op jit(solution)/shard_map/ppermute | solution.py:425
  20.8 2.6 arrange.2
  25.7 2.0 collective-permute-start.25
  30.4 5.7 %collective-permute-done.26 = bf16[1,128,256]{2,1,0:T(8,128)(2,1)S(1)} collective-permute-done((bf16[1,128,256]{2,1,0:T(8,128)(2,1)S(1)}, bf16[1,128,256]{2,1,0:T(8,128)(2,1)S(1)}, u32[]{:S(2)}, u32[]{:S(2)}) %collective-permute-start.26) | collective-permute-done | bytes 65568 | tf_op jit(solution)/shard_map/ppermute | solution.py:425
  36.1 1.6 collective-permute-start.28
  40.9 1.5 collective-permute-start.5
  43.8 1.5 collective-permute-start.29
  45.8 15.7 %collective-permute-done.29.refs_2_ = bf16[1,384,256]{2,1,0:T(8,128)(2,1)S(1)} collective-permute-done((bf16[1,384,256]{2,1,0:T(8,128)(2,1)S(1)}, bf16[1,384,256]{2,1,0:T(8,128)(2,1)S(1)}, u32[]{:S(2)}, u32[]{:S(2)}) %collective-permute-start.29) | collective-permute-done | bytes 196640 | tf_op jit(solution)/shard_map/ppermute | solution.py:422
  61.5 3.1 %collective-permute-start.35 = (bf16[8,16,2048]{2,1,0:T(8,128)(2,1)S(1)}, bf16[8,16,2048]{2,1,0:T(8,128)(2,1)}, u32[]{:S(2)}, u32[]{:S(2)}) collective-permute-start(bf16[8,16,2048]{2,1,0:T(8,128)(2,1)S(1)} %bitcast.110), channel_id=1, source_target_pairs={{0,2},{1,3},{2,0},{3,1},{4,6},{5,7},{6,4},{7,5},{8,10},{9,11},{10,... | collective-permute-start | bytes 1572872 | tf_op jit(solution)/shard_map/ppermute | solution.py:425
  66.9 1.9 collective-permute-start.14
  69.0 2.4 collective-permute-start.16
  71.4 8.1 %decode.4.refs_16_.refs_10_ = bf16[1024,2048]{1,0:T(8,128)(2,1)} custom-call(bf16[8,16,2048]{2,1,0:T(8,128)(2,1)} %bitcast.112, bf16[8,128,256]{2,1,0:T(8,128)(2,1)} %bitcast.128), custom_call_target="tpu_custom_call" | custom-call | flops 4294967296 | bytes 4194304 | tf_op jit(solution)/shard_map/decode/pallas_call | solution.py:79
  79.6 19.6 %collective-permute-done.14 = bf16[64,1024]{1,0:T(8,128)(2,1)S(1)} collective-permute-done((bf16[64,1024]{1,0:T(8,128)(2,1)S(1)}, bf16[64,1024]{1,0:T(8,128)(2,1)S(1)}, u32[]{:S(2)}, u32[]{:S(2)}) %collective-permute-start.14) | collective-permute-done | bytes 131104 | tf_op jit(solution)/shard_map/ppermute | solution.py:425
  99.2 1.5 collective-permute-start.7
  100.7 1.5 collective-permute-start.8
  103.3 3.4 %arrange.3.refs_1_.refs_2_ = bf16[8,384,256]{2,1,0:T(8,128)(2,1)} custom-call(s32[8]{0:T(128)} %iota_xor_fusion.order.places, bf16[1,384,256]{2,1,0:T(8,128)(2,1)} %copy-done.17, bf16[1,384,256]{2,1,0:T(8,128)(2,1)} %copy-done.18, bf16[1,384,256]{2,1,0:T(8,128)(2,1)} %copy-done.19, bf16[1,384,256]{2,1,0:T(8,128)(2,1)} %copy-done.20, ...), custom_call_target="tpu_custom_call" | custom-call | bytes 6291456 | tf_op jit(solution)/shard_map/arrange/pallas_call | solution.py:43
  109.7 8.2 %decode.6.refs_18_ = bf16[1024,2048]{1,0:T(8,128)(2,1)} custom-call(bf16[8,16,2048]{2,1,0:T(8,128)(2,1)} %collective-permute-done.35.refs_0_, bf16[8,384,256]{2,1,0:T(8,128)(2,1)} %arrange.3.refs_1_.refs_2_), custom_call_target="tpu_custom_call" | custom-call | flops 4294967296 | bytes 4194304 | tf_op jit(solution)/shard_map/decode/pallas_call | solution.py:79
  117.9 1.6 collective-permute-start.17
  119.4 1.5 collective-permute-start.18
  121.4 8.1 %decode.5.refs_17_ = bf16[1024,2048]{1,0:T(8,128)(2,1)} custom-call(bf16[8,16,2048]{2,1,0:T(8,128)(2,1)} %collective-permute-done.24.refs_0_, bf16[8,384,256]{2,1,0:T(8,128)(2,1)} %arrange.3.refs_1_.refs_2_), custom_call_target="tpu_custom_call" | custom-call | flops 4294967296 | bytes 4194304 | tf_op jit(solution)/shard_map/decode/pallas_call | solution.py:79
  129.9 9.1 %collective-permute-done.18.refs_10_ = bf16[3,64,1024]{2,1,0:T(8,128)(2,1)S(1)} collective-permute-done((bf16[3,64,1024]{2,1,0:T(8,128)(2,1)S(1)}, bf16[3,64,1024]{2,1,0:T(8,128)(2,1)S(1)}, u32[]{:S(2)}, u32[]{:S(2)}) %collective-permute-start.18) | collective-permute-done | bytes 393248 | tf_op jit(solution)/shard_map/ppermute | solution.py:422
  140.5 8.2 %decode.7.refs_19_ = bf16[1024,2048]{1,0:T(8,128)(2,1)} custom-call(bf16[8,16,2048]{2,1,0:T(8,128)(2,1)} %copy-done.45, bf16[8,16,2048]{2,1,0:T(8,128)(2,1)} %copy-done.44, bf16[8,384,256]{2,1,0:T(8,128)(2,1)} %arrange.3.refs_1_.refs_2_), custom_call_target="tpu_custom_call" | custom-call | flops 4294967296 | bytes 4194304 | tf_op jit(solution)/shard_map/decode/pallas_call | solution.py:79
  150.3 16.5 %scores.1 = (f32[512,2048]{1,0:T(8,128)}, f32[8,512]{1,0:T(8,128)}, bf16[512,1024]{1,0:T(8,128)(2,1)}) custom-call(bf16[64,1024]{1,0:T(8,128)(2,1)} %copy-done.32, bf16[64,1024]{1,0:T(8,128)(2,1)} %copy-done.51, bf16[64,1024]{1,0:T(8,128)(2,1)} %copy-done.52, bf16[64,1024]{1,0:T(8,128)(2,1)} %copy-done.53, bf16[64,1024]{1,0:T(8,128)(2,1)} %copy-done.54, ...), custom_call_target="tpu_custom_call" | custom-call | flops 8589934592 | bytes 16777216 | tf_op jit(solution)/shard_map/scores/pallas_call | solution.py:170
  171.8 1.9 collective-permute-done.40.refs_3_
  175.6 7.3 %score_grads.1 = (bf16[512,2048]{1,0:T(8,128)(2,1)}, f32[4,64,1024]{2,1,0:T(8,128)}, f32[4,64,1024]{2,1,0:T(8,128)}, f32[8,512]{1,0:T(8,128)}) custom-call(f32[8,512]{1,0:T(8,128)} %get-tuple-element.25.refs_0_, f32[8,512]{1,0:T(8,128)} %copy-done.37, f32[8,512]{1,0:T(8,128)} %copy-done.38, f32[8,512]{1,0:T(8,128)} %copy-done.39, f32[8,512]{1,0:T(8,128)} %copy-done.40, ...), custom_call_target="tpu_custom_call" | custom-call | flops 2147483648 | bytes 6291456 | tf_op jit(solution)/shard_map/score_grads/pallas_call | solution.py:244
  187.0 1.6 collective-permute-start.46
  189.1 1.5 collective-permute-start.48
  190.5 6.3 %multiply_convert_fusion.grads = bf16[1024,2048]{1,0:T(8,128)(2,1)} fusion(bf16[512,1024]{1,0:T(8,128)(2,1)} %get-tuple-element.34, bf16[512,2048]{1,0:T(8,128)(2,1)} %get-tuple-element.36), kind=kOutput, calls=%fused_computation.1 | convolution fusion | flops 2151677952 | bytes 7340032 | tf_op jit(solution)/shard_map/dot_general | solution.py:508
  196.9 5.1 %book_grads.4 = f32[32,8,256]{2,1,0:T(8,128)} custom-call(s32[2]{0:T(128)} %get-tuple-element.51.order, bf16[1024,2048]{1,0:T(8,128)(2,1)} %multiply_convert_fusion.grads, bf16[8,16,2048]{2,1,0:T(8,128)(2,1)} %bitcast.113), custom_call_target="tpu_custom_call" | custom-call | flops 1073741824 | bytes 1048576 | tf_op jit(solution)/shard_map/book_grads/pallas_call | solution.py:309
  202.0 7.9 %book_grads.5 = f32[64,8,256]{2,1,0:T(8,128)} custom-call(s32[4]{0:T(128)} %pad_add_fusion.order, bf16[1024,2048]{1,0:T(8,128)(2,1)} %multiply_convert_fusion.grads, bf16[8,16,2048]{2,1,0:T(8,128)(2,1)} %bitcast.114), custom_call_target="tpu_custom_call" | custom-call | flops 2147483648 | bytes 2097152 | tf_op jit(solution)/shard_map/book_grads/pallas_call | solution.py:309
  209.9 5.3 %book_grads.3 = f32[32,8,256]{2,1,0:T(8,128)} custom-call(s32[2]{0:T(128)} %get-tuple-element.49.order, bf16[1024,2048]{1,0:T(8,128)(2,1)} %multiply_convert_fusion.grads, bf16[8,16,2048]{2,1,0:T(8,128)(2,1)} %bitcast.115), custom_call_target="tpu_custom_call" | custom-call | flops 1073741824 | bytes 1048576 | tf_op jit(solution)/shard_map/book_grads/pallas_call | solution.py:309
  217.1 1.6 collective-permute-start.49
  219.2 1.5 collective-permute-start.51
  221.6 1.6 collective-permute-start.60
  223.4 3.3 %collective-permute-done.50.refs_2_ = bf16[64,1024]{1,0:T(8,128)(2,1)S(1)} collective-permute-done((bf16[64,1024]{1,0:T(8,128)(2,1)S(1)}, bf16[64,1024]{1,0:T(8,128)(2,1)S(1)}, u32[]{:S(2)}, u32[]{:S(2)}) %collective-permute-start.50) | collective-permute-done | bytes 131104 | tf_op jit(solution)/shard_map/ppermute | solution.py:422
  232.1 4.1 %back_part.1 = (bf16[128,512]{1,0:T(8,128)(2,1)}, bf16[128,512]{1,0:T(8,128)(2,1)}, bf16[128,512]{1,0:T(8,128)(2,1)}, bf16[128,512]{1,0:T(8,128)(2,1)}, bf16[512,1024]{1,0:T(8,128)(2,1)}) custom-call(s32[8]{0:T(128)} %fusion.32.order, bf16[64,1024]{1,0:T(8,128)(2,1)} %copy-done.14, bf16[64,1024]{1,0:T(8,128)(2,1)} %copy-done.25, ...), custom_call_target="tpu_custom_call" | custom-call | flops 536870912 | bytes 2097152 | tf_op jit(solution)/shard_map/back_part/pallas_call | solution.py:349
  236.3 3.6 %collective-permute-start.56 = (bf16[128,512]{1,0:T(8,128)(2,1)}, bf16[128,512]{1,0:T(8,128)(2,1)S(1)}, u32[]{:S(2)}, u32[]{:S(2)}) collective-permute-start(bf16[128,512]{1,0:T(8,128)(2,1)} %get-tuple-element.31), channel_id=1, source_target_pairs={{0,1},{1,0},{2,3},{3,2},{4,5},{5,4},{6,7},{7,6},{8,9},{9,8},{10,11... | collective-permute-start | bytes 393224 | tf_op jit(solution)/shard_map/ppermute | solution.py:425
  241.2 1.5 collective-permute-start.58
  242.8 2.8 %collective-permute-done.56 = bf16[128,512]{1,0:T(8,128)(2,1)S(1)} collective-permute-done((bf16[128,512]{1,0:T(8,128)(2,1)}, bf16[128,512]{1,0:T(8,128)(2,1)S(1)}, u32[]{:S(2)}, u32[]{:S(2)}) %collective-permute-start.56) | collective-permute-done | bytes 131104 | tf_op jit(solution)/shard_map/ppermute | solution.py:425
  245.5 7.4 %collective-permute-done.57 = bf16[128,512]{1,0:T(8,128)(2,1)S(1)} collective-permute-done((bf16[128,512]{1,0:T(8,128)(2,1)}, bf16[128,512]{1,0:T(8,128)(2,1)S(1)}, u32[]{:S(2)}, u32[]{:S(2)}) %collective-permute-start.57) | collective-permute-done | bytes 131104 | tf_op jit(solution)/shard_map/ppermute | solution.py:425
  253.9 1.5 collective-permute-start.64
  258.0 2.9 %collective-permute-done.64.refs_1_.refs_9_ = bf16[128,768]{1,0:T(8,128)(2,1)S(1)} collective-permute-done((bf16[128,768]{1,0:T(8,128)(2,1)S(1)}, bf16[128,768]{1,0:T(8,128)(2,1)S(1)}, u32[]{:S(2)}, u32[]{:S(2)}) %collective-permute-start.64) | collective-permute-done | bytes 196640 | tf_op jit(solution)/shard_map/ppermute | solution.py:422
  261.0 3.3 %collective-permute-done.65.refs_2_.refs_10_ = bf16[128,768]{1,0:T(8,128)(2,1)S(1)} collective-permute-done((bf16[128,768]{1,0:T(8,128)(2,1)S(1)}, bf16[128,768]{1,0:T(8,128)(2,1)S(1)}, u32[]{:S(2)}, u32[]{:S(2)}) %collective-permute-start.65) | collective-permute-done | bytes 196640 | tf_op jit(solution)/shard_map/ppermute | solution.py:422
  264.8 3.3 %fusion.40 = f32[512,1024]{1,0:T(8,128)} fusion(bf16[512,512]{1,0:T(8,128)(2,1)S(1)} %bitcast.109, bf16[512,1024]{1,0:T(8,128)(2,1)} %get-tuple-element.38), kind=kOutput, calls=%fused_computation.90 | convolution fusion | flops 536870912 | bytes 3670016 | tf_op jit(solution)/shard_map/dot_general | solution.py:539
  268.9 4.9 %tail.1 = (bf16[128,4096]{1,0:T(8,128)(2,1)}, f32[8,128,256]{2,1,0:T(8,128)}) custom-call(s32[8]{0:T(128)} %fusion.36.order, s32[8]{0:T(128)} %iota_xor_fusion.order.places, bf16[128,768]{1,0:T(8,128)(2,1)} %copy-done.4, bf16[128,768]{1,0:T(8,128)(2,1)} %copy-done.6, bf16[128,768]{1,0:T(8,128)(2,1)} %copy-done.7, bf16[128,768]{1,0:T(8,128)(2,1)} %copy-done.8, ...), custom_call_target="tpu_custom_call" | custom-call | flops 4194304 | bytes 4194304 | tf_op jit(solution)/shard_map/tail/pallas_call | solution.py:396
  (261 shorter events, 53.4 us)
Async XLA Ops:
  4.0 9.8 %collective-permute-start = (bf16[128,512]{1,0:T(8,128)(2,1)S(1)}, bf16[128,512]{1,0:T(8,128)(2,1)S(1)}, u32[]{:S(2)}, u32[]{:S(2)}) collective-permute-start(bf16[128,512]{1,0:T(8,128)(2,1)S(1)} %multiply_convert_fusion.1), channel_id=1, source_target_pairs={{0,1},{1,0},{2,3},{3,2},{4,5},{5,4},{6,7},{7,6},{8,9},{9,8},{10,11... | collective-permute-start | bytes 393224 | tf_op jit(solution)/shard_map/ppermute | solution.py:425
  7.2 12.9 %collective-permute-start.1 = (bf16[128,512]{1,0:T(8,128)(2,1)S(1)}, bf16[128,512]{1,0:T(8,128)(2,1)S(1)}, u32[]{:S(2)}, u32[]{:S(2)}) collective-permute-start(bf16[128,512]{1,0:T(8,128)(2,1)S(1)} %multiply_convert_fusion.1), channel_id=1, source_target_pairs={{0,2},{1,3},{2,0},{3,1},{4,6},{5,7},{6,4},{7,5},{8,10},{9,11},{10,... | collective-permute-start | bytes 393224 | tf_op jit(solution)/shard_map/ppermute | solution.py:425
  9.8 10.3 %collective-permute-start.2 = (bf16[128,512]{1,0:T(8,128)(2,1)S(1)}, bf16[128,512]{1,0:T(8,128)(2,1)S(1)}, u32[]{:S(2)}, u32[]{:S(2)}) collective-permute-start(bf16[128,512]{1,0:T(8,128)(2,1)S(1)} %multiply_convert_fusion.1), channel_id=1, source_target_pairs={{0,3},{1,2},{2,1},{3,0},{4,7},{5,6},{6,5},{7,4},{8,11},{9,10},{10,... | collective-permute-start | bytes 393224 | tf_op jit(solution)/shard_map/ppermute | solution.py:425
  24.8 14.3 %collective-permute-start.3 = (f32[4,64,1024]{2,1,0:T(8,128)S(1)}, f32[4,64,1024]{2,1,0:T(8,128)}, u32[]{:S(2)}, u32[]{:S(2)}) collective-permute-start(f32[4,64,1024]{2,1,0:T(8,128)S(1)} %fusion), channel_id=1, source_target_pairs={{0,4},{4,0},{8,12},{12,8},{16,20},{20,16},{24,28},{28,24},{1,5},{5... | collective-permute-start | bytes 3145736 | tf_op jit(solution)/shard_map/ppermute | solution.py:419
  27.7 8.4 %collective-permute-start.26 = (bf16[1,128,256]{2,1,0:T(8,128)(2,1)S(1)}, bf16[1,128,256]{2,1,0:T(8,128)(2,1)S(1)}, u32[]{:S(2)}, u32[]{:S(2)}) collective-permute-start(bf16[1,128,256]{2,1,0:T(8,128)(2,1)S(1)} %constant_dynamic-slice_fusion.1), channel_id=1, source_target_pairs={{0,2},{1,3},{2,0},{3,1},{4,6},{5,7},{6,4},{7,5},{8,10},{9,11},{10,... | collective-permute-start | bytes 196616 | tf_op jit(solution)/shard_map/ppermute | solution.py:425
  28.7 7.4 %collective-permute-start.27 = (bf16[1,128,256]{2,1,0:T(8,128)(2,1)S(1)}, bf16[1,128,256]{2,1,0:T(8,128)(2,1)S(1)}, u32[]{:S(2)}, u32[]{:S(2)}) collective-permute-start(bf16[1,128,256]{2,1,0:T(8,128)(2,1)S(1)} %constant_dynamic-slice_fusion.1), channel_id=1, source_target_pairs={{0,3},{1,2},{2,1},{3,0},{4,7},{5,6},{6,5},{7,4},{8,11},{9,10},{10,... | collective-permute-start | bytes 196616 | tf_op jit(solution)/shard_map/ppermute | solution.py:425
  36.1 9.2 %collective-permute-start.28 = (bf16[1,384,256]{2,1,0:T(8,128)(2,1)S(1)}, bf16[1,384,256]{2,1,0:T(8,128)(2,1)S(1)}, u32[]{:S(2)}, u32[]{:S(2)}) collective-permute-start(bf16[1,384,256]{2,1,0:T(8,128)(2,1)S(1)} %constant_dynamic-update-slice_fusion.refs_0_), channel_id=1, source_target_pairs={{0,8},{4,12},{8,0},{12,4},{16,24},{20,28},{24,16},{28,20},{1,9},{5... | collective-permute-start | bytes 589832 | tf_op jit(solution)/shard_map/ppermute | solution.py:422
  40.3 24.4 %collective-permute-start.4 = (f32[64,1024]{1,0:T(8,128)S(1)}, f32[64,1024]{1,0:T(8,128)S(1)}, u32[]{:S(2)}, u32[]{:S(2)}) collective-permute-start(f32[64,1024]{1,0:T(8,128)S(1)} %get-tuple-element.43), channel_id=1, source_target_pairs={{0,8},{4,12},{8,0},{12,4},{16,24},{20,28},{24,16},{28,20},{1,9},{5... | collective-permute-start | bytes 786440 | tf_op jit(solution)/shard_map/ppermute | solution.py:422
  40.9 24.3 %collective-permute-start.5 = (f32[64,1024]{1,0:T(8,128)S(1)}, f32[64,1024]{1,0:T(8,128)S(1)}, u32[]{:S(2)}, u32[]{:S(2)}) collective-permute-start(f32[64,1024]{1,0:T(8,128)S(1)} %get-tuple-element.45), channel_id=1, source_target_pairs={{0,16},{4,20},{8,24},{12,28},{16,0},{20,4},{24,8},{28,12},{1,17},{... | collective-permute-start | bytes 786440 | tf_op jit(solution)/shard_map/ppermute | solution.py:422
  42.4 22.9 %collective-permute-start.6 = (f32[64,1024]{1,0:T(8,128)S(1)}, f32[64,1024]{1,0:T(8,128)S(1)}, u32[]{:S(2)}, u32[]{:S(2)}) collective-permute-start(f32[64,1024]{1,0:T(8,128)S(1)} %get-tuple-element.44), channel_id=1, source_target_pairs={{0,24},{4,28},{8,16},{12,20},{16,8},{20,12},{24,0},{28,4},{1,25},{... | collective-permute-start | bytes 786440 | tf_op jit(solution)/shard_map/ppermute | solution.py:422
  43.8 17.7 %collective-permute-start.29 = (bf16[1,384,256]{2,1,0:T(8,128)(2,1)S(1)}, bf16[1,384,256]{2,1,0:T(8,128)(2,1)S(1)}, u32[]{:S(2)}, u32[]{:S(2)}) collective-permute-start(bf16[1,384,256]{2,1,0:T(8,128)(2,1)S(1)} %constant_dynamic-update-slice_fusion.refs_0_), channel_id=1, source_target_pairs={{0,16},{4,20},{8,24},{12,28},{16,0},{20,4},{24,8},{28,12},{1,17},{... | collective-permute-start | bytes 589832 | tf_op jit(solution)/shard_map/ppermute | solution.py:422
  45.3 19.3 %collective-permute-start.30 = (bf16[1,384,256]{2,1,0:T(8,128)(2,1)S(1)}, bf16[1,384,256]{2,1,0:T(8,128)(2,1)S(1)}, u32[]{:S(2)}, u32[]{:S(2)}) collective-permute-start(bf16[1,384,256]{2,1,0:T(8,128)(2,1)S(1)} %constant_dynamic-update-slice_fusion.refs_0_), channel_id=1, source_target_pairs={{0,24},{4,28},{8,16},{12,20},{16,8},{20,12},{24,0},{28,4},{1,25},{... | collective-permute-start | bytes 589832 | tf_op jit(solution)/shard_map/ppermute | solution.py:422
  61.5 45.1 %collective-permute-start.35 = (bf16[8,16,2048]{2,1,0:T(8,128)(2,1)S(1)}, bf16[8,16,2048]{2,1,0:T(8,128)(2,1)}, u32[]{:S(2)}, u32[]{:S(2)}) collective-permute-start(bf16[8,16,2048]{2,1,0:T(8,128)(2,1)S(1)} %bitcast.110), channel_id=1, source_target_pairs={{0,2},{1,3},{2,0},{3,1},{4,6},{5,7},{6,4},{7,5},{8,10},{9,11},{10,... | collective-permute-start | bytes 1572872 | tf_op jit(solution)/shard_map/ppermute | solution.py:425
  66.8 40.0 %collective-permute-start.24 = (bf16[8,16,2048]{2,1,0:T(8,128)(2,1)S(1)}, bf16[8,16,2048]{2,1,0:T(8,128)(2,1)}, u32[]{:S(2)}, u32[]{:S(2)}) collective-permute-start(bf16[8,16,2048]{2,1,0:T(8,128)(2,1)S(1)} %bitcast.111), channel_id=1, source_target_pairs={{0,1},{1,0},{2,3},{3,2},{4,5},{5,4},{6,7},{7,6},{8,9},{9,8},{10,11... | collective-permute-start | bytes 1572872 | tf_op jit(solution)/shard_map/ppermute | solution.py:425
  66.9 32.3 %collective-permute-start.14 = (bf16[64,1024]{1,0:T(8,128)(2,1)S(1)}, bf16[64,1024]{1,0:T(8,128)(2,1)S(1)}, u32[]{:S(2)}, u32[]{:S(2)}) collective-permute-start(bf16[64,1024]{1,0:T(8,128)(2,1)S(1)} %fusion.19.refs_0_), channel_id=1, source_target_pairs={{0,1},{1,0},{2,3},{3,2},{4,5},{5,4},{6,7},{7,6},{8,9},{9,8},{10,11... | collective-permute-start | bytes 393224 | tf_op jit(solution)/shard_map/ppermute | solution.py:425
  68.9 31.8 %collective-permute-start.15 = (bf16[64,1024]{1,0:T(8,128)(2,1)S(1)}, bf16[64,1024]{1,0:T(8,128)(2,1)S(1)}, u32[]{:S(2)}, u32[]{:S(2)}) collective-permute-start(bf16[64,1024]{1,0:T(8,128)(2,1)S(1)} %fusion.19.refs_0_), channel_id=1, source_target_pairs={{0,2},{1,3},{2,0},{3,1},{4,6},{5,7},{6,4},{7,5},{8,10},{9,11},{10,... | collective-permute-start | bytes 393224 | tf_op jit(solution)/shard_map/ppermute | solution.py:425
  69.0 33.2 %collective-permute-start.16 = (bf16[64,1024]{1,0:T(8,128)(2,1)S(1)}, bf16[64,1024]{1,0:T(8,128)(2,1)S(1)}, u32[]{:S(2)}, u32[]{:S(2)}) collective-permute-start(bf16[64,1024]{1,0:T(8,128)(2,1)S(1)} %fusion.19.refs_0_), channel_id=1, source_target_pairs={{0,3},{1,2},{2,1},{3,0},{4,7},{5,6},{6,5},{7,4},{8,11},{9,10},{10,... | collective-permute-start | bytes 393224 | tf_op jit(solution)/shard_map/ppermute | solution.py:425
  99.2 8.9 %collective-permute-start.7 = (bf16[64,1024]{1,0:T(8,128)(2,1)S(1)}, bf16[64,1024]{1,0:T(8,128)(2,1)S(1)}, u32[]{:S(2)}, u32[]{:S(2)}) collective-permute-start(bf16[64,1024]{1,0:T(8,128)(2,1)S(1)} %fusion.19.refs_0_), channel_id=1, source_target_pairs={{0,8},{4,12},{8,0},{12,4},{16,24},{20,28},{24,16},{28,20},{1,9},{5... | collective-permute-start | bytes 393224 | tf_op jit(solution)/shard_map/ppermute | solution.py:422
  100.7 8.3 %collective-permute-start.8 = (bf16[64,1024]{1,0:T(8,128)(2,1)S(1)}, bf16[64,1024]{1,0:T(8,128)(2,1)S(1)}, u32[]{:S(2)}, u32[]{:S(2)}) collective-permute-start(bf16[64,1024]{1,0:T(8,128)(2,1)S(1)} %fusion.19.refs_0_), channel_id=1, source_target_pairs={{0,16},{4,20},{8,24},{12,28},{16,0},{20,4},{24,8},{28,12},{1,17},{... | collective-permute-start | bytes 393224 | tf_op jit(solution)/shard_map/ppermute | solution.py:422
  102.2 7.3 %collective-permute-start.9 = (bf16[64,1024]{1,0:T(8,128)(2,1)S(1)}, bf16[64,1024]{1,0:T(8,128)(2,1)S(1)}, u32[]{:S(2)}, u32[]{:S(2)}) collective-permute-start(bf16[64,1024]{1,0:T(8,128)(2,1)S(1)} %fusion.19.refs_0_), channel_id=1, source_target_pairs={{0,24},{4,28},{8,16},{12,20},{16,8},{20,12},{24,0},{28,4},{1,25},{... | collective-permute-start | bytes 393224 | tf_op jit(solution)/shard_map/ppermute | solution.py:422
  106.7 11.2 %collective-permute-start.10 = (bf16[64,1024]{1,0:T(8,128)(2,1)S(1)}, bf16[64,1024]{1,0:T(8,128)(2,1)S(1)}, u32[]{:S(2)}, u32[]{:S(2)}) collective-permute-start(bf16[64,1024]{1,0:T(8,128)(2,1)S(1)} %fusion.19.refs_0_), channel_id=1, source_target_pairs={{0,4},{4,0},{8,12},{12,8},{16,20},{20,16},{24,28},{28,24},{1,5},{5... | collective-permute-start | bytes 393224 | tf_op jit(solution)/shard_map/ppermute | solution.py:419
  106.8 32.8 %collective-permute-start.37 = (bf16[8,16,2048]{2,1,0:T(8,128)(2,1)}, bf16[8,16,2048]{2,1,0:T(8,128)(2,1)S(1)}, u32[]{:S(2)}, u32[]{:S(2)}) collective-permute-start(bf16[8,16,2048]{2,1,0:T(8,128)(2,1)} %collective-permute-done.35.refs_0_), channel_id=1, source_target_pairs={{1,0},{2,3},{5,4},{6,7},{9,8},{10,11},{13,12},{14,15},{17,16},{18,... | collective-permute-start | bytes 1572872 | tf_op jit(solution)/shard_map/ppermute | solution.py:486
  108.1 31.5 %collective-permute-start.36 = (bf16[8,16,2048]{2,1,0:T(8,128)(2,1)S(1)}, bf16[8,16,2048]{2,1,0:T(8,128)(2,1)S(1)}, u32[]{:S(2)}, u32[]{:S(2)}) collective-permute-start(bf16[8,16,2048]{2,1,0:T(8,128)(2,1)S(1)} %bitcast.116), channel_id=1, source_target_pairs={{1,2},{2,1},{5,6},{6,5},{9,10},{10,9},{13,14},{14,13},{17,18},{18,... | collective-permute-start | bytes 1572872 | tf_op jit(solution)/shard_map/ppermute | solution.py:486
  109.0 10.4 %collective-permute-start.11 = (bf16[64,1024]{1,0:T(8,128)(2,1)S(1)}, bf16[64,1024]{1,0:T(8,128)(2,1)}, u32[]{:S(2)}, u32[]{:S(2)}) collective-permute-start(bf16[64,1024]{1,0:T(8,128)(2,1)S(1)} %collective-permute-done.7.refs_1_), channel_id=1, source_target_pairs={{0,4},{4,0},{8,12},{12,8},{16,20},{20,16},{24,28},{28,24},{1,5},{5... | collective-permute-start | bytes 393224 | tf_op jit(solution)/shard_map/ppermute | solution.py:419
  109.6 11.4 %collective-permute-start.12 = (bf16[64,1024]{1,0:T(8,128)(2,1)S(1)}, bf16[64,1024]{1,0:T(8,128)(2,1)}, u32[]{:S(2)}, u32[]{:S(2)}) collective-permute-start(bf16[64,1024]{1,0:T(8,128)(2,1)S(1)} %collective-permute-done.8.refs_2_), channel_id=1, source_target_pairs={{0,4},{4,0},{8,12},{12,8},{16,20},{20,16},{24,28},{28,24},{1,5},{5... | collective-permute-start | bytes 393224 | tf_op jit(solution)/shard_map/ppermute | solution.py:419
  117.9 12.1 %collective-permute-start.17 = (bf16[3,64,1024]{2,1,0:T(8,128)(2,1)S(1)}, bf16[3,64,1024]{2,1,0:T(8,128)(2,1)S(1)}, u32[]{:S(2)}, u32[]{:S(2)}) collective-permute-start(bf16[3,64,1024]{2,1,0:T(8,128)(2,1)S(1)} %pad_maximum_fusion.refs_8_), channel_id=1, source_target_pairs={{0,8},{4,12},{8,0},{12,4},{16,24},{20,28},{24,16},{28,20},{1,9},{5... | collective-permute-start | bytes 1179656 | tf_op jit(solution)/shard_map/ppermute | solution.py:422
  119.4 19.6 %collective-permute-start.18 = (bf16[3,64,1024]{2,1,0:T(8,128)(2,1)S(1)}, bf16[3,64,1024]{2,1,0:T(8,128)(2,1)S(1)}, u32[]{:S(2)}, u32[]{:S(2)}) collective-permute-start(bf16[3,64,1024]{2,1,0:T(8,128)(2,1)S(1)} %pad_maximum_fusion.refs_8_), channel_id=1, source_target_pairs={{0,16},{4,20},{8,24},{12,28},{16,0},{20,4},{24,8},{28,12},{1,17},{... | collective-permute-start | bytes 1179656 | tf_op jit(solution)/shard_map/ppermute | solution.py:422
  121.0 18.1 %collective-permute-start.19 = (bf16[3,64,1024]{2,1,0:T(8,128)(2,1)S(1)}, bf16[3,64,1024]{2,1,0:T(8,128)(2,1)S(1)}, u32[]{:S(2)}, u32[]{:S(2)}) collective-permute-start(bf16[3,64,1024]{2,1,0:T(8,128)(2,1)S(1)} %pad_maximum_fusion.refs_8_), channel_id=1, source_target_pairs={{0,24},{4,28},{8,16},{12,20},{16,8},{20,12},{24,0},{28,4},{1,25},{... | collective-permute-start | bytes 1179656 | tf_op jit(solution)/shard_map/ppermute | solution.py:422
  129.9 18.8 %collective-permute-start.20 = (bf16[3,64,1024]{2,1,0:T(8,128)(2,1)S(1)}, bf16[3,64,1024]{2,1,0:T(8,128)(2,1)S(1)}, u32[]{:S(2)}, u32[]{:S(2)}) collective-permute-start(bf16[3,64,1024]{2,1,0:T(8,128)(2,1)S(1)} %pad_maximum_fusion.refs_8_), channel_id=1, source_target_pairs={{0,4},{4,0},{8,12},{12,8},{16,20},{20,16},{24,28},{28,24},{1,5},{5... | collective-permute-start | bytes 1179656 | tf_op jit(solution)/shard_map/ppermute | solution.py:419
  139.0 9.8 %collective-permute-start.13 = (bf16[64,1024]{1,0:T(8,128)(2,1)}, bf16[64,1024]{1,0:T(8,128)(2,1)}, u32[]{:S(2)}, u32[]{:S(2)}) collective-permute-start(bf16[64,1024]{1,0:T(8,128)(2,1)} %copy-done.53), channel_id=1, source_target_pairs={{0,4},{4,0},{8,12},{12,8},{16,20},{20,16},{24,28},{28,24},{1,5},{5... | collective-permute-start | bytes 393224 | tf_op jit(solution)/shard_map/ppermute | solution.py:419
  139.0 9.8 %collective-permute-start.21 = (bf16[3,64,1024]{2,1,0:T(8,128)(2,1)S(1)}, bf16[3,64,1024]{2,1,0:T(8,128)(2,1)}, u32[]{:S(2)}, u32[]{:S(2)}) collective-permute-start(bf16[3,64,1024]{2,1,0:T(8,128)(2,1)S(1)} %collective-permute-done.17.refs_9_), channel_id=1, source_target_pairs={{0,4},{4,0},{8,12},{12,8},{16,20},{20,16},{24,28},{28,24},{1,5},{5... | collective-permute-start | bytes 1179656 | tf_op jit(solution)/shard_map/ppermute | solution.py:419
  139.5 9.3 %collective-permute-start.22 = (bf16[3,64,1024]{2,1,0:T(8,128)(2,1)S(1)}, bf16[3,64,1024]{2,1,0:T(8,128)(2,1)}, u32[]{:S(2)}, u32[]{:S(2)}) collective-permute-start(bf16[3,64,1024]{2,1,0:T(8,128)(2,1)S(1)} %collective-permute-done.18.refs_10_), channel_id=1, source_target_pairs={{0,4},{4,0},{8,12},{12,8},{16,20},{20,16},{24,28},{28,24},{1,5},{5... | collective-permute-start | bytes 1179656 | tf_op jit(solution)/shard_map/ppermute | solution.py:419
  139.6 9.2 %collective-permute-start.23 = (bf16[3,64,1024]{2,1,0:T(8,128)(2,1)S(1)}, bf16[3,64,1024]{2,1,0:T(8,128)(2,1)S(1)}, u32[]{:S(2)}, u32[]{:S(2)}) collective-permute-start(bf16[3,64,1024]{2,1,0:T(8,128)(2,1)S(1)} %collective-permute-done.19.refs_11_), channel_id=1, source_target_pairs={{0,4},{4,0},{8,12},{12,8},{16,20},{20,16},{24,28},{28,24},{1,5},{5... | collective-permute-start | bytes 1179656 | tf_op jit(solution)/shard_map/ppermute | solution.py:419
  187.0 28.8 %collective-permute-start.46 = (f32[64,1024]{1,0:T(8,128)S(1)}, f32[64,1024]{1,0:T(8,128)}, u32[]{:S(2)}, u32[]{:S(2)}) collective-permute-start(f32[64,1024]{1,0:T(8,128)S(1)} %get-tuple-element.40), channel_id=1, source_target_pairs={{0,8},{4,12},{8,0},{12,4},{16,24},{20,28},{24,16},{28,20},{1,9},{5... | collective-permute-start | bytes 786440 | tf_op jit(solution)/shard_map/ppermute | solution.py:422
  188.5 27.3 %collective-permute-start.47 = (f32[64,1024]{1,0:T(8,128)S(1)}, f32[64,1024]{1,0:T(8,128)}, u32[]{:S(2)}, u32[]{:S(2)}) collective-permute-start(f32[64,1024]{1,0:T(8,128)S(1)} %get-tuple-element.42), channel_id=1, source_target_pairs={{0,16},{4,20},{8,24},{12,28},{16,0},{20,4},{24,8},{28,12},{1,17},{... | collective-permute-start | bytes 786440 | tf_op jit(solution)/shard_map/ppermute | solution.py:422
  189.1 26.8 %collective-permute-start.48 = (f32[64,1024]{1,0:T(8,128)S(1)}, f32[64,1024]{1,0:T(8,128)}, u32[]{:S(2)}, u32[]{:S(2)}) collective-permute-start(f32[64,1024]{1,0:T(8,128)S(1)} %get-tuple-element.41), channel_id=1, source_target_pairs={{0,24},{4,28},{8,16},{12,20},{16,8},{20,12},{24,0},{28,4},{1,25},{... | collective-permute-start | bytes 786440 | tf_op jit(solution)/shard_map/ppermute | solution.py:422
  202.0 18.6 %collective-permute-start.59 = (f32[2,128,256]{2,1,0:T(8,128)}, f32[2,128,256]{2,1,0:T(8,128)S(1)}, u32[]{:S(2)}, u32[]{:S(2)}) collective-permute-start(f32[2,128,256]{2,1,0:T(8,128)} %bitcast.118), channel_id=1, source_target_pairs={{0,4},{4,0},{8,12},{12,8},{16,20},{20,16},{24,28},{28,24},{1,5},{5... | collective-permute-start | bytes 786440 | tf_op jit(solution)/shard_map/ppermute | solution.py:419
  218.7 8.0 %collective-permute-start.50 = (bf16[64,1024]{1,0:T(8,128)(2,1)S(1)}, bf16[64,1024]{1,0:T(8,128)(2,1)S(1)}, u32[]{:S(2)}, u32[]{:S(2)}) collective-permute-start(bf16[64,1024]{1,0:T(8,128)(2,1)S(1)} %fusion.11.refs_0_), channel_id=1, source_target_pairs={{0,16},{4,20},{8,24},{12,28},{16,0},{20,4},{24,8},{28,12},{1,17},{... | collective-permute-start | bytes 393224 | tf_op jit(solution)/shard_map/ppermute | solution.py:422
  219.2 7.5 %collective-permute-start.51 = (bf16[64,1024]{1,0:T(8,128)(2,1)S(1)}, bf16[64,1024]{1,0:T(8,128)(2,1)S(1)}, u32[]{:S(2)}, u32[]{:S(2)}) collective-permute-start(bf16[64,1024]{1,0:T(8,128)(2,1)S(1)} %fusion.11.refs_0_), channel_id=1, source_target_pairs={{0,24},{4,28},{8,16},{12,20},{16,8},{20,12},{24,0},{28,4},{1,25},{... | collective-permute-start | bytes 393224 | tf_op jit(solution)/shard_map/ppermute | solution.py:422
  221.6 19.6 %collective-permute-start.60 = (bf16[128,256]{1,0:T(8,128)(2,1)S(1)}, bf16[128,256]{1,0:T(8,128)(2,1)S(1)}, u32[]{:S(2)}, u32[]{:S(2)}) collective-permute-start(bf16[128,256]{1,0:T(8,128)(2,1)S(1)} %fusion.25), channel_id=1, source_target_pairs={{0,8},{4,12},{8,0},{12,4},{16,24},{20,28},{24,16},{28,20},{1,9},{5... | collective-permute-start | bytes 196616 | tf_op jit(solution)/shard_map/ppermute | solution.py:422
  227.3 15.4 %collective-permute-start.62 = (bf16[128,256]{1,0:T(8,128)(2,1)S(1)}, bf16[128,256]{1,0:T(8,128)(2,1)S(1)}, u32[]{:S(2)}, u32[]{:S(2)}) collective-permute-start(bf16[128,256]{1,0:T(8,128)(2,1)S(1)} %get-tuple-element.46), channel_id=1, source_target_pairs={{0,16},{4,20},{8,24},{12,28},{16,0},{20,4},{24,8},{28,12},{1,17},{... | collective-permute-start | bytes 196616 | tf_op jit(solution)/shard_map/ppermute | solution.py:422
  227.8 14.9 %collective-permute-start.63 = (bf16[128,256]{1,0:T(8,128)(2,1)S(1)}, bf16[128,256]{1,0:T(8,128)(2,1)S(1)}, u32[]{:S(2)}, u32[]{:S(2)}) collective-permute-start(bf16[128,256]{1,0:T(8,128)(2,1)S(1)} %get-tuple-element.47), channel_id=1, source_target_pairs={{0,24},{4,28},{8,16},{12,20},{16,8},{20,12},{24,0},{28,4},{1,25},{... | collective-permute-start | bytes 196616 | tf_op jit(solution)/shard_map/ppermute | solution.py:422
  236.3 9.3 %collective-permute-start.56 = (bf16[128,512]{1,0:T(8,128)(2,1)}, bf16[128,512]{1,0:T(8,128)(2,1)S(1)}, u32[]{:S(2)}, u32[]{:S(2)}) collective-permute-start(bf16[128,512]{1,0:T(8,128)(2,1)} %get-tuple-element.31), channel_id=1, source_target_pairs={{0,1},{1,0},{2,3},{3,2},{4,5},{5,4},{6,7},{7,6},{8,9},{9,8},{10,11... | collective-permute-start | bytes 393224 | tf_op jit(solution)/shard_map/ppermute | solution.py:425
  239.9 13.1 %collective-permute-start.57 = (bf16[128,512]{1,0:T(8,128)(2,1)}, bf16[128,512]{1,0:T(8,128)(2,1)S(1)}, u32[]{:S(2)}, u32[]{:S(2)}) collective-permute-start(bf16[128,512]{1,0:T(8,128)(2,1)} %get-tuple-element.32), channel_id=1, source_target_pairs={{0,2},{1,3},{2,0},{3,1},{4,6},{5,7},{6,4},{7,5},{8,10},{9,11},{10,... | collective-permute-start | bytes 393224 | tf_op jit(solution)/shard_map/ppermute | solution.py:425
  241.2 11.7 %collective-permute-start.58 = (bf16[128,512]{1,0:T(8,128)(2,1)}, bf16[128,512]{1,0:T(8,128)(2,1)S(1)}, u32[]{:S(2)}, u32[]{:S(2)}) collective-permute-start(bf16[128,512]{1,0:T(8,128)(2,1)} %get-tuple-element.33), channel_id=1, source_target_pairs={{0,3},{1,2},{2,1},{3,0},{4,7},{5,6},{6,5},{7,4},{8,11},{9,10},{10,... | collective-permute-start | bytes 393224 | tf_op jit(solution)/shard_map/ppermute | solution.py:425
  255.5 8.8 %collective-permute-start.65 = (bf16[128,768]{1,0:T(8,128)(2,1)S(1)}, bf16[128,768]{1,0:T(8,128)(2,1)S(1)}, u32[]{:S(2)}, u32[]{:S(2)}) collective-permute-start(bf16[128,768]{1,0:T(8,128)(2,1)S(1)} %pad_maximum_fusion.1.refs_0_.refs_8_), channel_id=1, source_target_pairs={{0,16},{4,20},{8,24},{12,28},{16,0},{20,4},{24,8},{28,12},{1,17},{... | collective-permute-start | bytes 589832 | tf_op jit(solution)/shard_map/ppermute | solution.py:422
  256.1 8.2 %collective-permute-start.66 = (bf16[128,768]{1,0:T(8,128)(2,1)S(1)}, bf16[128,768]{1,0:T(8,128)(2,1)S(1)}, u32[]{:S(2)}, u32[]{:S(2)}) collective-permute-start(bf16[128,768]{1,0:T(8,128)(2,1)S(1)} %pad_maximum_fusion.1.refs_0_.refs_8_), channel_id=1, source_target_pairs={{0,24},{4,28},{8,16},{12,20},{16,8},{20,12},{24,0},{28,4},{1,25},{... | collective-permute-start | bytes 589832 | tf_op jit(solution)/shard_map/ppermute | solution.py:422
  258.0 10.0 %collective-permute-start.67 = (bf16[128,768]{1,0:T(8,128)(2,1)S(1)}, bf16[128,768]{1,0:T(8,128)(2,1)S(1)}, u32[]{:S(2)}, u32[]{:S(2)}) collective-permute-start(bf16[128,768]{1,0:T(8,128)(2,1)S(1)} %pad_maximum_fusion.1.refs_0_.refs_8_), channel_id=1, source_target_pairs={{0,4},{4,0},{8,12},{12,8},{16,20},{20,16},{24,28},{28,24},{1,5},{5... | collective-permute-start | bytes 589832 | tf_op jit(solution)/shard_map/ppermute | solution.py:419
  (78 other events, 701.5 us)

commit v4 on v3

--- a/solution.py
+++ b/solution.py
@@ -582,8 +582,12 @@
 
 
 def solution(mesh):
-    in_specs = (P("qry", None), P(), P("psg", "qry"), P("psg", "qry"), P("qry", None, None), P())
-    out_specs = (P("qry"), P("qry", None), P("psg", "qry"), P("qry", None, None))
+    rows, split = P("qry", None), P("psg", "qry")
+    book = P("qry", None, None)
     return jax.shard_map(
-        run_device, mesh=mesh, in_specs=in_specs, out_specs=out_specs, check_vma=False
-    )
+        run_device,
+        mesh=mesh,
+        in_specs=(rows, P(), split, split, book, P()),
+        out_specs=(P("qry"), rows, split, book),
+        check_vma=False,
+    )

time: 275 us -> 275 us (level)
  no operation moved by 1% of the time
where the time goes in v4:
time: 275 us; the launch traced here: 274 us
  Pallas kernels  89.8 us (33%)
  waiting for transfers between devices  82.2 us (30%)
  starting transfers between devices  63.2 us (23%)
  other arithmetic  14.1 us (5%)
  matrix products  12.4 us (5%)
  local copies, waits for them, and re-layouts  10.7 us (4%)
    ppermute x14, waiting for transfers between devices, turn(): return lax.ppermute(x, 'qry', [(i, i ^ k) for i in range(owners)])  42 us
    ppermute x27, waiting for transfers between devices, chip(): return lax.ppermute(x, 'psg', [(i, i ^ 2 * k) for i in range(shards)])  38.1 us
    pallas_call x4, Pallas kernels, decode(): pl.pallas_call(decode_body, grid=(slices // 2,), in_specs=[pl.BlockSpec((...  32.7 us
    ppermute x27, starting transfers between devices, chip(): return lax.ppermute(x, 'psg', [(i, i ^ 2 * k) for i in range(shards)])  31.9 us
    ppermute x14, starting transfers between devices, turn(): return lax.ppermute(x, 'qry', [(i, i ^ k) for i in range(owners)])  24.3 us
    pallas_call x3, Pallas kernels, book_grads(): pl.pallas_call(functools.partial(book_body, 32, 4), grid_spec=pltpu.Prefe...  18.3 us
    pallas_call x1, Pallas kernels, scores_of(): pl.pallas_call(functools.partial(score_body, chunks, blocks), grid=(width...  16.5 us
    pallas_call x1, Pallas kernels, score_grads(): pl.pallas_call(functools.partial(grad_body, len(stats)), grid=(width // t...  7.29 us
  transfers between devices with their start and end apart: 71, of which 17 were waited for; matrix products, arithmetic and copies ran while one was open for 9% of the time, Pallas kernels for 21%

profile of v4, /device:TPU:0, one launch (start us, length us, event | category | flops | bytes accessed | tf_op | source)
XLA Modules:
  0.0 273.8 jit_solution(4177422792371940793)
XLA Ops:
  0.6 1.6 multiply_reduce_fusion
  4.0 3.1 %collective-permute-start = (bf16[128,512]{1,0:T(8,128)(2,1)S(1)}, bf16[128,512]{1,0:T(8,128)(2,1)S(1)}, u32[]{:S(2)}, u32[]{:S(2)}) collective-permute-start(bf16[128,512]{1,0:T(8,128)(2,1)S(1)} %multiply_convert_fusion.1), channel_id=1, source_target_pairs={{0,1},{1,0},{2,3},{3,2},{4,5},{5,4},{6,7},{7,6},{8,9},{9,8},{10,11... | collective-permute-start | bytes 393224 | tf_op jit(solution)/shard_map/ppermute | solution.py:425
  7.2 2.6 collective-permute-start.1
  13.8 6.2 %collective-permute-done.1 = bf16[128,512]{1,0:T(8,128)(2,1)S(1)} collective-permute-done((bf16[128,512]{1,0:T(8,128)(2,1)S(1)}, bf16[128,512]{1,0:T(8,128)(2,1)S(1)}, u32[]{:S(2)}, u32[]{:S(2)}) %collective-permute-start.1) | collective-permute-done | bytes 131104 | tf_op jit(solution)/shard_map/ppermute | solution.py:425
  20.8 2.6 arrange.2
  25.7 2.0 collective-permute-start.25
  30.4 5.7 %collective-permute-done.26 = bf16[1,128,256]{2,1,0:T(8,128)(2,1)S(1)} collective-permute-done((bf16[1,128,256]{2,1,0:T(8,128)(2,1)S(1)}, bf16[1,128,256]{2,1,0:T(8,128)(2,1)S(1)}, u32[]{:S(2)}, u32[]{:S(2)}) %collective-permute-start.26) | collective-permute-done | bytes 65568 | tf_op jit(solution)/shard_map/ppermute | solution.py:425
  36.1 1.6 collective-permute-start.28
  40.9 1.5 collective-permute-start.5
  43.8 1.5 collective-permute-start.29
  45.8 15.7 %collective-permute-done.29.refs_2_ = bf16[1,384,256]{2,1,0:T(8,128)(2,1)S(1)} collective-permute-done((bf16[1,384,256]{2,1,0:T(8,128)(2,1)S(1)}, bf16[1,384,256]{2,1,0:T(8,128)(2,1)S(1)}, u32[]{:S(2)}, u32[]{:S(2)}) %collective-permute-start.29) | collective-permute-done | bytes 196640 | tf_op jit(solution)/shard_map/ppermute | solution.py:422
  61.5 3.1 %collective-permute-start.35 = (bf16[8,16,2048]{2,1,0:T(8,128)(2,1)S(1)}, bf16[8,16,2048]{2,1,0:T(8,128)(2,1)}, u32[]{:S(2)}, u32[]{:S(2)}) collective-permute-start(bf16[8,16,2048]{2,1,0:T(8,128)(2,1)S(1)} %bitcast.110), channel_id=1, source_target_pairs={{0,2},{1,3},{2,0},{3,1},{4,6},{5,7},{6,4},{7,5},{8,10},{9,11},{10,... | collective-permute-start | bytes 1572872 | tf_op jit(solution)/shard_map/ppermute | solution.py:425
  66.9 1.9 collective-permute-start.14
  69.0 2.4 collective-permute-start.16
  71.4 8.1 %decode.4.refs_16_.refs_10_ = bf16[1024,2048]{1,0:T(8,128)(2,1)} custom-call(bf16[8,16,2048]{2,1,0:T(8,128)(2,1)} %bitcast.112, bf16[8,128,256]{2,1,0:T(8,128)(2,1)} %bitcast.128), custom_call_target="tpu_custom_call" | custom-call | flops 4294967296 | bytes 4194304 | tf_op jit(solution)/shard_map/decode/pallas_call | solution.py:79
  79.6 19.6 %collective-permute-done.14 = bf16[64,1024]{1,0:T(8,128)(2,1)S(1)} collective-permute-done((bf16[64,1024]{1,0:T(8,128)(2,1)S(1)}, bf16[64,1024]{1,0:T(8,128)(2,1)S(1)}, u32[]{:S(2)}, u32[]{:S(2)}) %collective-permute-start.14) | collective-permute-done | bytes 131104 | tf_op jit(solution)/shard_map/ppermute | solution.py:425
  99.2 1.5 collective-permute-start.7
  100.7 1.5 collective-permute-start.8
  103.3 3.4 %arrange.3.refs_1_.refs_2_ = bf16[8,384,256]{2,1,0:T(8,128)(2,1)} custom-call(s32[8]{0:T(128)} %iota_xor_fusion.order.places, bf16[1,384,256]{2,1,0:T(8,128)(2,1)} %copy-done.17, bf16[1,384,256]{2,1,0:T(8,128)(2,1)} %copy-done.18, bf16[1,384,256]{2,1,0:T(8,128)(2,1)} %copy-done.19, bf16[1,384,256]{2,1,0:T(8,128)(2,1)} %copy-done.20, ...), custom_call_target="tpu_custom_call" | custom-call | bytes 6291456 | tf_op jit(solution)/shard_map/arrange/pallas_call | solution.py:43
  109.7 8.2 %decode.6.refs_18_ = bf16[1024,2048]{1,0:T(8,128)(2,1)} custom-call(bf16[8,16,2048]{2,1,0:T(8,128)(2,1)} %collective-permute-done.35.refs_0_, bf16[8,384,256]{2,1,0:T(8,128)(2,1)} %arrange.3.refs_1_.refs_2_), custom_call_target="tpu_custom_call" | custom-call | flops 4294967296 | bytes 4194304 | tf_op jit(solution)/shard_map/decode/pallas_call | solution.py:79
  117.9 1.6 collective-permute-start.17
  119.4 1.5 collective-permute-start.18
  121.4 8.1 %decode.5.refs_17_ = bf16[1024,2048]{1,0:T(8,128)(2,1)} custom-call(bf16[8,16,2048]{2,1,0:T(8,128)(2,1)} %collective-permute-done.24.refs_0_, bf16[8,384,256]{2,1,0:T(8,128)(2,1)} %arrange.3.refs_1_.refs_2_), custom_call_target="tpu_custom_call" | custom-call | flops 4294967296 | bytes 4194304 | tf_op jit(solution)/shard_map/decode/pallas_call | solution.py:79
  129.9 9.1 %collective-permute-done.18.refs_10_ = bf16[3,64,1024]{2,1,0:T(8,128)(2,1)S(1)} collective-permute-done((bf16[3,64,1024]{2,1,0:T(8,128)(2,1)S(1)}, bf16[3,64,1024]{2,1,0:T(8,128)(2,1)S(1)}, u32[]{:S(2)}, u32[]{:S(2)}) %collective-permute-start.18) | collective-permute-done | bytes 393248 | tf_op jit(solution)/shard_map/ppermute | solution.py:422
  140.5 8.2 %decode.7.refs_19_ = bf16[1024,2048]{1,0:T(8,128)(2,1)} custom-call(bf16[8,16,2048]{2,1,0:T(8,128)(2,1)} %copy-done.45, bf16[8,16,2048]{2,1,0:T(8,128)(2,1)} %copy-done.44, bf16[8,384,256]{2,1,0:T(8,128)(2,1)} %arrange.3.refs_1_.refs_2_), custom_call_target="tpu_custom_call" | custom-call | flops 4294967296 | bytes 4194304 | tf_op jit(solution)/shard_map/decode/pallas_call | solution.py:79
  150.3 16.5 %scores.1 = (f32[512,2048]{1,0:T(8,128)}, f32[8,512]{1,0:T(8,128)}, bf16[512,1024]{1,0:T(8,128)(2,1)}) custom-call(bf16[64,1024]{1,0:T(8,128)(2,1)} %copy-done.32, bf16[64,1024]{1,0:T(8,128)(2,1)} %copy-done.51, bf16[64,1024]{1,0:T(8,128)(2,1)} %copy-done.52, bf16[64,1024]{1,0:T(8,128)(2,1)} %copy-done.53, bf16[64,1024]{1,0:T(8,128)(2,1)} %copy-done.54, ...), custom_call_target="tpu_custom_call" | custom-call | flops 8589934592 | bytes 16777216 | tf_op jit(solution)/shard_map/scores/pallas_call | solution.py:170
  171.8 1.9 collective-permute-done.40.refs_3_
  175.6 7.3 %score_grads.1 = (bf16[512,2048]{1,0:T(8,128)(2,1)}, f32[4,64,1024]{2,1,0:T(8,128)}, f32[4,64,1024]{2,1,0:T(8,128)}, f32[8,512]{1,0:T(8,128)}) custom-call(f32[8,512]{1,0:T(8,128)} %get-tuple-element.25.refs_0_, f32[8,512]{1,0:T(8,128)} %copy-done.37, f32[8,512]{1,0:T(8,128)} %copy-done.38, f32[8,512]{1,0:T(8,128)} %copy-done.39, f32[8,512]{1,0:T(8,128)} %copy-done.40, ...), custom_call_target="tpu_custom_call" | custom-call | flops 2147483648 | bytes 6291456 | tf_op jit(solution)/shard_map/score_grads/pallas_call | solution.py:244
  187.0 1.6 collective-permute-start.46
  189.1 1.5 collective-permute-start.48
  190.5 6.3 %multiply_convert_fusion.grads = bf16[1024,2048]{1,0:T(8,128)(2,1)} fusion(bf16[512,1024]{1,0:T(8,128)(2,1)} %get-tuple-element.34, bf16[512,2048]{1,0:T(8,128)(2,1)} %get-tuple-element.36), kind=kOutput, calls=%fused_computation.1 | convolution fusion | flops 2151677952 | bytes 7340032 | tf_op jit(solution)/shard_map/dot_general | solution.py:508
  196.9 5.1 %book_grads.4 = f32[32,8,256]{2,1,0:T(8,128)} custom-call(s32[2]{0:T(128)} %get-tuple-element.51.order, bf16[1024,2048]{1,0:T(8,128)(2,1)} %multiply_convert_fusion.grads, bf16[8,16,2048]{2,1,0:T(8,128)(2,1)} %bitcast.113), custom_call_target="tpu_custom_call" | custom-call | flops 1073741824 | bytes 1048576 | tf_op jit(solution)/shard_map/book_grads/pallas_call | solution.py:309
  202.0 7.9 %book_grads.5 = f32[64,8,256]{2,1,0:T(8,128)} custom-call(s32[4]{0:T(128)} %pad_add_fusion.order, bf16[1024,2048]{1,0:T(8,128)(2,1)} %multiply_convert_fusion.grads, bf16[8,16,2048]{2,1,0:T(8,128)(2,1)} %bitcast.114), custom_call_target="tpu_custom_call" | custom-call | flops 2147483648 | bytes 2097152 | tf_op jit(solution)/shard_map/book_grads/pallas_call | solution.py:309
  209.9 5.3 %book_grads.3 = f32[32,8,256]{2,1,0:T(8,128)} custom-call(s32[2]{0:T(128)} %get-tuple-element.49.order, bf16[1024,2048]{1,0:T(8,128)(2,1)} %multiply_convert_fusion.grads, bf16[8,16,2048]{2,1,0:T(8,128)(2,1)} %bitcast.115), custom_call_target="tpu_custom_call" | custom-call | flops 1073741824 | bytes 1048576 | tf_op jit(solution)/shard_map/book_grads/pallas_call | solution.py:309
  217.1 1.6 collective-permute-start.49
  219.2 1.5 collective-permute-start.51
  221.6 1.6 collective-permute-start.60
  223.4 3.3 %collective-permute-done.50.refs_2_ = bf16[64,1024]{1,0:T(8,128)(2,1)S(1)} collective-permute-done((bf16[64,1024]{1,0:T(8,128)(2,1)S(1)}, bf16[64,1024]{1,0:T(8,128)(2,1)S(1)}, u32[]{:S(2)}, u32[]{:S(2)}) %collective-permute-start.50) | collective-permute-done | bytes 131104 | tf_op jit(solution)/shard_map/ppermute | solution.py:422
  232.1 4.1 %back_part.1 = (bf16[128,512]{1,0:T(8,128)(2,1)}, bf16[128,512]{1,0:T(8,128)(2,1)}, bf16[128,512]{1,0:T(8,128)(2,1)}, bf16[128,512]{1,0:T(8,128)(2,1)}, bf16[512,1024]{1,0:T(8,128)(2,1)}) custom-call(s32[8]{0:T(128)} %fusion.32.order, bf16[64,1024]{1,0:T(8,128)(2,1)} %copy-done.14, bf16[64,1024]{1,0:T(8,128)(2,1)} %copy-done.25, ...), custom_call_target="tpu_custom_call" | custom-call | flops 536870912 | bytes 2097152 | tf_op jit(solution)/shard_map/back_part/pallas_call | solution.py:349
  236.3 3.6 %collective-permute-start.56 = (bf16[128,512]{1,0:T(8,128)(2,1)}, bf16[128,512]{1,0:T(8,128)(2,1)S(1)}, u32[]{:S(2)}, u32[]{:S(2)}) collective-permute-start(bf16[128,512]{1,0:T(8,128)(2,1)} %get-tuple-element.31), channel_id=1, source_target_pairs={{0,1},{1,0},{2,3},{3,2},{4,5},{5,4},{6,7},{7,6},{8,9},{9,8},{10,11... | collective-permute-start | bytes 393224 | tf_op jit(solution)/shard_map/ppermute | solution.py:425
  241.2 1.5 collective-permute-start.58
  242.8 2.8 %collective-permute-done.56 = bf16[128,512]{1,0:T(8,128)(2,1)S(1)} collective-permute-done((bf16[128,512]{1,0:T(8,128)(2,1)}, bf16[128,512]{1,0:T(8,128)(2,1)S(1)}, u32[]{:S(2)}, u32[]{:S(2)}) %collective-permute-start.56) | collective-permute-done | bytes 131104 | tf_op jit(solution)/shard_map/ppermute | solution.py:425
  245.5 7.4 %collective-permute-done.57 = bf16[128,512]{1,0:T(8,128)(2,1)S(1)} collective-permute-done((bf16[128,512]{1,0:T(8,128)(2,1)}, bf16[128,512]{1,0:T(8,128)(2,1)S(1)}, u32[]{:S(2)}, u32[]{:S(2)}) %collective-permute-start.57) | collective-permute-done | bytes 131104 | tf_op jit(solution)/shard_map/ppermute | solution.py:425
  253.9 1.5 collective-permute-start.64
  258.0 2.9 %collective-permute-done.64.refs_1_.refs_9_ = bf16[128,768]{1,0:T(8,128)(2,1)S(1)} collective-permute-done((bf16[128,768]{1,0:T(8,128)(2,1)S(1)}, bf16[128,768]{1,0:T(8,128)(2,1)S(1)}, u32[]{:S(2)}, u32[]{:S(2)}) %collective-permute-start.64) | collective-permute-done | bytes 196640 | tf_op jit(solution)/shard_map/ppermute | solution.py:422
  261.0 3.3 %collective-permute-done.65.refs_2_.refs_10_ = bf16[128,768]{1,0:T(8,128)(2,1)S(1)} collective-permute-done((bf16[128,768]{1,0:T(8,128)(2,1)S(1)}, bf16[128,768]{1,0:T(8,128)(2,1)S(1)}, u32[]{:S(2)}, u32[]{:S(2)}) %collective-permute-start.65) | collective-permute-done | bytes 196640 | tf_op jit(solution)/shard_map/ppermute | solution.py:422
  264.8 3.3 %fusion.40 = f32[512,1024]{1,0:T(8,128)} fusion(bf16[512,512]{1,0:T(8,128)(2,1)S(1)} %bitcast.109, bf16[512,1024]{1,0:T(8,128)(2,1)} %get-tuple-element.38), kind=kOutput, calls=%fused_computation.90 | convolution fusion | flops 536870912 | bytes 3670016 | tf_op jit(solution)/shard_map/dot_general | solution.py:539
  268.9 4.9 %tail.1 = (bf16[128,4096]{1,0:T(8,128)(2,1)}, f32[8,128,256]{2,1,0:T(8,128)}) custom-call(s32[8]{0:T(128)} %fusion.36.order, s32[8]{0:T(128)} %iota_xor_fusion.order.places, bf16[128,768]{1,0:T(8,128)(2,1)} %copy-done.4, bf16[128,768]{1,0:T(8,128)(2,1)} %copy-done.6, bf16[128,768]{1,0:T(8,128)(2,1)} %copy-done.7, bf16[128,768]{1,0:T(8,128)(2,1)} %copy-done.8, ...), custom_call_target="tpu_custom_call" | custom-call | flops 4194304 | bytes 4194304 | tf_op jit(solution)/shard_map/tail/pallas_call | solution.py:396
  (261 shorter events, 53.4 us)
Async XLA Ops:
  4.0 9.8 %collective-permute-start = (bf16[128,512]{1,0:T(8,128)(2,1)S(1)}, bf16[128,512]{1,0:T(8,128)(2,1)S(1)}, u32[]{:S(2)}, u32[]{:S(2)}) collective-permute-start(bf16[128,512]{1,0:T(8,128)(2,1)S(1)} %multiply_convert_fusion.1), channel_id=1, source_target_pairs={{0,1},{1,0},{2,3},{3,2},{4,5},{5,4},{6,7},{7,6},{8,9},{9,8},{10,11... | collective-permute-start | bytes 393224 | tf_op jit(solution)/shard_map/ppermute | solution.py:425
  7.2 12.9 %collective-permute-start.1 = (bf16[128,512]{1,0:T(8,128)(2,1)S(1)}, bf16[128,512]{1,0:T(8,128)(2,1)S(1)}, u32[]{:S(2)}, u32[]{:S(2)}) collective-permute-start(bf16[128,512]{1,0:T(8,128)(2,1)S(1)} %multiply_convert_fusion.1), channel_id=1, source_target_pairs={{0,2},{1,3},{2,0},{3,1},{4,6},{5,7},{6,4},{7,5},{8,10},{9,11},{10,... | collective-permute-start | bytes 393224 | tf_op jit(solution)/shard_map/ppermute | solution.py:425
  9.8 10.3 %collective-permute-start.2 = (bf16[128,512]{1,0:T(8,128)(2,1)S(1)}, bf16[128,512]{1,0:T(8,128)(2,1)S(1)}, u32[]{:S(2)}, u32[]{:S(2)}) collective-permute-start(bf16[128,512]{1,0:T(8,128)(2,1)S(1)} %multiply_convert_fusion.1), channel_id=1, source_target_pairs={{0,3},{1,2},{2,1},{3,0},{4,7},{5,6},{6,5},{7,4},{8,11},{9,10},{10,... | collective-permute-start | bytes 393224 | tf_op jit(solution)/shard_map/ppermute | solution.py:425
  24.8 14.3 %collective-permute-start.3 = (f32[4,64,1024]{2,1,0:T(8,128)S(1)}, f32[4,64,1024]{2,1,0:T(8,128)}, u32[]{:S(2)}, u32[]{:S(2)}) collective-permute-start(f32[4,64,1024]{2,1,0:T(8,128)S(1)} %fusion), channel_id=1, source_target_pairs={{0,4},{4,0},{8,12},{12,8},{16,20},{20,16},{24,28},{28,24},{1,5},{5... | collective-permute-start | bytes 3145736 | tf_op jit(solution)/shard_map/ppermute | solution.py:419
  27.7 8.4 %collective-permute-start.26 = (bf16[1,128,256]{2,1,0:T(8,128)(2,1)S(1)}, bf16[1,128,256]{2,1,0:T(8,128)(2,1)S(1)}, u32[]{:S(2)}, u32[]{:S(2)}) collective-permute-start(bf16[1,128,256]{2,1,0:T(8,128)(2,1)S(1)} %constant_dynamic-slice_fusion.1), channel_id=1, source_target_pairs={{0,2},{1,3},{2,0},{3,1},{4,6},{5,7},{6,4},{7,5},{8,10},{9,11},{10,... | collective-permute-start | bytes 196616 | tf_op jit(solution)/shard_map/ppermute | solution.py:425
  28.7 7.4 %collective-permute-start.27 = (bf16[1,128,256]{2,1,0:T(8,128)(2,1)S(1)}, bf16[1,128,256]{2,1,0:T(8,128)(2,1)S(1)}, u32[]{:S(2)}, u32[]{:S(2)}) collective-permute-start(bf16[1,128,256]{2,1,0:T(8,128)(2,1)S(1)} %constant_dynamic-slice_fusion.1), channel_id=1, source_target_pairs={{0,3},{1,2},{2,1},{3,0},{4,7},{5,6},{6,5},{7,4},{8,11},{9,10},{10,... | collective-permute-start | bytes 196616 | tf_op jit(solution)/shard_map/ppermute | solution.py:425
  36.1 9.2 %collective-permute-start.28 = (bf16[1,384,256]{2,1,0:T(8,128)(2,1)S(1)}, bf16[1,384,256]{2,1,0:T(8,128)(2,1)S(1)}, u32[]{:S(2)}, u32[]{:S(2)}) collective-permute-start(bf16[1,384,256]{2,1,0:T(8,128)(2,1)S(1)} %constant_dynamic-update-slice_fusion.refs_0_), channel_id=1, source_target_pairs={{0,8},{4,12},{8,0},{12,4},{16,24},{20,28},{24,16},{28,20},{1,9},{5... | collective-permute-start | bytes 589832 | tf_op jit(solution)/shard_map/ppermute | solution.py:422
  40.3 24.4 %collective-permute-start.4 = (f32[64,1024]{1,0:T(8,128)S(1)}, f32[64,1024]{1,0:T(8,128)S(1)}, u32[]{:S(2)}, u32[]{:S(2)}) collective-permute-start(f32[64,1024]{1,0:T(8,128)S(1)} %get-tuple-element.43), channel_id=1, source_target_pairs={{0,8},{4,12},{8,0},{12,4},{16,24},{20,28},{24,16},{28,20},{1,9},{5... | collective-permute-start | bytes 786440 | tf_op jit(solution)/shard_map/ppermute | solution.py:422
  40.9 24.3 %collective-permute-start.5 = (f32[64,1024]{1,0:T(8,128)S(1)}, f32[64,1024]{1,0:T(8,128)S(1)}, u32[]{:S(2)}, u32[]{:S(2)}) collective-permute-start(f32[64,1024]{1,0:T(8,128)S(1)} %get-tuple-element.45), channel_id=1, source_target_pairs={{0,16},{4,20},{8,24},{12,28},{16,0},{20,4},{24,8},{28,12},{1,17},{... | collective-permute-start | bytes 786440 | tf_op jit(solution)/shard_map/ppermute | solution.py:422
  42.4 22.9 %collective-permute-start.6 = (f32[64,1024]{1,0:T(8,128)S(1)}, f32[64,1024]{1,0:T(8,128)S(1)}, u32[]{:S(2)}, u32[]{:S(2)}) collective-permute-start(f32[64,1024]{1,0:T(8,128)S(1)} %get-tuple-element.44), channel_id=1, source_target_pairs={{0,24},{4,28},{8,16},{12,20},{16,8},{20,12},{24,0},{28,4},{1,25},{... | collective-permute-start | bytes 786440 | tf_op jit(solution)/shard_map/ppermute | solution.py:422
  43.8 17.7 %collective-permute-start.29 = (bf16[1,384,256]{2,1,0:T(8,128)(2,1)S(1)}, bf16[1,384,256]{2,1,0:T(8,128)(2,1)S(1)}, u32[]{:S(2)}, u32[]{:S(2)}) collective-permute-start(bf16[1,384,256]{2,1,0:T(8,128)(2,1)S(1)} %constant_dynamic-update-slice_fusion.refs_0_), channel_id=1, source_target_pairs={{0,16},{4,20},{8,24},{12,28},{16,0},{20,4},{24,8},{28,12},{1,17},{... | collective-permute-start | bytes 589832 | tf_op jit(solution)/shard_map/ppermute | solution.py:422
  45.3 19.3 %collective-permute-start.30 = (bf16[1,384,256]{2,1,0:T(8,128)(2,1)S(1)}, bf16[1,384,256]{2,1,0:T(8,128)(2,1)S(1)}, u32[]{:S(2)}, u32[]{:S(2)}) collective-permute-start(bf16[1,384,256]{2,1,0:T(8,128)(2,1)S(1)} %constant_dynamic-update-slice_fusion.refs_0_), channel_id=1, source_target_pairs={{0,24},{4,28},{8,16},{12,20},{16,8},{20,12},{24,0},{28,4},{1,25},{... | collective-permute-start | bytes 589832 | tf_op jit(solution)/shard_map/ppermute | solution.py:422
  61.5 45.1 %collective-permute-start.35 = (bf16[8,16,2048]{2,1,0:T(8,128)(2,1)S(1)}, bf16[8,16,2048]{2,1,0:T(8,128)(2,1)}, u32[]{:S(2)}, u32[]{:S(2)}) collective-permute-start(bf16[8,16,2048]{2,1,0:T(8,128)(2,1)S(1)} %bitcast.110), channel_id=1, source_target_pairs={{0,2},{1,3},{2,0},{3,1},{4,6},{5,7},{6,4},{7,5},{8,10},{9,11},{10,... | collective-permute-start | bytes 1572872 | tf_op jit(solution)/shard_map/ppermute | solution.py:425
  66.8 40.0 %collective-permute-start.24 = (bf16[8,16,2048]{2,1,0:T(8,128)(2,1)S(1)}, bf16[8,16,2048]{2,1,0:T(8,128)(2,1)}, u32[]{:S(2)}, u32[]{:S(2)}) collective-permute-start(bf16[8,16,2048]{2,1,0:T(8,128)(2,1)S(1)} %bitcast.111), channel_id=1, source_target_pairs={{0,1},{1,0},{2,3},{3,2},{4,5},{5,4},{6,7},{7,6},{8,9},{9,8},{10,11... | collective-permute-start | bytes 1572872 | tf_op jit(solution)/shard_map/ppermute | solution.py:425
  66.9 32.3 %collective-permute-start.14 = (bf16[64,1024]{1,0:T(8,128)(2,1)S(1)}, bf16[64,1024]{1,0:T(8,128)(2,1)S(1)}, u32[]{:S(2)}, u32[]{:S(2)}) collective-permute-start(bf16[64,1024]{1,0:T(8,128)(2,1)S(1)} %fusion.19.refs_0_), channel_id=1, source_target_pairs={{0,1},{1,0},{2,3},{3,2},{4,5},{5,4},{6,7},{7,6},{8,9},{9,8},{10,11... | collective-permute-start | bytes 393224 | tf_op jit(solution)/shard_map/ppermute | solution.py:425
  68.9 31.8 %collective-permute-start.15 = (bf16[64,1024]{1,0:T(8,128)(2,1)S(1)}, bf16[64,1024]{1,0:T(8,128)(2,1)S(1)}, u32[]{:S(2)}, u32[]{:S(2)}) collective-permute-start(bf16[64,1024]{1,0:T(8,128)(2,1)S(1)} %fusion.19.refs_0_), channel_id=1, source_target_pairs={{0,2},{1,3},{2,0},{3,1},{4,6},{5,7},{6,4},{7,5},{8,10},{9,11},{10,... | collective-permute-start | bytes 393224 | tf_op jit(solution)/shard_map/ppermute | solution.py:425
  69.0 33.2 %collective-permute-start.16 = (bf16[64,1024]{1,0:T(8,128)(2,1)S(1)}, bf16[64,1024]{1,0:T(8,128)(2,1)S(1)}, u32[]{:S(2)}, u32[]{:S(2)}) collective-permute-start(bf16[64,1024]{1,0:T(8,128)(2,1)S(1)} %fusion.19.refs_0_), channel_id=1, source_target_pairs={{0,3},{1,2},{2,1},{3,0},{4,7},{5,6},{6,5},{7,4},{8,11},{9,10},{10,... | collective-permute-start | bytes 393224 | tf_op jit(solution)/shard_map/ppermute | solution.py:425
  99.2 8.9 %collective-permute-start.7 = (bf16[64,1024]{1,0:T(8,128)(2,1)S(1)}, bf16[64,1024]{1,0:T(8,128)(2,1)S(1)}, u32[]{:S(2)}, u32[]{:S(2)}) collective-permute-start(bf16[64,1024]{1,0:T(8,128)(2,1)S(1)} %fusion.19.refs_0_), channel_id=1, source_target_pairs={{0,8},{4,12},{8,0},{12,4},{16,24},{20,28},{24,16},{28,20},{1,9},{5... | collective-permute-start | bytes 393224 | tf_op jit(solution)/shard_map/ppermute | solution.py:422
  100.7 8.3 %collective-permute-start.8 = (bf16[64,1024]{1,0:T(8,128)(2,1)S(1)}, bf16[64,1024]{1,0:T(8,128)(2,1)S(1)}, u32[]{:S(2)}, u32[]{:S(2)}) collective-permute-start(bf16[64,1024]{1,0:T(8,128)(2,1)S(1)} %fusion.19.refs_0_), channel_id=1, source_target_pairs={{0,16},{4,20},{8,24},{12,28},{16,0},{20,4},{24,8},{28,12},{1,17},{... | collective-permute-start | bytes 393224 | tf_op jit(solution)/shard_map/ppermute | solution.py:422
  102.2 7.3 %collective-permute-start.9 = (bf16[64,1024]{1,0:T(8,128)(2,1)S(1)}, bf16[64,1024]{1,0:T(8,128)(2,1)S(1)}, u32[]{:S(2)}, u32[]{:S(2)}) collective-permute-start(bf16[64,1024]{1,0:T(8,128)(2,1)S(1)} %fusion.19.refs_0_), channel_id=1, source_target_pairs={{0,24},{4,28},{8,16},{12,20},{16,8},{20,12},{24,0},{28,4},{1,25},{... | collective-permute-start | bytes 393224 | tf_op jit(solution)/shard_map/ppermute | solution.py:422
  106.7 11.2 %collective-permute-start.10 = (bf16[64,1024]{1,0:T(8,128)(2,1)S(1)}, bf16[64,1024]{1,0:T(8,128)(2,1)S(1)}, u32[]{:S(2)}, u32[]{:S(2)}) collective-permute-start(bf16[64,1024]{1,0:T(8,128)(2,1)S(1)} %fusion.19.refs_0_), channel_id=1, source_target_pairs={{0,4},{4,0},{8,12},{12,8},{16,20},{20,16},{24,28},{28,24},{1,5},{5... | collective-permute-start | bytes 393224 | tf_op jit(solution)/shard_map/ppermute | solution.py:419
  106.8 32.8 %collective-permute-start.37 = (bf16[8,16,2048]{2,1,0:T(8,128)(2,1)}, bf16[8,16,2048]{2,1,0:T(8,128)(2,1)S(1)}, u32[]{:S(2)}, u32[]{:S(2)}) collective-permute-start(bf16[8,16,2048]{2,1,0:T(8,128)(2,1)} %collective-permute-done.35.refs_0_), channel_id=1, source_target_pairs={{1,0},{2,3},{5,4},{6,7},{9,8},{10,11},{13,12},{14,15},{17,16},{18,... | collective-permute-start | bytes 1572872 | tf_op jit(solution)/shard_map/ppermute | solution.py:486
  108.1 31.5 %collective-permute-start.36 = (bf16[8,16,2048]{2,1,0:T(8,128)(2,1)S(1)}, bf16[8,16,2048]{2,1,0:T(8,128)(2,1)S(1)}, u32[]{:S(2)}, u32[]{:S(2)}) collective-permute-start(bf16[8,16,2048]{2,1,0:T(8,128)(2,1)S(1)} %bitcast.116), channel_id=1, source_target_pairs={{1,2},{2,1},{5,6},{6,5},{9,10},{10,9},{13,14},{14,13},{17,18},{18,... | collective-permute-start | bytes 1572872 | tf_op jit(solution)/shard_map/ppermute | solution.py:486
  109.0 10.4 %collective-permute-start.11 = (bf16[64,1024]{1,0:T(8,128)(2,1)S(1)}, bf16[64,1024]{1,0:T(8,128)(2,1)}, u32[]{:S(2)}, u32[]{:S(2)}) collective-permute-start(bf16[64,1024]{1,0:T(8,128)(2,1)S(1)} %collective-permute-done.7.refs_1_), channel_id=1, source_target_pairs={{0,4},{4,0},{8,12},{12,8},{16,20},{20,16},{24,28},{28,24},{1,5},{5... | collective-permute-start | bytes 393224 | tf_op jit(solution)/shard_map/ppermute | solution.py:419
  109.6 11.4 %collective-permute-start.12 = (bf16[64,1024]{1,0:T(8,128)(2,1)S(1)}, bf16[64,1024]{1,0:T(8,128)(2,1)}, u32[]{:S(2)}, u32[]{:S(2)}) collective-permute-start(bf16[64,1024]{1,0:T(8,128)(2,1)S(1)} %collective-permute-done.8.refs_2_), channel_id=1, source_target_pairs={{0,4},{4,0},{8,12},{12,8},{16,20},{20,16},{24,28},{28,24},{1,5},{5... | collective-permute-start | bytes 393224 | tf_op jit(solution)/shard_map/ppermute | solution.py:419
  117.9 12.1 %collective-permute-start.17 = (bf16[3,64,1024]{2,1,0:T(8,128)(2,1)S(1)}, bf16[3,64,1024]{2,1,0:T(8,128)(2,1)S(1)}, u32[]{:S(2)}, u32[]{:S(2)}) collective-permute-start(bf16[3,64,1024]{2,1,0:T(8,128)(2,1)S(1)} %pad_maximum_fusion.refs_8_), channel_id=1, source_target_pairs={{0,8},{4,12},{8,0},{12,4},{16,24},{20,28},{24,16},{28,20},{1,9},{5... | collective-permute-start | bytes 1179656 | tf_op jit(solution)/shard_map/ppermute | solution.py:422
  119.4 19.6 %collective-permute-start.18 = (bf16[3,64,1024]{2,1,0:T(8,128)(2,1)S(1)}, bf16[3,64,1024]{2,1,0:T(8,128)(2,1)S(1)}, u32[]{:S(2)}, u32[]{:S(2)}) collective-permute-start(bf16[3,64,1024]{2,1,0:T(8,128)(2,1)S(1)} %pad_maximum_fusion.refs_8_), channel_id=1, source_target_pairs={{0,16},{4,20},{8,24},{12,28},{16,0},{20,4},{24,8},{28,12},{1,17},{... | collective-permute-start | bytes 1179656 | tf_op jit(solution)/shard_map/ppermute | solution.py:422
  121.0 18.1 %collective-permute-start.19 = (bf16[3,64,1024]{2,1,0:T(8,128)(2,1)S(1)}, bf16[3,64,1024]{2,1,0:T(8,128)(2,1)S(1)}, u32[]{:S(2)}, u32[]{:S(2)}) collective-permute-start(bf16[3,64,1024]{2,1,0:T(8,128)(2,1)S(1)} %pad_maximum_fusion.refs_8_), channel_id=1, source_target_pairs={{0,24},{4,28},{8,16},{12,20},{16,8},{20,12},{24,0},{28,4},{1,25},{... | collective-permute-start | bytes 1179656 | tf_op jit(solution)/shard_map/ppermute | solution.py:422
  129.9 18.8 %collective-permute-start.20 = (bf16[3,64,1024]{2,1,0:T(8,128)(2,1)S(1)}, bf16[3,64,1024]{2,1,0:T(8,128)(2,1)S(1)}, u32[]{:S(2)}, u32[]{:S(2)}) collective-permute-start(bf16[3,64,1024]{2,1,0:T(8,128)(2,1)S(1)} %pad_maximum_fusion.refs_8_), channel_id=1, source_target_pairs={{0,4},{4,0},{8,12},{12,8},{16,20},{20,16},{24,28},{28,24},{1,5},{5... | collective-permute-start | bytes 1179656 | tf_op jit(solution)/shard_map/ppermute | solution.py:419
  139.0 9.8 %collective-permute-start.13 = (bf16[64,1024]{1,0:T(8,128)(2,1)}, bf16[64,1024]{1,0:T(8,128)(2,1)}, u32[]{:S(2)}, u32[]{:S(2)}) collective-permute-start(bf16[64,1024]{1,0:T(8,128)(2,1)} %copy-done.53), channel_id=1, source_target_pairs={{0,4},{4,0},{8,12},{12,8},{16,20},{20,16},{24,28},{28,24},{1,5},{5... | collective-permute-start | bytes 393224 | tf_op jit(solution)/shard_map/ppermute | solution.py:419
  139.0 9.8 %collective-permute-start.21 = (bf16[3,64,1024]{2,1,0:T(8,128)(2,1)S(1)}, bf16[3,64,1024]{2,1,0:T(8,128)(2,1)}, u32[]{:S(2)}, u32[]{:S(2)}) collective-permute-start(bf16[3,64,1024]{2,1,0:T(8,128)(2,1)S(1)} %collective-permute-done.17.refs_9_), channel_id=1, source_target_pairs={{0,4},{4,0},{8,12},{12,8},{16,20},{20,16},{24,28},{28,24},{1,5},{5... | collective-permute-start | bytes 1179656 | tf_op jit(solution)/shard_map/ppermute | solution.py:419
  139.5 9.3 %collective-permute-start.22 = (bf16[3,64,1024]{2,1,0:T(8,128)(2,1)S(1)}, bf16[3,64,1024]{2,1,0:T(8,128)(2,1)}, u32[]{:S(2)}, u32[]{:S(2)}) collective-permute-start(bf16[3,64,1024]{2,1,0:T(8,128)(2,1)S(1)} %collective-permute-done.18.refs_10_), channel_id=1, source_target_pairs={{0,4},{4,0},{8,12},{12,8},{16,20},{20,16},{24,28},{28,24},{1,5},{5... | collective-permute-start | bytes 1179656 | tf_op jit(solution)/shard_map/ppermute | solution.py:419
  139.6 9.2 %collective-permute-start.23 = (bf16[3,64,1024]{2,1,0:T(8,128)(2,1)S(1)}, bf16[3,64,1024]{2,1,0:T(8,128)(2,1)S(1)}, u32[]{:S(2)}, u32[]{:S(2)}) collective-permute-start(bf16[3,64,1024]{2,1,0:T(8,128)(2,1)S(1)} %collective-permute-done.19.refs_11_), channel_id=1, source_target_pairs={{0,4},{4,0},{8,12},{12,8},{16,20},{20,16},{24,28},{28,24},{1,5},{5... | collective-permute-start | bytes 1179656 | tf_op jit(solution)/shard_map/ppermute | solution.py:419
  187.0 28.8 %collective-permute-start.46 = (f32[64,1024]{1,0:T(8,128)S(1)}, f32[64,1024]{1,0:T(8,128)}, u32[]{:S(2)}, u32[]{:S(2)}) collective-permute-start(f32[64,1024]{1,0:T(8,128)S(1)} %get-tuple-element.40), channel_id=1, source_target_pairs={{0,8},{4,12},{8,0},{12,4},{16,24},{20,28},{24,16},{28,20},{1,9},{5... | collective-permute-start | bytes 786440 | tf_op jit(solution)/shard_map/ppermute | solution.py:422
  188.5 27.3 %collective-permute-start.47 = (f32[64,1024]{1,0:T(8,128)S(1)}, f32[64,1024]{1,0:T(8,128)}, u32[]{:S(2)}, u32[]{:S(2)}) collective-permute-start(f32[64,1024]{1,0:T(8,128)S(1)} %get-tuple-element.42), channel_id=1, source_target_pairs={{0,16},{4,20},{8,24},{12,28},{16,0},{20,4},{24,8},{28,12},{1,17},{... | collective-permute-start | bytes 786440 | tf_op jit(solution)/shard_map/ppermute | solution.py:422
  189.1 26.8 %collective-permute-start.48 = (f32[64,1024]{1,0:T(8,128)S(1)}, f32[64,1024]{1,0:T(8,128)}, u32[]{:S(2)}, u32[]{:S(2)}) collective-permute-start(f32[64,1024]{1,0:T(8,128)S(1)} %get-tuple-element.41), channel_id=1, source_target_pairs={{0,24},{4,28},{8,16},{12,20},{16,8},{20,12},{24,0},{28,4},{1,25},{... | collective-permute-start | bytes 786440 | tf_op jit(solution)/shard_map/ppermute | solution.py:422
  202.0 18.6 %collective-permute-start.59 = (f32[2,128,256]{2,1,0:T(8,128)}, f32[2,128,256]{2,1,0:T(8,128)S(1)}, u32[]{:S(2)}, u32[]{:S(2)}) collective-permute-start(f32[2,128,256]{2,1,0:T(8,128)} %bitcast.118), channel_id=1, source_target_pairs={{0,4},{4,0},{8,12},{12,8},{16,20},{20,16},{24,28},{28,24},{1,5},{5... | collective-permute-start | bytes 786440 | tf_op jit(solution)/shard_map/ppermute | solution.py:419
  218.7 8.0 %collective-permute-start.50 = (bf16[64,1024]{1,0:T(8,128)(2,1)S(1)}, bf16[64,1024]{1,0:T(8,128)(2,1)S(1)}, u32[]{:S(2)}, u32[]{:S(2)}) collective-permute-start(bf16[64,1024]{1,0:T(8,128)(2,1)S(1)} %fusion.11.refs_0_), channel_id=1, source_target_pairs={{0,16},{4,20},{8,24},{12,28},{16,0},{20,4},{24,8},{28,12},{1,17},{... | collective-permute-start | bytes 393224 | tf_op jit(solution)/shard_map/ppermute | solution.py:422
  219.2 7.5 %collective-permute-start.51 = (bf16[64,1024]{1,0:T(8,128)(2,1)S(1)}, bf16[64,1024]{1,0:T(8,128)(2,1)S(1)}, u32[]{:S(2)}, u32[]{:S(2)}) collective-permute-start(bf16[64,1024]{1,0:T(8,128)(2,1)S(1)} %fusion.11.refs_0_), channel_id=1, source_target_pairs={{0,24},{4,28},{8,16},{12,20},{16,8},{20,12},{24,0},{28,4},{1,25},{... | collective-permute-start | bytes 393224 | tf_op jit(solution)/shard_map/ppermute | solution.py:422
  221.6 19.6 %collective-permute-start.60 = (bf16[128,256]{1,0:T(8,128)(2,1)S(1)}, bf16[128,256]{1,0:T(8,128)(2,1)S(1)}, u32[]{:S(2)}, u32[]{:S(2)}) collective-permute-start(bf16[128,256]{1,0:T(8,128)(2,1)S(1)} %fusion.25), channel_id=1, source_target_pairs={{0,8},{4,12},{8,0},{12,4},{16,24},{20,28},{24,16},{28,20},{1,9},{5... | collective-permute-start | bytes 196616 | tf_op jit(solution)/shard_map/ppermute | solution.py:422
  227.3 15.4 %collective-permute-start.62 = (bf16[128,256]{1,0:T(8,128)(2,1)S(1)}, bf16[128,256]{1,0:T(8,128)(2,1)S(1)}, u32[]{:S(2)}, u32[]{:S(2)}) collective-permute-start(bf16[128,256]{1,0:T(8,128)(2,1)S(1)} %get-tuple-element.46), channel_id=1, source_target_pairs={{0,16},{4,20},{8,24},{12,28},{16,0},{20,4},{24,8},{28,12},{1,17},{... | collective-permute-start | bytes 196616 | tf_op jit(solution)/shard_map/ppermute | solution.py:422
  227.8 14.9 %collective-permute-start.63 = (bf16[128,256]{1,0:T(8,128)(2,1)S(1)}, bf16[128,256]{1,0:T(8,128)(2,1)S(1)}, u32[]{:S(2)}, u32[]{:S(2)}) collective-permute-start(bf16[128,256]{1,0:T(8,128)(2,1)S(1)} %get-tuple-element.47), channel_id=1, source_target_pairs={{0,24},{4,28},{8,16},{12,20},{16,8},{20,12},{24,0},{28,4},{1,25},{... | collective-permute-start | bytes 196616 | tf_op jit(solution)/shard_map/ppermute | solution.py:422
  236.3 9.3 %collective-permute-start.56 = (bf16[128,512]{1,0:T(8,128)(2,1)}, bf16[128,512]{1,0:T(8,128)(2,1)S(1)}, u32[]{:S(2)}, u32[]{:S(2)}) collective-permute-start(bf16[128,512]{1,0:T(8,128)(2,1)} %get-tuple-element.31), channel_id=1, source_target_pairs={{0,1},{1,0},{2,3},{3,2},{4,5},{5,4},{6,7},{7,6},{8,9},{9,8},{10,11... | collective-permute-start | bytes 393224 | tf_op jit(solution)/shard_map/ppermute | solution.py:425
  239.9 13.1 %collective-permute-start.57 = (bf16[128,512]{1,0:T(8,128)(2,1)}, bf16[128,512]{1,0:T(8,128)(2,1)S(1)}, u32[]{:S(2)}, u32[]{:S(2)}) collective-permute-start(bf16[128,512]{1,0:T(8,128)(2,1)} %get-tuple-element.32), channel_id=1, source_target_pairs={{0,2},{1,3},{2,0},{3,1},{4,6},{5,7},{6,4},{7,5},{8,10},{9,11},{10,... | collective-permute-start | bytes 393224 | tf_op jit(solution)/shard_map/ppermute | solution.py:425
  241.2 11.7 %collective-permute-start.58 = (bf16[128,512]{1,0:T(8,128)(2,1)}, bf16[128,512]{1,0:T(8,128)(2,1)S(1)}, u32[]{:S(2)}, u32[]{:S(2)}) collective-permute-start(bf16[128,512]{1,0:T(8,128)(2,1)} %get-tuple-element.33), channel_id=1, source_target_pairs={{0,3},{1,2},{2,1},{3,0},{4,7},{5,6},{6,5},{7,4},{8,11},{9,10},{10,... | collective-permute-start | bytes 393224 | tf_op jit(solution)/shard_map/ppermute | solution.py:425
  255.5 8.8 %collective-permute-start.65 = (bf16[128,768]{1,0:T(8,128)(2,1)S(1)}, bf16[128,768]{1,0:T(8,128)(2,1)S(1)}, u32[]{:S(2)}, u32[]{:S(2)}) collective-permute-start(bf16[128,768]{1,0:T(8,128)(2,1)S(1)} %pad_maximum_fusion.1.refs_0_.refs_8_), channel_id=1, source_target_pairs={{0,16},{4,20},{8,24},{12,28},{16,0},{20,4},{24,8},{28,12},{1,17},{... | collective-permute-start | bytes 589832 | tf_op jit(solution)/shard_map/ppermute | solution.py:422
  256.1 8.2 %collective-permute-start.66 = (bf16[128,768]{1,0:T(8,128)(2,1)S(1)}, bf16[128,768]{1,0:T(8,128)(2,1)S(1)}, u32[]{:S(2)}, u32[]{:S(2)}) collective-permute-start(bf16[128,768]{1,0:T(8,128)(2,1)S(1)} %pad_maximum_fusion.1.refs_0_.refs_8_), channel_id=1, source_target_pairs={{0,24},{4,28},{8,16},{12,20},{16,8},{20,12},{24,0},{28,4},{1,25},{... | collective-permute-start | bytes 589832 | tf_op jit(solution)/shard_map/ppermute | solution.py:422
  258.0 10.0 %collective-permute-start.67 = (bf16[128,768]{1,0:T(8,128)(2,1)S(1)}, bf16[128,768]{1,0:T(8,128)(2,1)S(1)}, u32[]{:S(2)}, u32[]{:S(2)}) collective-permute-start(bf16[128,768]{1,0:T(8,128)(2,1)S(1)} %pad_maximum_fusion.1.refs_0_.refs_8_), channel_id=1, source_target_pairs={{0,4},{4,0},{8,12},{12,8},{16,20},{20,16},{24,28},{28,24},{1,5},{5... | collective-permute-start | bytes 589832 | tf_op jit(solution)/shard_map/ppermute | solution.py:419
  (78 other events, 701.5 us)

commit v5 on v4

--- a/solution.py
+++ b/solution.py
@@ -54,23 +54,30 @@
     )(order, *pieces)
 
 
+def look_up(code, values):
+    width = code.shape[1]
+    full = jnp.broadcast_to(code, (8, width))
+    low = full & 127
+    high = full >= 128
+    values = values.astype(f32)
+    first, second = values[:, :128], values[:, 128:]
+    pieces = []
+    for c in range(width // 128):
+        lanes = slice(c * 128, (c + 1) * 128)
+        a = jnp.take_along_axis(first, low[:, lanes], axis=1, mode="promise_in_bounds")
+        b = jnp.take_along_axis(second, low[:, lanes], axis=1, mode="promise_in_bounds")
+        pieces.append(jnp.where(high[:, lanes], b, a))
+    return jnp.concatenate(pieces, axis=1).astype(bf16)
+
+
 def decode_body(*refs):
     parts, table, out, index = refs[:-3], refs[-3], refs[-2], refs[-1]
-    pair, count, width = index.shape
+    slices, count, _ = index.shape
     index[...] = sum(codes[...].astype(f32) for codes in parts).astype(jnp.int32)
-    for j, m in [(j, m) for j in range(pair) for m in range(count)]:
-        full = jnp.broadcast_to(index[j, m : m + 1, :], (8, width))
-        low = full & 127
-        high = full >= 128
-        values = table[j, pl.ds(m * 8, 8), :].astype(f32)
-        first, second = values[:, :128], values[:, 128:]
-        pieces = []
-        for c in range(width // 128):
-            lanes = slice(c * 128, (c + 1) * 128)
-            a = jnp.take_along_axis(first, low[:, lanes], axis=1, mode="promise_in_bounds")
-            b = jnp.take_along_axis(second, low[:, lanes], axis=1, mode="promise_in_bounds")
-            pieces.append(jnp.where(high[:, lanes], b, a))
-        out[pl.ds((j * count + m) * 8, 8), :] = jnp.concatenate(pieces, axis=1).astype(bf16)
+    for j in range(slices):
+        for m in range(count):
+            value = look_up(index[j, m : m + 1, :], table[j, pl.ds(m * 8, 8), :])
+            out[pl.ds((j * count + m) * 8, 8), :] = value
 
 
 def decode(parts, tables, layer):
@@ -93,12 +100,13 @@
     return jnp.broadcast_to(row, (128, row.shape[1])).T
 
 
-def score_body(chunks, blocks, *refs):
+def score_body(chunks, blocks, parts, *refs):
     own, others = refs[:chunks], refs[chunks : 2 * chunks]
-    tables = refs[2 * chunks : 2 * chunks + blocks]
-    target, scores, stats, own_rows, held, places, packed = refs[2 * chunks + blocks :]
+    rest = refs[2 * chunks :]
+    tables, codes, rest = rest[: blocks - 1], rest[blocks - 1 : blocks - 1 + parts], rest[blocks - 1 + parts :]
+    book, target, scores, stats, own_rows, held, places, packed, index, last_table = rest
     step, last = pl.program_id(0), pl.num_programs(0) - 1
-    tile = tables[0].shape[1]
+    tile = last_table.shape[1]
     height = own[0].shape[0]
     rows = scores.shape[0]
     group = 128
@@ -114,9 +122,16 @@
         packed[...] = jnp.zeros_like(packed)
 
     def multiply():
+        index[...] = sum(code[...].astype(f32) for code in codes).astype(jnp.int32)
+        slices, count = index.shape[:2]
+        for j in range(slices):
+            for m in range(count):
+                value = look_up(index[j, m : m + 1, :], book[j, pl.ds(m * 8, 8), :])
+                last_table[pl.ds((j * count + m) * 8, 8), :] = value
         total = jnp.dot(held[0], tables[0][...], preferred_element_type=f32)
-        for b in range(1, blocks):
+        for b in range(1, blocks - 1):
             total += jnp.dot(held[b], tables[b][...], preferred_element_type=f32)
+        total += jnp.dot(held[blocks - 1], last_table[...], preferred_element_type=f32)
         scores[:, pl.ds(pl.multiple_of(step * tile, tile), tile)] = total * score_scale
 
     def reduce(t):
@@ -162,17 +177,24 @@
             )
 
 
-def scores_of(own, queries, tables, target):
-    chunks, blocks = len(queries), len(tables)
+def scores_of(own, queries, tables, codes, books, target):
+    chunks, blocks = len(queries), len(tables) + 1
     height, depth = own[0].shape
     width = tables[0].shape[1]
     rows, tile = chunks * height, min(512, width)
+    slices, count = codes[0].shape[:2]
+    levels = books.shape[2]
+    now = lambda i: jnp.minimum(i, width // tile - 1)
     return pl.pallas_call(
-        functools.partial(score_body, chunks, blocks),
+        functools.partial(score_body, chunks, blocks, len(codes)),
         grid=(width // tile + 1,),
         in_specs=[whole(q) for q in own + queries]
-        + [pl.BlockSpec((depth, tile), lambda i: (0, jnp.minimum(i, width // tile - 1))) for _ in tables]
-        + [whole(target)],
+        + [pl.BlockSpec((depth, tile), lambda i: (0, now(i))) for _ in tables]
+        + [pl.BlockSpec((slices, count, tile), lambda i: (0, 0, now(i))) for _ in codes]
+        + [
+            pl.BlockSpec((slices, count * 8, levels), lambda i: (0, blocks - 2, 0)),
+            whole(target),
+        ],
         out_specs=[
             pl.BlockSpec((rows, width), lambda i: (0, 0)),
             pl.BlockSpec((8, rows), lambda i: (0, 0)),
@@ -187,12 +209,14 @@
             pltpu.VMEM((blocks, rows, depth), bf16),
             pltpu.VMEM((rows, 128), f32),
             pltpu.VMEM((rows, 128), f32),
+            pltpu.VMEM((slices, count, tile), jnp.int32),
+            pltpu.VMEM((depth, tile), bf16),
         ],
         cost_estimate=cost(
             2 * rows * blocks * depth * width, blocks * depth * width * 2, rows * width
         ),
         name="scores",
-    )(*own, *queries, *tables, target)
+    )(*own, *queries, *tables, *codes, books, target)
 
 
 def shuffle(value, offset, chunk):
@@ -239,7 +263,7 @@
 
 def score_grads(scores, stats, target, passages):
     rows, width = scores.shape
-    depth, tile = passages.shape[0], min(512, width)
+    depth, tile = passages.shape[0], min(1024, width)
     term = (len(stats) // 2, rows // len(stats), depth)
     return pl.pallas_call(
         functools.partial(grad_body, len(stats)),
@@ -494,10 +518,13 @@
             codes[k] = [hop(waiting, [(1, 2), (2, 1)]), hop(passed, [(1, 0), (2, 3)])]
         else:
             codes[k] = [turn(codes_own if k <= owners // 2 else waiting, k)]
-        passages.append(decode(codes[k], books, k - 1))
+        if k < owners - 1:
+            passages.append(decode(codes[k], books, k - 1))
 
     query_chunks = near_queries + far_queries
-    scores, stats, own_rows_all = scores_of(own_chunks, query_chunks, passages, targets)
+    scores, stats, own_rows_all = scores_of(
+        own_chunks, query_chunks, passages, codes[owners - 1], books, targets
+    )
     near_stats, far_stats = collect(stats)
     score_grad, near_term, far_term, losses_all = score_grads(
         scores, near_stats + far_stats, targets, passages[0]

time: 275 us -> 266 us (0.967)
  Pallas kernels: 89.8 us -> 81 us
    pallas_call x4 -> x3, Pallas kernels: 32.7 us -> 24.5 us  [decode(): pl.pallas_call(decode_body, grid=(slices // 2,), in_specs=[pl.BlockSpec((...]
    ppermute x14, waiting for transfers between devices: 42 us -> 45.9 us  [turn(): return lax.ppermute(x, 'qry', [(i, i ^ k) for i in range(owners)])]
    ppermute x27, waiting for transfers between devices: 38.1 us -> 35 us  [chip(): return lax.ppermute(x, 'psg', [(i, i ^ 2 * k) for i in range(shards)])]
  transfers between devices with their start and end apart: 71 -> 71, of which waited for: 17 -> 22; matrix products, arithmetic and copies ran while one was open for 9% -> 9% of each run, Pallas kernels for 21% -> 19%
where the time goes in v5:
time: 266 us; the launch traced here: 264 us
  waiting for transfers between devices  83 us (31%)
  Pallas kernels  81 us (30%)
  starting transfers between devices  61.9 us (23%)
  other arithmetic  14 us (5%)
  matrix products  12.4 us (5%)
  local copies, waits for them, and re-layouts  10.5 us (4%)
    ppermute x14, waiting for transfers between devices, turn(): return lax.ppermute(x, 'qry', [(i, i ^ k) for i in range(owners)])  45.9 us
    ppermute x27, waiting for transfers between devices, chip(): return lax.ppermute(x, 'psg', [(i, i ^ 2 * k) for i in range(shards)])  35 us
    ppermute x27, starting transfers between devices, chip(): return lax.ppermute(x, 'psg', [(i, i ^ 2 * k) for i in range(shards)])  34.6 us
    pallas_call x3, Pallas kernels, decode(): pl.pallas_call(decode_body, grid=(slices // 2,), in_specs=[pl.BlockSpec((...  24.5 us
    ppermute x14, starting transfers between devices, turn(): return lax.ppermute(x, 'qry', [(i, i ^ k) for i in range(owners)])  22.3 us
    pallas_call x3, Pallas kernels, book_grads(): pl.pallas_call(functools.partial(book_body, 32, 4), grid_spec=pltpu.Prefe...  18.3 us
    pallas_call x1, Pallas kernels, scores_of(): pl.pallas_call(functools.partial(score_body, chunks, blocks, len(codes)),...  16.5 us
    pallas_call x1, Pallas kernels, score_grads(): pl.pallas_call(functools.partial(grad_body, len(stats)), grid=(width // t...  6.61 us
  transfers between devices with their start and end apart: 71, of which 22 were waited for; matrix products, arithmetic and copies ran while one was open for 9% of the time, Pallas kernels for 19%

profile of v5, /device:TPU:0, one launch (start us, length us, event | category | flops | bytes accessed | tf_op | source)
XLA Modules:
  0.0 264.2 jit_solution(1230999288938945271)
XLA Ops:
  0.6 1.6 multiply_reduce_fusion
  4.0 3.1 %collective-permute-start = (bf16[128,512]{1,0:T(8,128)(2,1)S(1)}, bf16[128,512]{1,0:T(8,128)(2,1)S(1)}, u32[]{:S(2)}, u32[]{:S(2)}) collective-permute-start(bf16[128,512]{1,0:T(8,128)(2,1)S(1)} %multiply_convert_fusion.1), channel_id=1, source_target_pairs={{0,1},{1,0},{2,3},{3,2},{4,5},{5,4},{6,7},{7,6},{8,9},{9,8},{10,11... | collective-permute-start | bytes 393224 | tf_op jit(solution)/shard_map/ppermute | solution.py:449
  7.2 2.6 collective-permute-start.1
  13.9 6.2 %collective-permute-done.1 = bf16[128,512]{1,0:T(8,128)(2,1)S(1)} collective-permute-done((bf16[128,512]{1,0:T(8,128)(2,1)S(1)}, bf16[128,512]{1,0:T(8,128)(2,1)S(1)}, u32[]{:S(2)}, u32[]{:S(2)}) %collective-permute-start.1) | collective-permute-done | bytes 131104 | tf_op jit(solution)/shard_map/ppermute | solution.py:449
  20.7 2.6 arrange.2
  25.7 2.0 collective-permute-start.25
  28.6 1.5 collective-permute-start.27
  30.4 5.7 %collective-permute-done.26 = bf16[1,128,256]{2,1,0:T(8,128)(2,1)S(1)} collective-permute-done((bf16[1,128,256]{2,1,0:T(8,128)(2,1)S(1)}, bf16[1,128,256]{2,1,0:T(8,128)(2,1)S(1)}, u32[]{:S(2)}, u32[]{:S(2)}) %collective-permute-start.26) | collective-permute-done | bytes 65568 | tf_op jit(solution)/shard_map/ppermute | solution.py:449
  36.1 1.6 collective-permute-start.28
  37.6 1.5 collective-permute-start.29
  42.9 2.4 collective-permute-start.6
  45.8 12.6 %collective-permute-done.30.refs_3_ = bf16[1,384,256]{2,1,0:T(8,128)(2,1)S(1)} collective-permute-done((bf16[1,384,256]{2,1,0:T(8,128)(2,1)S(1)}, bf16[1,384,256]{2,1,0:T(8,128)(2,1)S(1)}, u32[]{:S(2)}, u32[]{:S(2)}) %collective-permute-start.30) | collective-permute-done | bytes 196640 | tf_op jit(solution)/shard_map/ppermute | solution.py:446
  58.4 3.1 %collective-permute-start.35 = (bf16[8,16,2048]{2,1,0:T(8,128)(2,1)S(1)}, bf16[8,16,2048]{2,1,0:T(8,128)(2,1)S(1)}, u32[]{:S(2)}, u32[]{:S(2)}) collective-permute-start(bf16[8,16,2048]{2,1,0:T(8,128)(2,1)S(1)} %bitcast.110), channel_id=1, source_target_pairs={{0,2},{1,3},{2,0},{3,1},{4,6},{5,7},{6,4},{7,5},{8,10},{9,11},{10,... | collective-permute-start | bytes 1572872 | tf_op jit(solution)/shard_map/ppermute | solution.py:449
  63.4 2.0 collective-permute-start.14
  65.5 2.4 collective-permute-start.16
  67.8 22.8 %collective-permute-done.14 = bf16[64,1024]{1,0:T(8,128)(2,1)S(1)} collective-permute-done((bf16[64,1024]{1,0:T(8,128)(2,1)S(1)}, bf16[64,1024]{1,0:T(8,128)(2,1)S(1)}, u32[]{:S(2)}, u32[]{:S(2)}) %collective-permute-start.14) | collective-permute-done | bytes 131104 | tf_op jit(solution)/shard_map/ppermute | solution.py:449
  90.6 1.5 collective-permute-start.7
  94.5 1.5 collective-permute-start.17
  97.3 1.6 collective-permute-done.9.refs_3_
  98.9 8.2 %decode.3.refs_16_.refs_10_ = bf16[1024,2048]{1,0:T(8,128)(2,1)} custom-call(bf16[8,16,2048]{2,1,0:T(8,128)(2,1)} %bitcast.112, bf16[8,128,256]{2,1,0:T(8,128)(2,1)} %bitcast.128), custom_call_target="tpu_custom_call" | custom-call | flops 4294967296 | bytes 4194304 | tf_op jit(solution)/shard_map/decode/pallas_call | solution.py:86
  107.7 3.4 %arrange.3.refs_1_.refs_21_ = bf16[8,384,256]{2,1,0:T(8,128)(2,1)} custom-call(s32[8]{0:T(128)} %iota_xor_fusion.order.places, bf16[1,384,256]{2,1,0:T(8,128)(2,1)} %copy-done.17, bf16[1,384,256]{2,1,0:T(8,128)(2,1)} %copy-done.18, bf16[1,384,256]{2,1,0:T(8,128)(2,1)} %copy-done.19, bf16[1,384,256]{2,1,0:T(8,128)(2,1)} %copy-done.20, ...), custom_call_target="tpu_custom_call" | custom-call | bytes 6291456 | tf_op jit(solution)/shard_map/arrange/pallas_call | solution.py:43
  111.1 2.4 collective-permute-start.18
  113.5 2.7 %collective-permute-start.19 = (bf16[3,64,1024]{2,1,0:T(8,128)(2,1)S(1)}, bf16[3,64,1024]{2,1,0:T(8,128)(2,1)S(1)}, u32[]{:S(2)}, u32[]{:S(2)}) collective-permute-start(bf16[3,64,1024]{2,1,0:T(8,128)(2,1)S(1)} %pad_maximum_fusion.refs_8_), channel_id=1, source_target_pairs={{0,24},{4,28},{8,16},{12,20},{16,8},{20,12},{24,0},{28,4},{1,25},{... | collective-permute-start | bytes 1179656 | tf_op jit(solution)/shard_map/ppermute | solution.py:446
  118.4 8.2 %decode.5.refs_18_ = bf16[1024,2048]{1,0:T(8,128)(2,1)} custom-call(bf16[8,16,2048]{2,1,0:T(8,128)(2,1)} %copy-done.44, bf16[8,384,256]{2,1,0:T(8,128)(2,1)} %arrange.3.refs_1_.refs_21_), custom_call_target="tpu_custom_call" | custom-call | flops 4294967296 | bytes 4194304 | tf_op jit(solution)/shard_map/decode/pallas_call | solution.py:86
  126.6 5.1 %collective-permute-done.18.refs_10_ = bf16[3,64,1024]{2,1,0:T(8,128)(2,1)S(1)} collective-permute-done((bf16[3,64,1024]{2,1,0:T(8,128)(2,1)S(1)}, bf16[3,64,1024]{2,1,0:T(8,128)(2,1)S(1)}, u32[]{:S(2)}, u32[]{:S(2)}) %collective-permute-start.18) | collective-permute-done | bytes 393248 | tf_op jit(solution)/shard_map/ppermute | solution.py:446
  132.3 8.1 %decode.4.refs_17_ = bf16[1024,2048]{1,0:T(8,128)(2,1)} custom-call(bf16[8,16,2048]{2,1,0:T(8,128)(2,1)} %copy-done.46, bf16[8,384,256]{2,1,0:T(8,128)(2,1)} %arrange.3.refs_1_.refs_21_), custom_call_target="tpu_custom_call" | custom-call | flops 4294967296 | bytes 4194304 | tf_op jit(solution)/shard_map/decode/pallas_call | solution.py:86
  142.1 16.5 %scores.1 = (f32[512,2048]{1,0:T(8,128)}, f32[8,512]{1,0:T(8,128)}, bf16[512,1024]{1,0:T(8,128)(2,1)}) custom-call(bf16[64,1024]{1,0:T(8,128)(2,1)} %copy-done.32, bf16[64,1024]{1,0:T(8,128)(2,1)} %collective-permute-done.7.refs_1_, bf16[64,1024]{1,0:T(8,128)(2,1)} %collective-permute-done.8.refs_2_, bf16[64,1024]{1,0:T(8,128)(2,1)} %collective-permute-done.9.refs_3_, ...), custom_call_target="tpu_custom_call" | custom-call | flops 8589934592 | bytes 16777216 | tf_op jit(solution)/shard_map/scores/pallas_call | solution.py:188
  158.7 3.0 %collective-permute-start.38 = (f32[8,512]{1,0:T(8,128)}, f32[8,512]{1,0:T(8,128)S(1)}, u32[]{:S(2)}, u32[]{:S(2)}) collective-permute-start(f32[8,512]{1,0:T(8,128)} %get-tuple-element.25.refs_0_), channel_id=1, source_target_pairs={{0,8},{4,12},{8,0},{12,4},{16,24},{20,28},{24,16},{28,20},{1,9},{5... | collective-permute-start | bytes 49160 | tf_op jit(solution)/shard_map/ppermute | solution.py:446
  163.8 1.9 collective-permute-done.39.refs_2_
  168.7 6.6 %score_grads.1 = (bf16[512,2048]{1,0:T(8,128)(2,1)}, f32[4,64,1024]{2,1,0:T(8,128)}, f32[4,64,1024]{2,1,0:T(8,128)}, f32[8,512]{1,0:T(8,128)}) custom-call(f32[8,512]{1,0:T(8,128)} %get-tuple-element.25.refs_0_, f32[8,512]{1,0:T(8,128)} %copy-done.37, f32[8,512]{1,0:T(8,128)} %copy-done.38, f32[8,512]{1,0:T(8,128)} %copy-done.39, f32[8,512]{1,0:T(8,128)} %copy-done.40, ...), custom_call_target="tpu_custom_call" | custom-call | flops 2147483648 | bytes 6291456 | tf_op jit(solution)/shard_map/score_grads/pallas_call | solution.py:268
  181.3 1.7 collective-permute-start.48
  183.0 6.3 %multiply_convert_fusion.grads = bf16[1024,2048]{1,0:T(8,128)(2,1)} fusion(bf16[512,1024]{1,0:T(8,128)(2,1)} %get-tuple-element.34, bf16[512,2048]{1,0:T(8,128)(2,1)} %get-tuple-element.36), kind=kOutput, calls=%fused_computation.1 | convolution fusion | flops 2151677952 | bytes 7340032 | tf_op jit(solution)/shard_map/dot_general | solution.py:535
  189.3 5.1 %book_grads.4 = f32[32,8,256]{2,1,0:T(8,128)} custom-call(s32[2]{0:T(128)} %get-tuple-element.51.order, bf16[1024,2048]{1,0:T(8,128)(2,1)} %multiply_convert_fusion.grads, bf16[8,16,2048]{2,1,0:T(8,128)(2,1)} %bitcast.113), custom_call_target="tpu_custom_call" | custom-call | flops 1073741824 | bytes 1048576 | tf_op jit(solution)/shard_map/book_grads/pallas_call | solution.py:333
  194.4 7.9 %book_grads.5 = f32[64,8,256]{2,1,0:T(8,128)} custom-call(s32[4]{0:T(128)} %pad_add_fusion.order, bf16[1024,2048]{1,0:T(8,128)(2,1)} %multiply_convert_fusion.grads, bf16[8,16,2048]{2,1,0:T(8,128)(2,1)} %bitcast.114), custom_call_target="tpu_custom_call" | custom-call | flops 2147483648 | bytes 2097152 | tf_op jit(solution)/shard_map/book_grads/pallas_call | solution.py:333
  202.3 5.3 %book_grads.3 = f32[32,8,256]{2,1,0:T(8,128)} custom-call(s32[2]{0:T(128)} %get-tuple-element.49.order, bf16[1024,2048]{1,0:T(8,128)(2,1)} %multiply_convert_fusion.grads, bf16[8,16,2048]{2,1,0:T(8,128)(2,1)} %bitcast.115), custom_call_target="tpu_custom_call" | custom-call | flops 1073741824 | bytes 1048576 | tf_op jit(solution)/shard_map/book_grads/pallas_call | solution.py:333
  211.3 1.7 collective-permute-start.51
  216.5 3.2 %collective-permute-done.51.refs_3_ = bf16[64,1024]{1,0:T(8,128)(2,1)S(1)} collective-permute-done((bf16[64,1024]{1,0:T(8,128)(2,1)S(1)}, bf16[64,1024]{1,0:T(8,128)(2,1)S(1)}, u32[]{:S(2)}, u32[]{:S(2)}) %collective-permute-start.51) | collective-permute-done | bytes 131104 | tf_op jit(solution)/shard_map/ppermute | solution.py:446
  224.4 4.1 %back_part.1 = (bf16[128,512]{1,0:T(8,128)(2,1)}, bf16[128,512]{1,0:T(8,128)(2,1)}, bf16[128,512]{1,0:T(8,128)(2,1)}, bf16[128,512]{1,0:T(8,128)(2,1)}, bf16[512,1024]{1,0:T(8,128)(2,1)}) custom-call(s32[8]{0:T(128)} %fusion.32.order, bf16[64,1024]{1,0:T(8,128)(2,1)} %copy-done.14, bf16[64,1024]{1,0:T(8,128)(2,1)} %copy-done.25, ...), custom_call_target="tpu_custom_call" | custom-call | flops 536870912 | bytes 2097152 | tf_op jit(solution)/shard_map/back_part/pallas_call | solution.py:373
  228.6 2.1 collective-permute-start.56
  231.5 1.5 collective-permute-start.58
  233.1 3.0 %collective-permute-done.56 = bf16[128,512]{1,0:T(8,128)(2,1)S(1)} collective-permute-done((bf16[128,512]{1,0:T(8,128)(2,1)}, bf16[128,512]{1,0:T(8,128)(2,1)S(1)}, u32[]{:S(2)}, u32[]{:S(2)}) %collective-permute-start.56) | collective-permute-done | bytes 131104 | tf_op jit(solution)/shard_map/ppermute | solution.py:449
  236.1 7.7 %collective-permute-done.57 = bf16[128,512]{1,0:T(8,128)(2,1)S(1)} collective-permute-done((bf16[128,512]{1,0:T(8,128)(2,1)}, bf16[128,512]{1,0:T(8,128)(2,1)S(1)}, u32[]{:S(2)}, u32[]{:S(2)}) %collective-permute-start.57) | collective-permute-done | bytes 131104 | tf_op jit(solution)/shard_map/ppermute | solution.py:449
  244.8 1.8 collective-permute-start.64
  246.9 1.4 collective-permute-start.66
  248.9 2.8 %collective-permute-done.64.refs_1_.refs_9_ = bf16[128,768]{1,0:T(8,128)(2,1)S(1)} collective-permute-done((bf16[128,768]{1,0:T(8,128)(2,1)S(1)}, bf16[128,768]{1,0:T(8,128)(2,1)S(1)}, u32[]{:S(2)}, u32[]{:S(2)}) %collective-permute-start.64) | collective-permute-done | bytes 196640 | tf_op jit(solution)/shard_map/ppermute | solution.py:446
  251.6 3.0 %collective-permute-done.65.refs_2_.refs_10_ = bf16[128,768]{1,0:T(8,128)(2,1)S(1)} collective-permute-done((bf16[128,768]{1,0:T(8,128)(2,1)S(1)}, bf16[128,768]{1,0:T(8,128)(2,1)S(1)}, u32[]{:S(2)}, u32[]{:S(2)}) %collective-permute-start.65) | collective-permute-done | bytes 196640 | tf_op jit(solution)/shard_map/ppermute | solution.py:446
  255.2 3.3 %fusion.40 = f32[512,1024]{1,0:T(8,128)} fusion(bf16[512,512]{1,0:T(8,128)(2,1)S(1)} %bitcast.109, bf16[512,1024]{1,0:T(8,128)(2,1)} %get-tuple-element.38), kind=kOutput, calls=%fused_computation.90 | convolution fusion | flops 536870912 | bytes 3670016 | tf_op jit(solution)/shard_map/dot_general | solution.py:566
  259.3 4.9 %tail.1 = (bf16[128,4096]{1,0:T(8,128)(2,1)}, f32[8,128,256]{2,1,0:T(8,128)}) custom-call(s32[8]{0:T(128)} %fusion.36.order, s32[8]{0:T(128)} %iota_xor_fusion.order.places, bf16[128,768]{1,0:T(8,128)(2,1)} %copy-done.4, bf16[128,768]{1,0:T(8,128)(2,1)} %copy-done.6, bf16[128,768]{1,0:T(8,128)(2,1)} %copy-done.7, bf16[128,768]{1,0:T(8,128)(2,1)} %copy-done.8, ...), custom_call_target="tpu_custom_call" | custom-call | flops 4194304 | bytes 4194304 | tf_op jit(solution)/shard_map/tail/pallas_call | solution.py:420
  (258 shorter events, 51.8 us)
Async XLA Ops:
  4.0 9.8 %collective-permute-start = (bf16[128,512]{1,0:T(8,128)(2,1)S(1)}, bf16[128,512]{1,0:T(8,128)(2,1)S(1)}, u32[]{:S(2)}, u32[]{:S(2)}) collective-permute-start(bf16[128,512]{1,0:T(8,128)(2,1)S(1)} %multiply_convert_fusion.1), channel_id=1, source_target_pairs={{0,1},{1,0},{2,3},{3,2},{4,5},{5,4},{6,7},{7,6},{8,9},{9,8},{10,11... | collective-permute-start | bytes 393224 | tf_op jit(solution)/shard_map/ppermute | solution.py:449
  7.2 12.9 %collective-permute-start.1 = (bf16[128,512]{1,0:T(8,128)(2,1)S(1)}, bf16[128,512]{1,0:T(8,128)(2,1)S(1)}, u32[]{:S(2)}, u32[]{:S(2)}) collective-permute-start(bf16[128,512]{1,0:T(8,128)(2,1)S(1)} %multiply_convert_fusion.1), channel_id=1, source_target_pairs={{0,2},{1,3},{2,0},{3,1},{4,6},{5,7},{6,4},{7,5},{8,10},{9,11},{10,... | collective-permute-start | bytes 393224 | tf_op jit(solution)/shard_map/ppermute | solution.py:449
  9.8 10.3 %collective-permute-start.2 = (bf16[128,512]{1,0:T(8,128)(2,1)S(1)}, bf16[128,512]{1,0:T(8,128)(2,1)S(1)}, u32[]{:S(2)}, u32[]{:S(2)}) collective-permute-start(bf16[128,512]{1,0:T(8,128)(2,1)S(1)} %multiply_convert_fusion.1), channel_id=1, source_target_pairs={{0,3},{1,2},{2,1},{3,0},{4,7},{5,6},{6,5},{7,4},{8,11},{9,10},{10,... | collective-permute-start | bytes 393224 | tf_op jit(solution)/shard_map/ppermute | solution.py:449
  24.7 15.8 %collective-permute-start.3 = (f32[4,64,1024]{2,1,0:T(8,128)S(1)}, f32[4,64,1024]{2,1,0:T(8,128)}, u32[]{:S(2)}, u32[]{:S(2)}) collective-permute-start(f32[4,64,1024]{2,1,0:T(8,128)S(1)} %fusion), channel_id=1, source_target_pairs={{0,4},{4,0},{8,12},{12,8},{16,20},{20,16},{24,28},{28,24},{1,5},{5... | collective-permute-start | bytes 3145736 | tf_op jit(solution)/shard_map/ppermute | solution.py:443
  27.6 8.4 %collective-permute-start.26 = (bf16[1,128,256]{2,1,0:T(8,128)(2,1)S(1)}, bf16[1,128,256]{2,1,0:T(8,128)(2,1)S(1)}, u32[]{:S(2)}, u32[]{:S(2)}) collective-permute-start(bf16[1,128,256]{2,1,0:T(8,128)(2,1)S(1)} %constant_dynamic-slice_fusion.1), channel_id=1, source_target_pairs={{0,2},{1,3},{2,0},{3,1},{4,6},{5,7},{6,4},{7,5},{8,10},{9,11},{10,... | collective-permute-start | bytes 196616 | tf_op jit(solution)/shard_map/ppermute | solution.py:449
  28.6 7.4 %collective-permute-start.27 = (bf16[1,128,256]{2,1,0:T(8,128)(2,1)S(1)}, bf16[1,128,256]{2,1,0:T(8,128)(2,1)S(1)}, u32[]{:S(2)}, u32[]{:S(2)}) collective-permute-start(bf16[1,128,256]{2,1,0:T(8,128)(2,1)S(1)} %constant_dynamic-slice_fusion.1), channel_id=1, source_target_pairs={{0,3},{1,2},{2,1},{3,0},{4,7},{5,6},{6,5},{7,4},{8,11},{9,10},{10,... | collective-permute-start | bytes 196616 | tf_op jit(solution)/shard_map/ppermute | solution.py:449
  36.1 9.2 %collective-permute-start.28 = (bf16[1,384,256]{2,1,0:T(8,128)(2,1)S(1)}, bf16[1,384,256]{2,1,0:T(8,128)(2,1)S(1)}, u32[]{:S(2)}, u32[]{:S(2)}) collective-permute-start(bf16[1,384,256]{2,1,0:T(8,128)(2,1)S(1)} %constant_dynamic-update-slice_fusion.refs_0_), channel_id=1, source_target_pairs={{0,8},{4,12},{8,0},{12,4},{16,24},{20,28},{24,16},{28,20},{1,9},{5... | collective-permute-start | bytes 589832 | tf_op jit(solution)/shard_map/ppermute | solution.py:446
  37.6 8.2 %collective-permute-start.29 = (bf16[1,384,256]{2,1,0:T(8,128)(2,1)S(1)}, bf16[1,384,256]{2,1,0:T(8,128)(2,1)S(1)}, u32[]{:S(2)}, u32[]{:S(2)}) collective-permute-start(bf16[1,384,256]{2,1,0:T(8,128)(2,1)S(1)} %constant_dynamic-update-slice_fusion.refs_0_), channel_id=1, source_target_pairs={{0,16},{4,20},{8,24},{12,28},{16,0},{20,4},{24,8},{28,12},{1,17},{... | collective-permute-start | bytes 589832 | tf_op jit(solution)/shard_map/ppermute | solution.py:446
  41.7 19.9 %collective-permute-start.4 = (f32[64,1024]{1,0:T(8,128)S(1)}, f32[64,1024]{1,0:T(8,128)S(1)}, u32[]{:S(2)}, u32[]{:S(2)}) collective-permute-start(f32[64,1024]{1,0:T(8,128)S(1)} %get-tuple-element.43), channel_id=1, source_target_pairs={{0,8},{4,12},{8,0},{12,4},{16,24},{20,28},{24,16},{28,20},{1,9},{5... | collective-permute-start | bytes 786440 | tf_op jit(solution)/shard_map/ppermute | solution.py:446
  42.3 19.4 %collective-permute-start.5 = (f32[64,1024]{1,0:T(8,128)S(1)}, f32[64,1024]{1,0:T(8,128)S(1)}, u32[]{:S(2)}, u32[]{:S(2)}) collective-permute-start(f32[64,1024]{1,0:T(8,128)S(1)} %get-tuple-element.45), channel_id=1, source_target_pairs={{0,16},{4,20},{8,24},{12,28},{16,0},{20,4},{24,8},{28,12},{1,17},{... | collective-permute-start | bytes 786440 | tf_op jit(solution)/shard_map/ppermute | solution.py:446
  42.9 19.3 %collective-permute-start.6 = (f32[64,1024]{1,0:T(8,128)S(1)}, f32[64,1024]{1,0:T(8,128)S(1)}, u32[]{:S(2)}, u32[]{:S(2)}) collective-permute-start(f32[64,1024]{1,0:T(8,128)S(1)} %get-tuple-element.44), channel_id=1, source_target_pairs={{0,24},{4,28},{8,16},{12,20},{16,8},{20,12},{24,0},{28,4},{1,25},{... | collective-permute-start | bytes 786440 | tf_op jit(solution)/shard_map/ppermute | solution.py:446
  45.3 13.1 %collective-permute-start.30 = (bf16[1,384,256]{2,1,0:T(8,128)(2,1)S(1)}, bf16[1,384,256]{2,1,0:T(8,128)(2,1)S(1)}, u32[]{:S(2)}, u32[]{:S(2)}) collective-permute-start(bf16[1,384,256]{2,1,0:T(8,128)(2,1)S(1)} %constant_dynamic-update-slice_fusion.refs_0_), channel_id=1, source_target_pairs={{0,24},{4,28},{8,16},{12,20},{16,8},{20,12},{24,0},{28,4},{1,25},{... | collective-permute-start | bytes 589832 | tf_op jit(solution)/shard_map/ppermute | solution.py:446
  45.8 15.7 %collective-permute-start.31 = (bf16[1,384,256]{2,1,0:T(8,128)(2,1)S(1)}, bf16[1,384,256]{2,1,0:T(8,128)(2,1)S(1)}, u32[]{:S(2)}, u32[]{:S(2)}) collective-permute-start(bf16[1,384,256]{2,1,0:T(8,128)(2,1)S(1)} %constant_dynamic-update-slice_fusion.refs_0_), channel_id=1, source_target_pairs={{0,4},{4,0},{8,12},{12,8},{16,20},{20,16},{24,28},{28,24},{1,5},{5... | collective-permute-start | bytes 589832 | tf_op jit(solution)/shard_map/ppermute | solution.py:443
  58.4 35.9 %collective-permute-start.35 = (bf16[8,16,2048]{2,1,0:T(8,128)(2,1)S(1)}, bf16[8,16,2048]{2,1,0:T(8,128)(2,1)S(1)}, u32[]{:S(2)}, u32[]{:S(2)}) collective-permute-start(bf16[8,16,2048]{2,1,0:T(8,128)(2,1)S(1)} %bitcast.110), channel_id=1, source_target_pairs={{0,2},{1,3},{2,0},{3,1},{4,6},{5,7},{6,4},{7,5},{8,10},{9,11},{10,... | collective-permute-start | bytes 1572872 | tf_op jit(solution)/shard_map/ppermute | solution.py:449
  61.5 32.9 %collective-permute-start.24 = (bf16[8,16,2048]{2,1,0:T(8,128)(2,1)S(1)}, bf16[8,16,2048]{2,1,0:T(8,128)(2,1)S(1)}, u32[]{:S(2)}, u32[]{:S(2)}) collective-permute-start(bf16[8,16,2048]{2,1,0:T(8,128)(2,1)S(1)} %bitcast.111), channel_id=1, source_target_pairs={{0,1},{1,0},{2,3},{3,2},{4,5},{5,4},{6,7},{7,6},{8,9},{9,8},{10,11... | collective-permute-start | bytes 1572872 | tf_op jit(solution)/shard_map/ppermute | solution.py:449
  63.4 27.2 %collective-permute-start.14 = (bf16[64,1024]{1,0:T(8,128)(2,1)S(1)}, bf16[64,1024]{1,0:T(8,128)(2,1)S(1)}, u32[]{:S(2)}, u32[]{:S(2)}) collective-permute-start(bf16[64,1024]{1,0:T(8,128)(2,1)S(1)} %fusion.19.refs_0_), channel_id=1, source_target_pairs={{0,1},{1,0},{2,3},{3,2},{4,5},{5,4},{6,7},{7,6},{8,9},{9,8},{10,11... | collective-permute-start | bytes 393224 | tf_op jit(solution)/shard_map/ppermute | solution.py:449
  65.4 26.7 %collective-permute-start.15 = (bf16[64,1024]{1,0:T(8,128)(2,1)S(1)}, bf16[64,1024]{1,0:T(8,128)(2,1)S(1)}, u32[]{:S(2)}, u32[]{:S(2)}) collective-permute-start(bf16[64,1024]{1,0:T(8,128)(2,1)S(1)} %fusion.19.refs_0_), channel_id=1, source_target_pairs={{0,2},{1,3},{2,0},{3,1},{4,6},{5,7},{6,4},{7,5},{8,10},{9,11},{10,... | collective-permute-start | bytes 393224 | tf_op jit(solution)/shard_map/ppermute | solution.py:449
  65.5 27.4 %collective-permute-start.16 = (bf16[64,1024]{1,0:T(8,128)(2,1)S(1)}, bf16[64,1024]{1,0:T(8,128)(2,1)S(1)}, u32[]{:S(2)}, u32[]{:S(2)}) collective-permute-start(bf16[64,1024]{1,0:T(8,128)(2,1)S(1)} %fusion.19.refs_0_), channel_id=1, source_target_pairs={{0,3},{1,2},{2,1},{3,0},{4,7},{5,6},{6,5},{7,4},{8,11},{9,10},{10,... | collective-permute-start | bytes 393224 | tf_op jit(solution)/shard_map/ppermute | solution.py:449
  94.4 16.8 %collective-permute-start.10 = (bf16[64,1024]{1,0:T(8,128)(2,1)S(1)}, bf16[64,1024]{1,0:T(8,128)(2,1)S(1)}, u32[]{:S(2)}, u32[]{:S(2)}) collective-permute-start(bf16[64,1024]{1,0:T(8,128)(2,1)S(1)} %fusion.19.refs_0_), channel_id=1, source_target_pairs={{0,4},{4,0},{8,12},{12,8},{16,20},{20,16},{24,28},{28,24},{1,5},{5... | collective-permute-start | bytes 393224 | tf_op jit(solution)/shard_map/ppermute | solution.py:443
  94.5 23.1 %collective-permute-start.17 = (bf16[3,64,1024]{2,1,0:T(8,128)(2,1)S(1)}, bf16[3,64,1024]{2,1,0:T(8,128)(2,1)}, u32[]{:S(2)}, u32[]{:S(2)}) collective-permute-start(bf16[3,64,1024]{2,1,0:T(8,128)(2,1)S(1)} %pad_maximum_fusion.refs_8_), channel_id=1, source_target_pairs={{0,8},{4,12},{8,0},{12,4},{16,24},{20,28},{24,16},{28,20},{1,9},{5... | collective-permute-start | bytes 1179656 | tf_op jit(solution)/shard_map/ppermute | solution.py:446
  96.7 16.8 %collective-permute-start.11 = (bf16[64,1024]{1,0:T(8,128)(2,1)}, bf16[64,1024]{1,0:T(8,128)(2,1)S(1)}, u32[]{:S(2)}, u32[]{:S(2)}) collective-permute-start(bf16[64,1024]{1,0:T(8,128)(2,1)} %collective-permute-done.7.refs_1_), channel_id=1, source_target_pairs={{0,4},{4,0},{8,12},{12,8},{16,20},{20,16},{24,28},{28,24},{1,5},{5... | collective-permute-start | bytes 393224 | tf_op jit(solution)/shard_map/ppermute | solution.py:443
  97.2 19.0 %collective-permute-start.12 = (bf16[64,1024]{1,0:T(8,128)(2,1)}, bf16[64,1024]{1,0:T(8,128)(2,1)}, u32[]{:S(2)}, u32[]{:S(2)}) collective-permute-start(bf16[64,1024]{1,0:T(8,128)(2,1)} %collective-permute-done.8.refs_2_), channel_id=1, source_target_pairs={{0,4},{4,0},{8,12},{12,8},{16,20},{20,16},{24,28},{28,24},{1,5},{5... | collective-permute-start | bytes 393224 | tf_op jit(solution)/shard_map/ppermute | solution.py:443
  98.9 17.4 %collective-permute-start.13 = (bf16[64,1024]{1,0:T(8,128)(2,1)}, bf16[64,1024]{1,0:T(8,128)(2,1)}, u32[]{:S(2)}, u32[]{:S(2)}) collective-permute-start(bf16[64,1024]{1,0:T(8,128)(2,1)} %collective-permute-done.9.refs_3_), channel_id=1, source_target_pairs={{0,4},{4,0},{8,12},{12,8},{16,20},{20,16},{24,28},{28,24},{1,5},{5... | collective-permute-start | bytes 393224 | tf_op jit(solution)/shard_map/ppermute | solution.py:443
  111.1 20.6 %collective-permute-start.18 = (bf16[3,64,1024]{2,1,0:T(8,128)(2,1)S(1)}, bf16[3,64,1024]{2,1,0:T(8,128)(2,1)S(1)}, u32[]{:S(2)}, u32[]{:S(2)}) collective-permute-start(bf16[3,64,1024]{2,1,0:T(8,128)(2,1)S(1)} %pad_maximum_fusion.refs_8_), channel_id=1, source_target_pairs={{0,16},{4,20},{8,24},{12,28},{16,0},{20,4},{24,8},{28,12},{1,17},{... | collective-permute-start | bytes 1179656 | tf_op jit(solution)/shard_map/ppermute | solution.py:446
  113.5 18.2 %collective-permute-start.19 = (bf16[3,64,1024]{2,1,0:T(8,128)(2,1)S(1)}, bf16[3,64,1024]{2,1,0:T(8,128)(2,1)S(1)}, u32[]{:S(2)}, u32[]{:S(2)}) collective-permute-start(bf16[3,64,1024]{2,1,0:T(8,128)(2,1)S(1)} %pad_maximum_fusion.refs_8_), channel_id=1, source_target_pairs={{0,24},{4,28},{8,16},{12,20},{16,8},{20,12},{24,0},{28,4},{1,25},{... | collective-permute-start | bytes 1179656 | tf_op jit(solution)/shard_map/ppermute | solution.py:446
  116.2 16.0 %collective-permute-start.20 = (bf16[3,64,1024]{2,1,0:T(8,128)(2,1)S(1)}, bf16[3,64,1024]{2,1,0:T(8,128)(2,1)}, u32[]{:S(2)}, u32[]{:S(2)}) collective-permute-start(bf16[3,64,1024]{2,1,0:T(8,128)(2,1)S(1)} %pad_maximum_fusion.refs_8_), channel_id=1, source_target_pairs={{0,4},{4,0},{8,12},{12,8},{16,20},{20,16},{24,28},{28,24},{1,5},{5... | collective-permute-start | bytes 1179656 | tf_op jit(solution)/shard_map/ppermute | solution.py:443
  116.2 24.2 %collective-permute-start.37 = (bf16[8,16,2048]{2,1,0:T(8,128)(2,1)S(1)}, bf16[8,16,2048]{2,1,0:T(8,128)(2,1)S(1)}, u32[]{:S(2)}, u32[]{:S(2)}) collective-permute-start(bf16[8,16,2048]{2,1,0:T(8,128)(2,1)S(1)} %copy-done.45), channel_id=1, source_target_pairs={{1,0},{2,3},{5,4},{6,7},{9,8},{10,11},{13,12},{14,15},{17,16},{18,... | collective-permute-start | bytes 1572872 | tf_op jit(solution)/shard_map/ppermute | solution.py:510
  117.6 22.9 %collective-permute-start.36 = (bf16[8,16,2048]{2,1,0:T(8,128)(2,1)S(1)}, bf16[8,16,2048]{2,1,0:T(8,128)(2,1)S(1)}, u32[]{:S(2)}, u32[]{:S(2)}) collective-permute-start(bf16[8,16,2048]{2,1,0:T(8,128)(2,1)S(1)} %bitcast.116), channel_id=1, source_target_pairs={{1,2},{2,1},{5,6},{6,5},{9,10},{10,9},{13,14},{14,13},{17,18},{18,... | collective-permute-start | bytes 1572872 | tf_op jit(solution)/shard_map/ppermute | solution.py:510
  131.7 8.8 %collective-permute-start.21 = (bf16[3,64,1024]{2,1,0:T(8,128)(2,1)}, bf16[3,64,1024]{2,1,0:T(8,128)(2,1)}, u32[]{:S(2)}, u32[]{:S(2)}) collective-permute-start(bf16[3,64,1024]{2,1,0:T(8,128)(2,1)} %collective-permute-done.17.refs_9_), channel_id=1, source_target_pairs={{0,4},{4,0},{8,12},{12,8},{16,20},{20,16},{24,28},{28,24},{1,5},{5... | collective-permute-start | bytes 1179656 | tf_op jit(solution)/shard_map/ppermute | solution.py:443
  131.7 8.8 %collective-permute-start.22 = (bf16[3,64,1024]{2,1,0:T(8,128)(2,1)S(1)}, bf16[3,64,1024]{2,1,0:T(8,128)(2,1)}, u32[]{:S(2)}, u32[]{:S(2)}) collective-permute-start(bf16[3,64,1024]{2,1,0:T(8,128)(2,1)S(1)} %collective-permute-done.18.refs_10_), channel_id=1, source_target_pairs={{0,4},{4,0},{8,12},{12,8},{16,20},{20,16},{24,28},{28,24},{1,5},{5... | collective-permute-start | bytes 1179656 | tf_op jit(solution)/shard_map/ppermute | solution.py:443
  132.2 8.3 %collective-permute-start.23 = (bf16[3,64,1024]{2,1,0:T(8,128)(2,1)S(1)}, bf16[3,64,1024]{2,1,0:T(8,128)(2,1)S(1)}, u32[]{:S(2)}, u32[]{:S(2)}) collective-permute-start(bf16[3,64,1024]{2,1,0:T(8,128)(2,1)S(1)} %collective-permute-done.19.refs_11_), channel_id=1, source_target_pairs={{0,4},{4,0},{8,12},{12,8},{16,20},{20,16},{24,28},{28,24},{1,5},{5... | collective-permute-start | bytes 1179656 | tf_op jit(solution)/shard_map/ppermute | solution.py:443
  179.4 28.8 %collective-permute-start.46 = (f32[64,1024]{1,0:T(8,128)S(1)}, f32[64,1024]{1,0:T(8,128)}, u32[]{:S(2)}, u32[]{:S(2)}) collective-permute-start(f32[64,1024]{1,0:T(8,128)S(1)} %get-tuple-element.40), channel_id=1, source_target_pairs={{0,8},{4,12},{8,0},{12,4},{16,24},{20,28},{24,16},{28,20},{1,9},{5... | collective-permute-start | bytes 786440 | tf_op jit(solution)/shard_map/ppermute | solution.py:446
  180.0 28.2 %collective-permute-start.47 = (f32[64,1024]{1,0:T(8,128)S(1)}, f32[64,1024]{1,0:T(8,128)}, u32[]{:S(2)}, u32[]{:S(2)}) collective-permute-start(f32[64,1024]{1,0:T(8,128)S(1)} %get-tuple-element.42), channel_id=1, source_target_pairs={{0,16},{4,20},{8,24},{12,28},{16,0},{20,4},{24,8},{28,12},{1,17},{... | collective-permute-start | bytes 786440 | tf_op jit(solution)/shard_map/ppermute | solution.py:446
  181.3 27.0 %collective-permute-start.48 = (f32[64,1024]{1,0:T(8,128)S(1)}, f32[64,1024]{1,0:T(8,128)}, u32[]{:S(2)}, u32[]{:S(2)}) collective-permute-start(f32[64,1024]{1,0:T(8,128)S(1)} %get-tuple-element.41), channel_id=1, source_target_pairs={{0,24},{4,28},{8,16},{12,20},{16,8},{20,12},{24,0},{28,4},{1,25},{... | collective-permute-start | bytes 786440 | tf_op jit(solution)/shard_map/ppermute | solution.py:446
  194.4 18.6 %collective-permute-start.59 = (f32[2,128,256]{2,1,0:T(8,128)}, f32[2,128,256]{2,1,0:T(8,128)S(1)}, u32[]{:S(2)}, u32[]{:S(2)}) collective-permute-start(f32[2,128,256]{2,1,0:T(8,128)} %bitcast.118), channel_id=1, source_target_pairs={{0,4},{4,0},{8,12},{12,8},{16,20},{20,16},{24,28},{28,24},{1,5},{5... | collective-permute-start | bytes 786440 | tf_op jit(solution)/shard_map/ppermute | solution.py:443
  211.3 8.4 %collective-permute-start.51 = (bf16[64,1024]{1,0:T(8,128)(2,1)S(1)}, bf16[64,1024]{1,0:T(8,128)(2,1)S(1)}, u32[]{:S(2)}, u32[]{:S(2)}) collective-permute-start(bf16[64,1024]{1,0:T(8,128)(2,1)S(1)} %fusion.11.refs_0_), channel_id=1, source_target_pairs={{0,24},{4,28},{8,16},{12,20},{16,8},{20,12},{24,0},{28,4},{1,25},{... | collective-permute-start | bytes 393224 | tf_op jit(solution)/shard_map/ppermute | solution.py:446
  213.1 6.7 %collective-permute-start.52 = (bf16[64,1024]{1,0:T(8,128)(2,1)S(1)}, bf16[64,1024]{1,0:T(8,128)(2,1)S(1)}, u32[]{:S(2)}, u32[]{:S(2)}) collective-permute-start(bf16[64,1024]{1,0:T(8,128)(2,1)S(1)} %fusion.11.refs_0_), channel_id=1, source_target_pairs={{0,4},{4,0},{8,12},{12,8},{16,20},{20,16},{24,28},{28,24},{1,5},{5... | collective-permute-start | bytes 393224 | tf_op jit(solution)/shard_map/ppermute | solution.py:443
  214.0 17.5 %collective-permute-start.60 = (bf16[128,256]{1,0:T(8,128)(2,1)S(1)}, bf16[128,256]{1,0:T(8,128)(2,1)S(1)}, u32[]{:S(2)}, u32[]{:S(2)}) collective-permute-start(bf16[128,256]{1,0:T(8,128)(2,1)S(1)} %fusion.25), channel_id=1, source_target_pairs={{0,8},{4,12},{8,0},{12,4},{16,24},{20,28},{24,16},{28,20},{1,9},{5... | collective-permute-start | bytes 196616 | tf_op jit(solution)/shard_map/ppermute | solution.py:446
  219.8 13.3 %collective-permute-start.62 = (bf16[128,256]{1,0:T(8,128)(2,1)S(1)}, bf16[128,256]{1,0:T(8,128)(2,1)S(1)}, u32[]{:S(2)}, u32[]{:S(2)}) collective-permute-start(bf16[128,256]{1,0:T(8,128)(2,1)S(1)} %get-tuple-element.46), channel_id=1, source_target_pairs={{0,16},{4,20},{8,24},{12,28},{16,0},{20,4},{24,8},{28,12},{1,17},{... | collective-permute-start | bytes 196616 | tf_op jit(solution)/shard_map/ppermute | solution.py:446
  220.2 12.8 %collective-permute-start.63 = (bf16[128,256]{1,0:T(8,128)(2,1)S(1)}, bf16[128,256]{1,0:T(8,128)(2,1)S(1)}, u32[]{:S(2)}, u32[]{:S(2)}) collective-permute-start(bf16[128,256]{1,0:T(8,128)(2,1)S(1)} %get-tuple-element.47), channel_id=1, source_target_pairs={{0,24},{4,28},{8,16},{12,20},{16,8},{20,12},{24,0},{28,4},{1,25},{... | collective-permute-start | bytes 196616 | tf_op jit(solution)/shard_map/ppermute | solution.py:446
  228.6 7.5 %collective-permute-start.56 = (bf16[128,512]{1,0:T(8,128)(2,1)}, bf16[128,512]{1,0:T(8,128)(2,1)S(1)}, u32[]{:S(2)}, u32[]{:S(2)}) collective-permute-start(bf16[128,512]{1,0:T(8,128)(2,1)} %get-tuple-element.31), channel_id=1, source_target_pairs={{0,1},{1,0},{2,3},{3,2},{4,5},{5,4},{6,7},{7,6},{8,9},{9,8},{10,11... | collective-permute-start | bytes 393224 | tf_op jit(solution)/shard_map/ppermute | solution.py:449
  230.7 13.1 %collective-permute-start.57 = (bf16[128,512]{1,0:T(8,128)(2,1)}, bf16[128,512]{1,0:T(8,128)(2,1)S(1)}, u32[]{:S(2)}, u32[]{:S(2)}) collective-permute-start(bf16[128,512]{1,0:T(8,128)(2,1)} %get-tuple-element.32), channel_id=1, source_target_pairs={{0,2},{1,3},{2,0},{3,1},{4,6},{5,7},{6,4},{7,5},{8,10},{9,11},{10,... | collective-permute-start | bytes 393224 | tf_op jit(solution)/shard_map/ppermute | solution.py:449
  231.5 12.3 %collective-permute-start.58 = (bf16[128,512]{1,0:T(8,128)(2,1)}, bf16[128,512]{1,0:T(8,128)(2,1)S(1)}, u32[]{:S(2)}, u32[]{:S(2)}) collective-permute-start(bf16[128,512]{1,0:T(8,128)(2,1)} %get-tuple-element.33), channel_id=1, source_target_pairs={{0,3},{1,2},{2,1},{3,0},{4,7},{5,6},{6,5},{7,4},{8,11},{9,10},{10,... | collective-permute-start | bytes 393224 | tf_op jit(solution)/shard_map/ppermute | solution.py:449
  244.8 6.8 %collective-permute-start.64 = (bf16[128,768]{1,0:T(8,128)(2,1)S(1)}, bf16[128,768]{1,0:T(8,128)(2,1)S(1)}, u32[]{:S(2)}, u32[]{:S(2)}) collective-permute-start(bf16[128,768]{1,0:T(8,128)(2,1)S(1)} %pad_maximum_fusion.1.refs_0_.refs_8_), channel_id=1, source_target_pairs={{0,8},{4,12},{8,0},{12,4},{16,24},{20,28},{24,16},{28,20},{1,9},{5... | collective-permute-start | bytes 589832 | tf_op jit(solution)/shard_map/ppermute | solution.py:446
  246.6 8.1 %collective-permute-start.65 = (bf16[128,768]{1,0:T(8,128)(2,1)S(1)}, bf16[128,768]{1,0:T(8,128)(2,1)S(1)}, u32[]{:S(2)}, u32[]{:S(2)}) collective-permute-start(bf16[128,768]{1,0:T(8,128)(2,1)S(1)} %pad_maximum_fusion.1.refs_0_.refs_8_), channel_id=1, source_target_pairs={{0,16},{4,20},{8,24},{12,28},{16,0},{20,4},{24,8},{28,12},{1,17},{... | collective-permute-start | bytes 589832 | tf_op jit(solution)/shard_map/ppermute | solution.py:446
  246.9 7.8 %collective-permute-start.66 = (bf16[128,768]{1,0:T(8,128)(2,1)S(1)}, bf16[128,768]{1,0:T(8,128)(2,1)S(1)}, u32[]{:S(2)}, u32[]{:S(2)}) collective-permute-start(bf16[128,768]{1,0:T(8,128)(2,1)S(1)} %pad_maximum_fusion.1.refs_0_.refs_8_), channel_id=1, source_target_pairs={{0,24},{4,28},{8,16},{12,20},{16,8},{20,12},{24,0},{28,4},{1,25},{... | collective-permute-start | bytes 589832 | tf_op jit(solution)/shard_map/ppermute | solution.py:446
  248.9 9.6 %collective-permute-start.67 = (bf16[128,768]{1,0:T(8,128)(2,1)S(1)}, bf16[128,768]{1,0:T(8,128)(2,1)S(1)}, u32[]{:S(2)}, u32[]{:S(2)}) collective-permute-start(bf16[128,768]{1,0:T(8,128)(2,1)S(1)} %pad_maximum_fusion.1.refs_0_.refs_8_), channel_id=1, source_target_pairs={{0,4},{4,0},{8,12},{12,8},{16,20},{20,16},{24,28},{28,24},{1,5},{5... | collective-permute-start | bytes 589832 | tf_op jit(solution)/shard_map/ppermute | solution.py:443
  251.6 6.8 %collective-permute-start.68 = (bf16[128,768]{1,0:T(8,128)(2,1)S(1)}, bf16[128,768]{1,0:T(8,128)(2,1)S(1)}, u32[]{:S(2)}, u32[]{:S(2)}) collective-permute-start(bf16[128,768]{1,0:T(8,128)(2,1)S(1)} %collective-permute-done.64.refs_1_.refs_9_), channel_id=1, source_target_pairs={{0,4},{4,0},{8,12},{12,8},{16,20},{20,16},{24,28},{28,24},{1,5},{5... | collective-permute-start | bytes 589832 | tf_op jit(solution)/shard_map/ppermute | solution.py:443
  (77 other events, 909.4 us)

commit v6 on v5

--- a/solution.py
+++ b/solution.py
@@ -552,10 +552,10 @@
 
     part = half // 2
     far_book = [core(book_of(swapped[half : half + part]))]
-    both = book_of(jnp.concatenate([swapped[half + part :], swapped[part:half]]))
-    far_book.append(core(both[:part]))
-    near_book = [book_of(swapped[:part]), both[part:]]
-    halves = [near_book[k // part][k % part] + far_book[k // part][k % part] for k in range(half)]
+    both = book_of(jnp.concatenate([swapped[half + part :], swapped[1:half]]))
+    far_book.append(core(both[: half - part]))
+    near_book = [book_of(swapped[:1])[0]] + [both[half - part + k] for k in range(half - 1)]
+    halves = [near_book[k] + far_book[k // part][k % part] for k in range(half)]
     book_sum = halves[0]
     for k in range(1, half):
         book_sum = book_sum + chip(halves[k].astype(bf16), k).astype(f32)

time: 266 us -> 265 us (level)
  waiting for transfers between devices: 83 us -> 79.4 us
    ppermute x27, waiting for transfers between devices: 35 us -> 32.1 us  [chip(): return lax.ppermute(x, 'psg', [(i, i ^ 2 * k) for i in range(shards)])]
    unnamed x110 -> x114, local copies, waits for them, and re-layouts: 5.08 us -> 5.67 us
  transfers between devices with their start and end apart: 71 -> 71, of which waited for: 22 -> 23; matrix products, arithmetic and copies ran while one was open for 9% -> 10% of each run, Pallas kernels for 19% -> 19%
where the time goes in v6:
time: 265 us; the launch traced here: 263 us
  Pallas kernels  80.9 us (31%)
  waiting for transfers between devices  79.4 us (30%)
  starting transfers between devices  62.7 us (24%)
  other arithmetic  13.9 us (5%)
  matrix products  12.4 us (5%)
  local copies, waits for them, and re-layouts  12.2 us (5%)
    ppermute x14, waiting for transfers between devices, turn(): return lax.ppermute(x, 'qry', [(i, i ^ k) for i in range(owners)])  44.7 us
    ppermute x27, starting transfers between devices, chip(): return lax.ppermute(x, 'psg', [(i, i ^ 2 * k) for i in range(shards)])  35.7 us
    ppermute x27, waiting for transfers between devices, chip(): return lax.ppermute(x, 'psg', [(i, i ^ 2 * k) for i in range(shards)])  32.1 us
    pallas_call x3, Pallas kernels, decode(): pl.pallas_call(decode_body, grid=(slices // 2,), in_specs=[pl.BlockSpec((...  24.5 us
    ppermute x14, starting transfers between devices, turn(): return lax.ppermute(x, 'qry', [(i, i ^ k) for i in range(owners)])  22.3 us
    pallas_call x3, Pallas kernels, book_grads(): pl.pallas_call(functools.partial(book_body, 32, 4), grid_spec=pltpu.Prefe...  18.2 us
    pallas_call x1, Pallas kernels, scores_of(): pl.pallas_call(functools.partial(score_body, chunks, blocks, len(codes)),...  16.6 us
    pallas_call x1, Pallas kernels, score_grads(): pl.pallas_call(functools.partial(grad_body, len(stats)), grid=(width // t...  6.61 us
  transfers between devices with their start and end apart: 71, of which 23 were waited for; matrix products, arithmetic and copies ran while one was open for 10% of the time, Pallas kernels for 19%

profile of v6, /device:TPU:0, one launch (start us, length us, event | category | flops | bytes accessed | tf_op | source)
XLA Modules:
  0.0 262.9 jit_solution(5616558064162037778)
XLA Ops:
  0.6 1.6 multiply_reduce_fusion
  4.0 3.1 %collective-permute-start = (bf16[128,512]{1,0:T(8,128)(2,1)S(1)}, bf16[128,512]{1,0:T(8,128)(2,1)S(1)}, u32[]{:S(2)}, u32[]{:S(2)}) collective-permute-start(bf16[128,512]{1,0:T(8,128)(2,1)S(1)} %multiply_convert_fusion.1), channel_id=1, source_target_pairs={{0,1},{1,0},{2,3},{3,2},{4,5},{5,4},{6,7},{7,6},{8,9},{9,8},{10,11... | collective-permute-start | bytes 393224 | tf_op jit(solution)/shard_map/ppermute | solution.py:449
  7.2 2.6 collective-permute-start.1
  13.9 6.2 %collective-permute-done.1 = bf16[128,512]{1,0:T(8,128)(2,1)S(1)} collective-permute-done((bf16[128,512]{1,0:T(8,128)(2,1)S(1)}, bf16[128,512]{1,0:T(8,128)(2,1)S(1)}, u32[]{:S(2)}, u32[]{:S(2)}) %collective-permute-start.1) | collective-permute-done | bytes 131104 | tf_op jit(solution)/shard_map/ppermute | solution.py:449
  20.8 2.6 arrange.2
  25.7 2.0 collective-permute-start.25
  28.6 1.5 collective-permute-start.27
  30.4 5.7 %collective-permute-done.26 = bf16[1,128,256]{2,1,0:T(8,128)(2,1)S(1)} collective-permute-done((bf16[1,128,256]{2,1,0:T(8,128)(2,1)S(1)}, bf16[1,128,256]{2,1,0:T(8,128)(2,1)S(1)}, u32[]{:S(2)}, u32[]{:S(2)}) %collective-permute-start.26) | collective-permute-done | bytes 65568 | tf_op jit(solution)/shard_map/ppermute | solution.py:449
  36.1 1.6 collective-permute-start.28
  37.6 1.5 collective-permute-start.29
  42.9 2.4 collective-permute-start.6
  45.8 12.6 %collective-permute-done.30.refs_3_ = bf16[1,384,256]{2,1,0:T(8,128)(2,1)S(1)} collective-permute-done((bf16[1,384,256]{2,1,0:T(8,128)(2,1)S(1)}, bf16[1,384,256]{2,1,0:T(8,128)(2,1)S(1)}, u32[]{:S(2)}, u32[]{:S(2)}) %collective-permute-start.30) | collective-permute-done | bytes 196640 | tf_op jit(solution)/shard_map/ppermute | solution.py:446
  58.4 3.1 %collective-permute-start.35 = (bf16[8,16,2048]{2,1,0:T(8,128)(2,1)S(1)}, bf16[8,16,2048]{2,1,0:T(8,128)(2,1)S(1)}, u32[]{:S(2)}, u32[]{:S(2)}) collective-permute-start(bf16[8,16,2048]{2,1,0:T(8,128)(2,1)S(1)} %bitcast.109), channel_id=1, source_target_pairs={{0,2},{1,3},{2,0},{3,1},{4,6},{5,7},{6,4},{7,5},{8,10},{9,11},{10,... | collective-permute-start | bytes 1572872 | tf_op jit(solution)/shard_map/ppermute | solution.py:449
  63.4 2.0 collective-permute-start.14
  65.4 2.4 collective-permute-start.16
  67.8 22.8 %collective-permute-done.14 = bf16[64,1024]{1,0:T(8,128)(2,1)S(1)} collective-permute-done((bf16[64,1024]{1,0:T(8,128)(2,1)S(1)}, bf16[64,1024]{1,0:T(8,128)(2,1)S(1)}, u32[]{:S(2)}, u32[]{:S(2)}) %collective-permute-start.14) | collective-permute-done | bytes 131104 | tf_op jit(solution)/shard_map/ppermute | solution.py:449
  90.6 1.5 collective-permute-start.7
  94.5 1.5 collective-permute-start.17
  97.2 1.6 collective-permute-done.9.refs_3_
  98.9 8.2 %decode.3.refs_16_.refs_10_ = bf16[1024,2048]{1,0:T(8,128)(2,1)} custom-call(bf16[8,16,2048]{2,1,0:T(8,128)(2,1)} %bitcast.111, bf16[8,128,256]{2,1,0:T(8,128)(2,1)} %bitcast.128), custom_call_target="tpu_custom_call" | custom-call | flops 4294967296 | bytes 4194304 | tf_op jit(solution)/shard_map/decode/pallas_call | solution.py:86
  107.7 3.4 %arrange.3.refs_1_.refs_21_ = bf16[8,384,256]{2,1,0:T(8,128)(2,1)} custom-call(s32[8]{0:T(128)} %iota_xor_fusion.order.places, bf16[1,384,256]{2,1,0:T(8,128)(2,1)} %copy-done.16, bf16[1,384,256]{2,1,0:T(8,128)(2,1)} %copy-done.17, bf16[1,384,256]{2,1,0:T(8,128)(2,1)} %copy-done.18, bf16[1,384,256]{2,1,0:T(8,128)(2,1)} %copy-done.19, ...), custom_call_target="tpu_custom_call" | custom-call | bytes 6291456 | tf_op jit(solution)/shard_map/arrange/pallas_call | solution.py:43
  111.0 2.4 collective-permute-start.18
  113.4 2.7 %collective-permute-start.19 = (bf16[3,64,1024]{2,1,0:T(8,128)(2,1)S(1)}, bf16[3,64,1024]{2,1,0:T(8,128)(2,1)S(1)}, u32[]{:S(2)}, u32[]{:S(2)}) collective-permute-start(bf16[3,64,1024]{2,1,0:T(8,128)(2,1)S(1)} %pad_maximum_fusion.refs_8_), channel_id=1, source_target_pairs={{0,24},{4,28},{8,16},{12,20},{16,8},{20,12},{24,0},{28,4},{1,25},{... | collective-permute-start | bytes 1179656 | tf_op jit(solution)/shard_map/ppermute | solution.py:446
  119.0 8.2 %decode.5.refs_18_ = bf16[1024,2048]{1,0:T(8,128)(2,1)} custom-call(bf16[8,16,2048]{2,1,0:T(8,128)(2,1)} %copy-done.43, bf16[8,384,256]{2,1,0:T(8,128)(2,1)} %arrange.3.refs_1_.refs_21_), custom_call_target="tpu_custom_call" | custom-call | flops 4294967296 | bytes 4194304 | tf_op jit(solution)/shard_map/decode/pallas_call | solution.py:86
  127.1 4.5 %collective-permute-done.18.refs_10_ = bf16[3,64,1024]{2,1,0:T(8,128)(2,1)S(1)} collective-permute-done((bf16[3,64,1024]{2,1,0:T(8,128)(2,1)S(1)}, bf16[3,64,1024]{2,1,0:T(8,128)(2,1)S(1)}, u32[]{:S(2)}, u32[]{:S(2)}) %collective-permute-start.18) | collective-permute-done | bytes 393248 | tf_op jit(solution)/shard_map/ppermute | solution.py:446
  132.2 8.1 %decode.4.refs_17_ = bf16[1024,2048]{1,0:T(8,128)(2,1)} custom-call(bf16[8,16,2048]{2,1,0:T(8,128)(2,1)} %copy-done.45, bf16[8,384,256]{2,1,0:T(8,128)(2,1)} %arrange.3.refs_1_.refs_21_), custom_call_target="tpu_custom_call" | custom-call | flops 4294967296 | bytes 4194304 | tf_op jit(solution)/shard_map/decode/pallas_call | solution.py:86
  142.0 16.6 %scores.1 = (f32[512,2048]{1,0:T(8,128)}, f32[8,512]{1,0:T(8,128)}, bf16[512,1024]{1,0:T(8,128)(2,1)}) custom-call(bf16[64,1024]{1,0:T(8,128)(2,1)} %copy-done.31, bf16[64,1024]{1,0:T(8,128)(2,1)} %copy-done.51, bf16[64,1024]{1,0:T(8,128)(2,1)} %copy-done.52, bf16[64,1024]{1,0:T(8,128)(2,1)} %copy-done.53, bf16[64,1024]{1,0:T(8,128)(2,1)} %collective-permute-done.10.refs_4_, ...), custom_call_target="tpu_custom_call" | custom-call | flops 8589934592 | bytes 16777216 | tf_op jit(solution)/shard_map/scores/pallas_call | solution.py:188
  158.6 3.0 %collective-permute-start.38 = (f32[8,512]{1,0:T(8,128)}, f32[8,512]{1,0:T(8,128)S(1)}, u32[]{:S(2)}, u32[]{:S(2)}) collective-permute-start(f32[8,512]{1,0:T(8,128)} %get-tuple-element.25.refs_0_), channel_id=1, source_target_pairs={{0,8},{4,12},{8,0},{12,4},{16,24},{20,28},{24,16},{28,20},{1,9},{5... | collective-permute-start | bytes 49160 | tf_op jit(solution)/shard_map/ppermute | solution.py:446
  163.7 1.9 collective-permute-done.39.refs_2_
  168.5 6.6 %score_grads.1 = (bf16[512,2048]{1,0:T(8,128)(2,1)}, f32[4,64,1024]{2,1,0:T(8,128)}, f32[4,64,1024]{2,1,0:T(8,128)}, f32[8,512]{1,0:T(8,128)}) custom-call(f32[8,512]{1,0:T(8,128)} %get-tuple-element.25.refs_0_, f32[8,512]{1,0:T(8,128)} %copy-done.35, f32[8,512]{1,0:T(8,128)} %copy-done.36, f32[8,512]{1,0:T(8,128)} %copy-done.37, f32[8,512]{1,0:T(8,128)} %copy-done.38, ...), custom_call_target="tpu_custom_call" | custom-call | flops 2147483648 | bytes 6291456 | tf_op jit(solution)/shard_map/score_grads/pallas_call | solution.py:268
  181.1 1.7 collective-permute-start.48
  182.8 6.3 %multiply_convert_fusion.grads = bf16[1024,2048]{1,0:T(8,128)(2,1)} fusion(bf16[512,1024]{1,0:T(8,128)(2,1)} %get-tuple-element.34, bf16[512,2048]{1,0:T(8,128)(2,1)} %get-tuple-element.36), kind=kOutput, calls=%fused_computation.1 | convolution fusion | flops 2151677952 | bytes 7340032 | tf_op jit(solution)/shard_map/dot_general | solution.py:535
  189.2 9.3 %book_grads.5 = f32[80,8,256]{2,1,0:T(8,128)} custom-call(s32[5]{0:T(128)} %pad_add_fusion.order, bf16[1024,2048]{1,0:T(8,128)(2,1)} %multiply_convert_fusion.grads, bf16[8,16,2048]{2,1,0:T(8,128)(2,1)} %bitcast.112), custom_call_target="tpu_custom_call" | custom-call | flops 2684354560 | bytes 2621440 | tf_op jit(solution)/shard_map/book_grads/pallas_call | solution.py:333
  199.6 5.1 %book_grads.4 = f32[32,8,256]{2,1,0:T(8,128)} custom-call(s32[2]{0:T(128)} %get-tuple-element.50.order, bf16[1024,2048]{1,0:T(8,128)(2,1)} %multiply_convert_fusion.grads, bf16[8,16,2048]{2,1,0:T(8,128)(2,1)} %bitcast.113), custom_call_target="tpu_custom_call" | custom-call | flops 1073741824 | bytes 1048576 | tf_op jit(solution)/shard_map/book_grads/pallas_call | solution.py:333
  208.3 1.7 collective-permute-start.51
  214.1 1.8 collective-permute-done.51.refs_3_
  217.1 1.7 collective-permute-start.62
  219.5 3.7 %book_grads.3 = f32[16,8,256]{2,1,0:T(8,128)} custom-call(s32[1]{0:T(128)} %bitcast.126, bf16[1024,2048]{1,0:T(8,128)(2,1)} %multiply_convert_fusion.grads, bf16[8,16,2048]{2,1,0:T(8,128)(2,1)} %bitcast.114), custom_call_target="tpu_custom_call" | custom-call | flops 536870912 | bytes 524288 | tf_op jit(solution)/shard_map/book_grads/pallas_call | solution.py:333
  224.6 4.1 %back_part.1 = (bf16[128,512]{1,0:T(8,128)(2,1)}, bf16[128,512]{1,0:T(8,128)(2,1)}, bf16[128,512]{1,0:T(8,128)(2,1)}, bf16[128,512]{1,0:T(8,128)(2,1)}, bf16[512,1024]{1,0:T(8,128)(2,1)}) custom-call(s32[8]{0:T(128)} %fusion.32.order, bf16[64,1024]{1,0:T(8,128)(2,1)} %copy-done.13, bf16[64,1024]{1,0:T(8,128)(2,1)} %copy-done.24, ...), custom_call_target="tpu_custom_call" | custom-call | flops 536870912 | bytes 2097152 | tf_op jit(solution)/shard_map/back_part/pallas_call | solution.py:373
  228.7 2.1 collective-permute-start.56
  231.7 1.5 collective-permute-start.58
  234.2 1.6 collective-permute-done.56
  235.8 7.9 %collective-permute-done.57 = bf16[128,512]{1,0:T(8,128)(2,1)S(1)} collective-permute-done((bf16[128,512]{1,0:T(8,128)(2,1)}, bf16[128,512]{1,0:T(8,128)(2,1)S(1)}, u32[]{:S(2)}, u32[]{:S(2)}) %collective-permute-start.57) | collective-permute-done | bytes 131104 | tf_op jit(solution)/shard_map/ppermute | solution.py:449
  245.5 1.7 collective-permute-start.65
  248.8 2.0 collective-permute-done.64.refs_1_.refs_9_
  250.7 1.8 collective-permute-done.65.refs_2_.refs_10_
  253.7 3.3 %fusion.40 = f32[512,1024]{1,0:T(8,128)} fusion(bf16[512,512]{1,0:T(8,128)(2,1)S(1)} %bitcast.108, bf16[512,1024]{1,0:T(8,128)(2,1)} %get-tuple-element.38), kind=kOutput, calls=%fused_computation.89 | convolution fusion | flops 536870912 | bytes 3670016 | tf_op jit(solution)/shard_map/dot_general | solution.py:566
  258.0 4.9 %tail.1 = (bf16[128,4096]{1,0:T(8,128)(2,1)}, f32[8,128,256]{2,1,0:T(8,128)}) custom-call(s32[8]{0:T(128)} %fusion.36.order, s32[8]{0:T(128)} %iota_xor_fusion.order.places, bf16[128,768]{1,0:T(8,128)(2,1)} %copy-done.4, bf16[128,768]{1,0:T(8,128)(2,1)} %copy-done.5, bf16[128,768]{1,0:T(8,128)(2,1)} %copy-done.6, bf16[128,768]{1,0:T(8,128)(2,1)} %copy-done.7, ...), custom_call_target="tpu_custom_call" | custom-call | flops 4194304 | bytes 4194304 | tf_op jit(solution)/shard_map/tail/pallas_call | solution.py:420
  (262 shorter events, 55.6 us)
Async XLA Ops:
  4.0 9.8 %collective-permute-start = (bf16[128,512]{1,0:T(8,128)(2,1)S(1)}, bf16[128,512]{1,0:T(8,128)(2,1)S(1)}, u32[]{:S(2)}, u32[]{:S(2)}) collective-permute-start(bf16[128,512]{1,0:T(8,128)(2,1)S(1)} %multiply_convert_fusion.1), channel_id=1, source_target_pairs={{0,1},{1,0},{2,3},{3,2},{4,5},{5,4},{6,7},{7,6},{8,9},{9,8},{10,11... | collective-permute-start | bytes 393224 | tf_op jit(solution)/shard_map/ppermute | solution.py:449
  7.2 12.9 %collective-permute-start.1 = (bf16[128,512]{1,0:T(8,128)(2,1)S(1)}, bf16[128,512]{1,0:T(8,128)(2,1)S(1)}, u32[]{:S(2)}, u32[]{:S(2)}) collective-permute-start(bf16[128,512]{1,0:T(8,128)(2,1)S(1)} %multiply_convert_fusion.1), channel_id=1, source_target_pairs={{0,2},{1,3},{2,0},{3,1},{4,6},{5,7},{6,4},{7,5},{8,10},{9,11},{10,... | collective-permute-start | bytes 393224 | tf_op jit(solution)/shard_map/ppermute | solution.py:449
  9.8 10.3 %collective-permute-start.2 = (bf16[128,512]{1,0:T(8,128)(2,1)S(1)}, bf16[128,512]{1,0:T(8,128)(2,1)S(1)}, u32[]{:S(2)}, u32[]{:S(2)}) collective-permute-start(bf16[128,512]{1,0:T(8,128)(2,1)S(1)} %multiply_convert_fusion.1), channel_id=1, source_target_pairs={{0,3},{1,2},{2,1},{3,0},{4,7},{5,6},{6,5},{7,4},{8,11},{9,10},{10,... | collective-permute-start | bytes 393224 | tf_op jit(solution)/shard_map/ppermute | solution.py:449
  24.7 15.8 %collective-permute-start.3 = (f32[4,64,1024]{2,1,0:T(8,128)S(1)}, f32[4,64,1024]{2,1,0:T(8,128)}, u32[]{:S(2)}, u32[]{:S(2)}) collective-permute-start(f32[4,64,1024]{2,1,0:T(8,128)S(1)} %fusion), channel_id=1, source_target_pairs={{0,4},{4,0},{8,12},{12,8},{16,20},{20,16},{24,28},{28,24},{1,5},{5... | collective-permute-start | bytes 3145736 | tf_op jit(solution)/shard_map/ppermute | solution.py:443
  27.6 8.4 %collective-permute-start.26 = (bf16[1,128,256]{2,1,0:T(8,128)(2,1)S(1)}, bf16[1,128,256]{2,1,0:T(8,128)(2,1)S(1)}, u32[]{:S(2)}, u32[]{:S(2)}) collective-permute-start(bf16[1,128,256]{2,1,0:T(8,128)(2,1)S(1)} %constant_dynamic-slice_fusion.1), channel_id=1, source_target_pairs={{0,2},{1,3},{2,0},{3,1},{4,6},{5,7},{6,4},{7,5},{8,10},{9,11},{10,... | collective-permute-start | bytes 196616 | tf_op jit(solution)/shard_map/ppermute | solution.py:449
  28.6 7.4 %collective-permute-start.27 = (bf16[1,128,256]{2,1,0:T(8,128)(2,1)S(1)}, bf16[1,128,256]{2,1,0:T(8,128)(2,1)S(1)}, u32[]{:S(2)}, u32[]{:S(2)}) collective-permute-start(bf16[1,128,256]{2,1,0:T(8,128)(2,1)S(1)} %constant_dynamic-slice_fusion.1), channel_id=1, source_target_pairs={{0,3},{1,2},{2,1},{3,0},{4,7},{5,6},{6,5},{7,4},{8,11},{9,10},{10,... | collective-permute-start | bytes 196616 | tf_op jit(solution)/shard_map/ppermute | solution.py:449
  36.1 9.2 %collective-permute-start.28 = (bf16[1,384,256]{2,1,0:T(8,128)(2,1)S(1)}, bf16[1,384,256]{2,1,0:T(8,128)(2,1)S(1)}, u32[]{:S(2)}, u32[]{:S(2)}) collective-permute-start(bf16[1,384,256]{2,1,0:T(8,128)(2,1)S(1)} %constant_dynamic-update-slice_fusion.refs_0_), channel_id=1, source_target_pairs={{0,8},{4,12},{8,0},{12,4},{16,24},{20,28},{24,16},{28,20},{1,9},{5... | collective-permute-start | bytes 589832 | tf_op jit(solution)/shard_map/ppermute | solution.py:446
  37.6 8.2 %collective-permute-start.29 = (bf16[1,384,256]{2,1,0:T(8,128)(2,1)S(1)}, bf16[1,384,256]{2,1,0:T(8,128)(2,1)S(1)}, u32[]{:S(2)}, u32[]{:S(2)}) collective-permute-start(bf16[1,384,256]{2,1,0:T(8,128)(2,1)S(1)} %constant_dynamic-update-slice_fusion.refs_0_), channel_id=1, source_target_pairs={{0,16},{4,20},{8,24},{12,28},{16,0},{20,4},{24,8},{28,12},{1,17},{... | collective-permute-start | bytes 589832 | tf_op jit(solution)/shard_map/ppermute | solution.py:446
  41.8 19.9 %collective-permute-start.4 = (f32[64,1024]{1,0:T(8,128)S(1)}, f32[64,1024]{1,0:T(8,128)S(1)}, u32[]{:S(2)}, u32[]{:S(2)}) collective-permute-start(f32[64,1024]{1,0:T(8,128)S(1)} %get-tuple-element.43), channel_id=1, source_target_pairs={{0,8},{4,12},{8,0},{12,4},{16,24},{20,28},{24,16},{28,20},{1,9},{5... | collective-permute-start | bytes 786440 | tf_op jit(solution)/shard_map/ppermute | solution.py:446
  42.4 19.4 %collective-permute-start.5 = (f32[64,1024]{1,0:T(8,128)S(1)}, f32[64,1024]{1,0:T(8,128)S(1)}, u32[]{:S(2)}, u32[]{:S(2)}) collective-permute-start(f32[64,1024]{1,0:T(8,128)S(1)} %get-tuple-element.45), channel_id=1, source_target_pairs={{0,16},{4,20},{8,24},{12,28},{16,0},{20,4},{24,8},{28,12},{1,17},{... | collective-permute-start | bytes 786440 | tf_op jit(solution)/shard_map/ppermute | solution.py:446
  42.9 19.3 %collective-permute-start.6 = (f32[64,1024]{1,0:T(8,128)S(1)}, f32[64,1024]{1,0:T(8,128)S(1)}, u32[]{:S(2)}, u32[]{:S(2)}) collective-permute-start(f32[64,1024]{1,0:T(8,128)S(1)} %get-tuple-element.44), channel_id=1, source_target_pairs={{0,24},{4,28},{8,16},{12,20},{16,8},{20,12},{24,0},{28,4},{1,25},{... | collective-permute-start | bytes 786440 | tf_op jit(solution)/shard_map/ppermute | solution.py:446
  45.3 13.1 %collective-permute-start.30 = (bf16[1,384,256]{2,1,0:T(8,128)(2,1)S(1)}, bf16[1,384,256]{2,1,0:T(8,128)(2,1)S(1)}, u32[]{:S(2)}, u32[]{:S(2)}) collective-permute-start(bf16[1,384,256]{2,1,0:T(8,128)(2,1)S(1)} %constant_dynamic-update-slice_fusion.refs_0_), channel_id=1, source_target_pairs={{0,24},{4,28},{8,16},{12,20},{16,8},{20,12},{24,0},{28,4},{1,25},{... | collective-permute-start | bytes 589832 | tf_op jit(solution)/shard_map/ppermute | solution.py:446
  45.8 15.7 %collective-permute-start.31 = (bf16[1,384,256]{2,1,0:T(8,128)(2,1)S(1)}, bf16[1,384,256]{2,1,0:T(8,128)(2,1)S(1)}, u32[]{:S(2)}, u32[]{:S(2)}) collective-permute-start(bf16[1,384,256]{2,1,0:T(8,128)(2,1)S(1)} %constant_dynamic-update-slice_fusion.refs_0_), channel_id=1, source_target_pairs={{0,4},{4,0},{8,12},{12,8},{16,20},{20,16},{24,28},{28,24},{1,5},{5... | collective-permute-start | bytes 589832 | tf_op jit(solution)/shard_map/ppermute | solution.py:443
  58.4 35.9 %collective-permute-start.35 = (bf16[8,16,2048]{2,1,0:T(8,128)(2,1)S(1)}, bf16[8,16,2048]{2,1,0:T(8,128)(2,1)S(1)}, u32[]{:S(2)}, u32[]{:S(2)}) collective-permute-start(bf16[8,16,2048]{2,1,0:T(8,128)(2,1)S(1)} %bitcast.109), channel_id=1, source_target_pairs={{0,2},{1,3},{2,0},{3,1},{4,6},{5,7},{6,4},{7,5},{8,10},{9,11},{10,... | collective-permute-start | bytes 1572872 | tf_op jit(solution)/shard_map/ppermute | solution.py:449
  61.5 32.9 %collective-permute-start.24 = (bf16[8,16,2048]{2,1,0:T(8,128)(2,1)S(1)}, bf16[8,16,2048]{2,1,0:T(8,128)(2,1)S(1)}, u32[]{:S(2)}, u32[]{:S(2)}) collective-permute-start(bf16[8,16,2048]{2,1,0:T(8,128)(2,1)S(1)} %bitcast.110), channel_id=1, source_target_pairs={{0,1},{1,0},{2,3},{3,2},{4,5},{5,4},{6,7},{7,6},{8,9},{9,8},{10,11... | collective-permute-start | bytes 1572872 | tf_op jit(solution)/shard_map/ppermute | solution.py:449
  63.4 27.3 %collective-permute-start.14 = (bf16[64,1024]{1,0:T(8,128)(2,1)S(1)}, bf16[64,1024]{1,0:T(8,128)(2,1)S(1)}, u32[]{:S(2)}, u32[]{:S(2)}) collective-permute-start(bf16[64,1024]{1,0:T(8,128)(2,1)S(1)} %fusion.19.refs_0_), channel_id=1, source_target_pairs={{0,1},{1,0},{2,3},{3,2},{4,5},{5,4},{6,7},{7,6},{8,9},{9,8},{10,11... | collective-permute-start | bytes 393224 | tf_op jit(solution)/shard_map/ppermute | solution.py:449
  65.4 26.7 %collective-permute-start.15 = (bf16[64,1024]{1,0:T(8,128)(2,1)S(1)}, bf16[64,1024]{1,0:T(8,128)(2,1)S(1)}, u32[]{:S(2)}, u32[]{:S(2)}) collective-permute-start(bf16[64,1024]{1,0:T(8,128)(2,1)S(1)} %fusion.19.refs_0_), channel_id=1, source_target_pairs={{0,2},{1,3},{2,0},{3,1},{4,6},{5,7},{6,4},{7,5},{8,10},{9,11},{10,... | collective-permute-start | bytes 393224 | tf_op jit(solution)/shard_map/ppermute | solution.py:449
  65.4 27.4 %collective-permute-start.16 = (bf16[64,1024]{1,0:T(8,128)(2,1)S(1)}, bf16[64,1024]{1,0:T(8,128)(2,1)S(1)}, u32[]{:S(2)}, u32[]{:S(2)}) collective-permute-start(bf16[64,1024]{1,0:T(8,128)(2,1)S(1)} %fusion.19.refs_0_), channel_id=1, source_target_pairs={{0,3},{1,2},{2,1},{3,0},{4,7},{5,6},{6,5},{7,4},{8,11},{9,10},{10,... | collective-permute-start | bytes 393224 | tf_op jit(solution)/shard_map/ppermute | solution.py:449
  94.4 16.7 %collective-permute-start.10 = (bf16[64,1024]{1,0:T(8,128)(2,1)S(1)}, bf16[64,1024]{1,0:T(8,128)(2,1)}, u32[]{:S(2)}, u32[]{:S(2)}) collective-permute-start(bf16[64,1024]{1,0:T(8,128)(2,1)S(1)} %fusion.19.refs_0_), channel_id=1, source_target_pairs={{0,4},{4,0},{8,12},{12,8},{16,20},{20,16},{24,28},{28,24},{1,5},{5... | collective-permute-start | bytes 393224 | tf_op jit(solution)/shard_map/ppermute | solution.py:443
  94.5 23.6 %collective-permute-start.17 = (bf16[3,64,1024]{2,1,0:T(8,128)(2,1)S(1)}, bf16[3,64,1024]{2,1,0:T(8,128)(2,1)}, u32[]{:S(2)}, u32[]{:S(2)}) collective-permute-start(bf16[3,64,1024]{2,1,0:T(8,128)(2,1)S(1)} %pad_maximum_fusion.refs_8_), channel_id=1, source_target_pairs={{0,8},{4,12},{8,0},{12,4},{16,24},{20,28},{24,16},{28,20},{1,9},{5... | collective-permute-start | bytes 1179656 | tf_op jit(solution)/shard_map/ppermute | solution.py:446
  96.6 16.8 %collective-permute-start.11 = (bf16[64,1024]{1,0:T(8,128)(2,1)S(1)}, bf16[64,1024]{1,0:T(8,128)(2,1)S(1)}, u32[]{:S(2)}, u32[]{:S(2)}) collective-permute-start(bf16[64,1024]{1,0:T(8,128)(2,1)S(1)} %collective-permute-done.7.refs_1_), channel_id=1, source_target_pairs={{0,4},{4,0},{8,12},{12,8},{16,20},{20,16},{24,28},{28,24},{1,5},{5... | collective-permute-start | bytes 393224 | tf_op jit(solution)/shard_map/ppermute | solution.py:443
  97.1 19.0 %collective-permute-start.12 = (bf16[64,1024]{1,0:T(8,128)(2,1)S(1)}, bf16[64,1024]{1,0:T(8,128)(2,1)S(1)}, u32[]{:S(2)}, u32[]{:S(2)}) collective-permute-start(bf16[64,1024]{1,0:T(8,128)(2,1)S(1)} %collective-permute-done.8.refs_2_), channel_id=1, source_target_pairs={{0,4},{4,0},{8,12},{12,8},{16,20},{20,16},{24,28},{28,24},{1,5},{5... | collective-permute-start | bytes 393224 | tf_op jit(solution)/shard_map/ppermute | solution.py:443
  98.8 18.0 %collective-permute-start.13 = (bf16[64,1024]{1,0:T(8,128)(2,1)S(1)}, bf16[64,1024]{1,0:T(8,128)(2,1)}, u32[]{:S(2)}, u32[]{:S(2)}) collective-permute-start(bf16[64,1024]{1,0:T(8,128)(2,1)S(1)} %collective-permute-done.9.refs_3_), channel_id=1, source_target_pairs={{0,4},{4,0},{8,12},{12,8},{16,20},{20,16},{24,28},{28,24},{1,5},{5... | collective-permute-start | bytes 393224 | tf_op jit(solution)/shard_map/ppermute | solution.py:443
  111.0 20.6 %collective-permute-start.18 = (bf16[3,64,1024]{2,1,0:T(8,128)(2,1)S(1)}, bf16[3,64,1024]{2,1,0:T(8,128)(2,1)S(1)}, u32[]{:S(2)}, u32[]{:S(2)}) collective-permute-start(bf16[3,64,1024]{2,1,0:T(8,128)(2,1)S(1)} %pad_maximum_fusion.refs_8_), channel_id=1, source_target_pairs={{0,16},{4,20},{8,24},{12,28},{16,0},{20,4},{24,8},{28,12},{1,17},{... | collective-permute-start | bytes 1179656 | tf_op jit(solution)/shard_map/ppermute | solution.py:446
  113.4 18.2 %collective-permute-start.19 = (bf16[3,64,1024]{2,1,0:T(8,128)(2,1)S(1)}, bf16[3,64,1024]{2,1,0:T(8,128)(2,1)S(1)}, u32[]{:S(2)}, u32[]{:S(2)}) collective-permute-start(bf16[3,64,1024]{2,1,0:T(8,128)(2,1)S(1)} %pad_maximum_fusion.refs_8_), channel_id=1, source_target_pairs={{0,24},{4,28},{8,16},{12,20},{16,8},{20,12},{24,0},{28,4},{1,25},{... | collective-permute-start | bytes 1179656 | tf_op jit(solution)/shard_map/ppermute | solution.py:446
  116.1 16.0 %collective-permute-start.20 = (bf16[3,64,1024]{2,1,0:T(8,128)(2,1)S(1)}, bf16[3,64,1024]{2,1,0:T(8,128)(2,1)}, u32[]{:S(2)}, u32[]{:S(2)}) collective-permute-start(bf16[3,64,1024]{2,1,0:T(8,128)(2,1)S(1)} %pad_maximum_fusion.refs_8_), channel_id=1, source_target_pairs={{0,4},{4,0},{8,12},{12,8},{16,20},{20,16},{24,28},{28,24},{1,5},{5... | collective-permute-start | bytes 1179656 | tf_op jit(solution)/shard_map/ppermute | solution.py:443
  116.8 23.6 %collective-permute-start.37 = (bf16[8,16,2048]{2,1,0:T(8,128)(2,1)S(1)}, bf16[8,16,2048]{2,1,0:T(8,128)(2,1)S(1)}, u32[]{:S(2)}, u32[]{:S(2)}) collective-permute-start(bf16[8,16,2048]{2,1,0:T(8,128)(2,1)S(1)} %copy-done.44), channel_id=1, source_target_pairs={{1,0},{2,3},{5,4},{6,7},{9,8},{10,11},{13,12},{14,15},{17,16},{18,... | collective-permute-start | bytes 1572872 | tf_op jit(solution)/shard_map/ppermute | solution.py:510
  118.1 22.3 %collective-permute-start.36 = (bf16[8,16,2048]{2,1,0:T(8,128)(2,1)S(1)}, bf16[8,16,2048]{2,1,0:T(8,128)(2,1)S(1)}, u32[]{:S(2)}, u32[]{:S(2)}) collective-permute-start(bf16[8,16,2048]{2,1,0:T(8,128)(2,1)S(1)} %bitcast.115), channel_id=1, source_target_pairs={{1,2},{2,1},{5,6},{6,5},{9,10},{10,9},{13,14},{14,13},{17,18},{18,... | collective-permute-start | bytes 1572872 | tf_op jit(solution)/shard_map/ppermute | solution.py:510
  131.6 8.8 %collective-permute-start.21 = (bf16[3,64,1024]{2,1,0:T(8,128)(2,1)}, bf16[3,64,1024]{2,1,0:T(8,128)(2,1)}, u32[]{:S(2)}, u32[]{:S(2)}) collective-permute-start(bf16[3,64,1024]{2,1,0:T(8,128)(2,1)} %collective-permute-done.17.refs_9_), channel_id=1, source_target_pairs={{0,4},{4,0},{8,12},{12,8},{16,20},{20,16},{24,28},{28,24},{1,5},{5... | collective-permute-start | bytes 1179656 | tf_op jit(solution)/shard_map/ppermute | solution.py:443
  131.6 8.7 %collective-permute-start.22 = (bf16[3,64,1024]{2,1,0:T(8,128)(2,1)S(1)}, bf16[3,64,1024]{2,1,0:T(8,128)(2,1)}, u32[]{:S(2)}, u32[]{:S(2)}) collective-permute-start(bf16[3,64,1024]{2,1,0:T(8,128)(2,1)S(1)} %collective-permute-done.18.refs_10_), channel_id=1, source_target_pairs={{0,4},{4,0},{8,12},{12,8},{16,20},{20,16},{24,28},{28,24},{1,5},{5... | collective-permute-start | bytes 1179656 | tf_op jit(solution)/shard_map/ppermute | solution.py:443
  132.1 8.3 %collective-permute-start.23 = (bf16[3,64,1024]{2,1,0:T(8,128)(2,1)S(1)}, bf16[3,64,1024]{2,1,0:T(8,128)(2,1)S(1)}, u32[]{:S(2)}, u32[]{:S(2)}) collective-permute-start(bf16[3,64,1024]{2,1,0:T(8,128)(2,1)S(1)} %collective-permute-done.19.refs_11_), channel_id=1, source_target_pairs={{0,4},{4,0},{8,12},{12,8},{16,20},{20,16},{24,28},{28,24},{1,5},{5... | collective-permute-start | bytes 1179656 | tf_op jit(solution)/shard_map/ppermute | solution.py:443
  179.3 25.9 %collective-permute-start.46 = (f32[64,1024]{1,0:T(8,128)S(1)}, f32[64,1024]{1,0:T(8,128)S(1)}, u32[]{:S(2)}, u32[]{:S(2)}) collective-permute-start(f32[64,1024]{1,0:T(8,128)S(1)} %get-tuple-element.40), channel_id=1, source_target_pairs={{0,8},{4,12},{8,0},{12,4},{16,24},{20,28},{24,16},{28,20},{1,9},{5... | collective-permute-start | bytes 786440 | tf_op jit(solution)/shard_map/ppermute | solution.py:446
  179.9 25.3 %collective-permute-start.47 = (f32[64,1024]{1,0:T(8,128)S(1)}, f32[64,1024]{1,0:T(8,128)}, u32[]{:S(2)}, u32[]{:S(2)}) collective-permute-start(f32[64,1024]{1,0:T(8,128)S(1)} %get-tuple-element.42), channel_id=1, source_target_pairs={{0,16},{4,20},{8,24},{12,28},{16,0},{20,4},{24,8},{28,12},{1,17},{... | collective-permute-start | bytes 786440 | tf_op jit(solution)/shard_map/ppermute | solution.py:446
  181.1 24.1 %collective-permute-start.48 = (f32[64,1024]{1,0:T(8,128)S(1)}, f32[64,1024]{1,0:T(8,128)}, u32[]{:S(2)}, u32[]{:S(2)}) collective-permute-start(f32[64,1024]{1,0:T(8,128)S(1)} %get-tuple-element.41), channel_id=1, source_target_pairs={{0,24},{4,28},{8,16},{12,20},{16,8},{20,12},{24,0},{28,4},{1,25},{... | collective-permute-start | bytes 786440 | tf_op jit(solution)/shard_map/ppermute | solution.py:446
  199.5 12.6 %collective-permute-start.61 = (f32[2,128,256]{2,1,0:T(8,128)S(1)}, f32[2,128,256]{2,1,0:T(8,128)S(1)}, u32[]{:S(2)}, u32[]{:S(2)}) collective-permute-start(f32[2,128,256]{2,1,0:T(8,128)S(1)} %bitcast.118), channel_id=1, source_target_pairs={{0,4},{4,0},{8,12},{12,8},{16,20},{20,16},{24,28},{28,24},{1,5},{5... | collective-permute-start | bytes 786440 | tf_op jit(solution)/shard_map/ppermute | solution.py:443
  204.7 11.2 %collective-permute-start.59 = (f32[2,128,256]{2,1,0:T(8,128)}, f32[2,128,256]{2,1,0:T(8,128)S(1)}, u32[]{:S(2)}, u32[]{:S(2)}) collective-permute-start(f32[2,128,256]{2,1,0:T(8,128)} %bitcast.117), channel_id=1, source_target_pairs={{0,4},{4,0},{8,12},{12,8},{16,20},{20,16},{24,28},{28,24},{1,5},{5... | collective-permute-start | bytes 786440 | tf_op jit(solution)/shard_map/ppermute | solution.py:443
  207.0 7.0 %collective-permute-start.50 = (bf16[64,1024]{1,0:T(8,128)(2,1)S(1)}, bf16[64,1024]{1,0:T(8,128)(2,1)S(1)}, u32[]{:S(2)}, u32[]{:S(2)}) collective-permute-start(bf16[64,1024]{1,0:T(8,128)(2,1)S(1)} %fusion.11.refs_0_), channel_id=1, source_target_pairs={{0,16},{4,20},{8,24},{12,28},{16,0},{20,4},{24,8},{28,12},{1,17},{... | collective-permute-start | bytes 393224 | tf_op jit(solution)/shard_map/ppermute | solution.py:446
  208.3 7.6 %collective-permute-start.51 = (bf16[64,1024]{1,0:T(8,128)(2,1)S(1)}, bf16[64,1024]{1,0:T(8,128)(2,1)S(1)}, u32[]{:S(2)}, u32[]{:S(2)}) collective-permute-start(bf16[64,1024]{1,0:T(8,128)(2,1)S(1)} %fusion.11.refs_0_), channel_id=1, source_target_pairs={{0,24},{4,28},{8,16},{12,20},{16,8},{20,12},{24,0},{28,4},{1,25},{... | collective-permute-start | bytes 393224 | tf_op jit(solution)/shard_map/ppermute | solution.py:446
  214.1 9.2 %collective-permute-start.54 = (bf16[64,1024]{1,0:T(8,128)(2,1)S(1)}, bf16[64,1024]{1,0:T(8,128)(2,1)S(1)}, u32[]{:S(2)}, u32[]{:S(2)}) collective-permute-start(bf16[64,1024]{1,0:T(8,128)(2,1)S(1)} %collective-permute-done.50.refs_2_), channel_id=1, source_target_pairs={{0,4},{4,0},{8,12},{12,8},{16,20},{20,16},{24,28},{28,24},{1,5},{5... | collective-permute-start | bytes 393224 | tf_op jit(solution)/shard_map/ppermute | solution.py:443
  215.9 7.4 %collective-permute-start.55 = (bf16[64,1024]{1,0:T(8,128)(2,1)S(1)}, bf16[64,1024]{1,0:T(8,128)(2,1)S(1)}, u32[]{:S(2)}, u32[]{:S(2)}) collective-permute-start(bf16[64,1024]{1,0:T(8,128)(2,1)S(1)} %collective-permute-done.51.refs_3_), channel_id=1, source_target_pairs={{0,4},{4,0},{8,12},{12,8},{16,20},{20,16},{24,28},{28,24},{1,5},{5... | collective-permute-start | bytes 393224 | tf_op jit(solution)/shard_map/ppermute | solution.py:443
  216.0 15.7 %collective-permute-start.60 = (bf16[128,256]{1,0:T(8,128)(2,1)S(1)}, bf16[128,256]{1,0:T(8,128)(2,1)S(1)}, u32[]{:S(2)}, u32[]{:S(2)}) collective-permute-start(bf16[128,256]{1,0:T(8,128)(2,1)S(1)} %get-tuple-element.48), channel_id=1, source_target_pairs={{0,8},{4,12},{8,0},{12,4},{16,24},{20,28},{24,16},{28,20},{1,9},{5... | collective-permute-start | bytes 196616 | tf_op jit(solution)/shard_map/ppermute | solution.py:446
  217.1 16.1 %collective-permute-start.62 = (bf16[128,256]{1,0:T(8,128)(2,1)S(1)}, bf16[128,256]{1,0:T(8,128)(2,1)S(1)}, u32[]{:S(2)}, u32[]{:S(2)}) collective-permute-start(bf16[128,256]{1,0:T(8,128)(2,1)S(1)} %get-tuple-element.46), channel_id=1, source_target_pairs={{0,16},{4,20},{8,24},{12,28},{16,0},{20,4},{24,8},{28,12},{1,17},{... | collective-permute-start | bytes 196616 | tf_op jit(solution)/shard_map/ppermute | solution.py:446
  218.8 14.4 %collective-permute-start.63 = (bf16[128,256]{1,0:T(8,128)(2,1)S(1)}, bf16[128,256]{1,0:T(8,128)(2,1)S(1)}, u32[]{:S(2)}, u32[]{:S(2)}) collective-permute-start(bf16[128,256]{1,0:T(8,128)(2,1)S(1)} %get-tuple-element.47), channel_id=1, source_target_pairs={{0,24},{4,28},{8,16},{12,20},{16,8},{20,12},{24,0},{28,4},{1,25},{... | collective-permute-start | bytes 196616 | tf_op jit(solution)/shard_map/ppermute | solution.py:446
  228.7 7.0 %collective-permute-start.56 = (bf16[128,512]{1,0:T(8,128)(2,1)}, bf16[128,512]{1,0:T(8,128)(2,1)S(1)}, u32[]{:S(2)}, u32[]{:S(2)}) collective-permute-start(bf16[128,512]{1,0:T(8,128)(2,1)} %get-tuple-element.31), channel_id=1, source_target_pairs={{0,1},{1,0},{2,3},{3,2},{4,5},{5,4},{6,7},{7,6},{8,9},{9,8},{10,11... | collective-permute-start | bytes 393224 | tf_op jit(solution)/shard_map/ppermute | solution.py:449
  230.9 12.8 %collective-permute-start.57 = (bf16[128,512]{1,0:T(8,128)(2,1)}, bf16[128,512]{1,0:T(8,128)(2,1)S(1)}, u32[]{:S(2)}, u32[]{:S(2)}) collective-permute-start(bf16[128,512]{1,0:T(8,128)(2,1)} %get-tuple-element.32), channel_id=1, source_target_pairs={{0,2},{1,3},{2,0},{3,1},{4,6},{5,7},{6,4},{7,5},{8,10},{9,11},{10,... | collective-permute-start | bytes 393224 | tf_op jit(solution)/shard_map/ppermute | solution.py:449
  231.7 12.0 %collective-permute-start.58 = (bf16[128,512]{1,0:T(8,128)(2,1)}, bf16[128,512]{1,0:T(8,128)(2,1)S(1)}, u32[]{:S(2)}, u32[]{:S(2)}) collective-permute-start(bf16[128,512]{1,0:T(8,128)(2,1)} %get-tuple-element.33), channel_id=1, source_target_pairs={{0,3},{1,2},{2,1},{3,0},{4,7},{5,6},{6,5},{7,4},{8,11},{9,10},{10,... | collective-permute-start | bytes 393224 | tf_op jit(solution)/shard_map/ppermute | solution.py:449
  245.5 7.0 %collective-permute-start.65 = (bf16[128,768]{1,0:T(8,128)(2,1)S(1)}, bf16[128,768]{1,0:T(8,128)(2,1)S(1)}, u32[]{:S(2)}, u32[]{:S(2)}) collective-permute-start(bf16[128,768]{1,0:T(8,128)(2,1)S(1)} %pad_maximum_fusion.1.refs_0_.refs_8_), channel_id=1, source_target_pairs={{0,16},{4,20},{8,24},{12,28},{16,0},{20,4},{24,8},{28,12},{1,17},{... | collective-permute-start | bytes 589832 | tf_op jit(solution)/shard_map/ppermute | solution.py:446
  248.7 8.3 %collective-permute-start.67 = (bf16[128,768]{1,0:T(8,128)(2,1)S(1)}, bf16[128,768]{1,0:T(8,128)(2,1)S(1)}, u32[]{:S(2)}, u32[]{:S(2)}) collective-permute-start(bf16[128,768]{1,0:T(8,128)(2,1)S(1)} %pad_maximum_fusion.1.refs_0_.refs_8_), channel_id=1, source_target_pairs={{0,4},{4,0},{8,12},{12,8},{16,20},{20,16},{24,28},{28,24},{1,5},{5... | collective-permute-start | bytes 589832 | tf_op jit(solution)/shard_map/ppermute | solution.py:443
  (79 other events, 931.5 us)
